TPU v7x, 32 devices: a whole 2x2x4 slice. The times are simulated.
32 devices in a mesh: group: 2 (over x), row: 16 (over z, y, core).
Axes of the slice: x: 2, y: 2, z: 4, core: 2. Of those that a mesh axis runs over, the one named last changes fastest.
Arguments:
- features: bfloat16 [256, 128, 384], P(('group', 'row')), parts along dimension 0, may hold values from -6 to 6
- qkv_weight: bfloat16 [384, 1152], replicated, may hold values from -0.5 to 0.5
- grad_output: bfloat16 [256, 128, 384], P(('group', 'row')), parts along dimension 0, may hold values from -6 to 6
Outputs:
- grad_features: bfloat16 [256, 128, 384], P(('group', 'row')), parts along dimension 0
- grad_weight: float32 [768, 1152], P(('group', 'row')), parts along dimension 0
There are 2 independent parts, one for each index of `group`. A program takes and returns all parts, laid end to end along the dimension named above; an argument that names none is the same for every part. Nothing has to cross between parts.
All inputs are finite; a program needn't handle non-finite values.
Results may differ from a plain program's by a relative error of at most 0.012.
The roundings to bfloat16 on the way count: a program that leaves them out, or rounds other values in their place, can miss the bound.
Values may be sent and summed in bfloat16 or wider, within the bound.
No kernel may reach another device: no remote copies, remote signals or barrier semaphores. Data moves between devices by JAX's collectives and lax.ppermute only.
A program may use at most 128 MiB of HBM per device.

v0:
```python
import functools
import jax
import jax.numpy as jnp
import numpy as np
from jax import lax
from jax.experimental import pallas as pl
from jax.experimental.pallas import tpu as pltpu
from jax.sharding import PartitionSpec as P

HEADS = 12
WINDOW = 7
DILATION = 2
HALO = 6
GROUPS = 3
BF = jnp.bfloat16
F32 = jnp.float32


def dot(a, b, ca=1, cb=0):
    return lax.dot_general(a, b, (((ca,), (cb,)), ((), ())), preferred_element_type=F32)


def column_maps():
    place = np.zeros((160, 128), np.float32)
    split = np.zeros((128, 128), np.float32)
    for col in range(128):
        place[80 * (col % 2) + col // 2 + 3, col] = 1
        split[64 * (col % 2) + col // 2, col] = 1
    return jnp.asarray(place, BF), jnp.asarray(split, BF)


def grads_kernel(edge_ref, x_ref, do_ref, w_ref, place_ref, split_ref,
                 dq_ref, acc_ref, dw_ref,
                 xk, xq, kv, q, do, bias, wkv):
    c = 32 ** -0.5 * 1.4426950408889634
    scale = 32 ** -0.5
    for g in range(GROUPS):
        wkv[:, 256 * g:256 * g + 128] = w_ref[:, 384 + 128 * g:384 + 128 * g + 128]
        wkv[:, 256 * g + 128:256 * g + 256] = w_ref[:, 768 + 128 * g:768 + 128 * g + 128]
    key = lax.broadcasted_iota(jnp.int32, (160, 128), 0)
    lane = lax.broadcasted_iota(jnp.int32, (160, 128), 1)
    krow, kcol = key // 16, key % 16
    qrow, qcol = (lane % 32) // 8, lane % 8
    drow, dcol = krow - qrow, kcol - qcol
    ok = (drow >= 0) & (drow <= 6) & (dcol >= 0) & (dcol <= 6)
    ok = ok & (krow >= edge_ref[0]) & (krow < edge_ref[1])
    for which, extra in enumerate((kcol >= 3, kcol >= 0, kcol < 11)):
        bias[which] = jnp.where(ok & extra, 0.0, -1e30).astype(F32)

    def project_row(row, carry):
        k, rp = row // 2, row % 2
        placed = dot(place_ref[...], x_ref[row]).astype(BF)
        xk[rp, 0, k] = placed[:80]
        xk[rp, 1, k] = placed[80:]
        both = dot(placed, wkv[...])
        for cp in range(2):
            for p in range(8):
                block = both[80 * cp + 8 * p:80 * cp + 8 * p + 16].astype(BF)
                for g in range(GROUPS):
                    kv[g, rp, cp, p, k] = block[:, 256 * g:256 * g + 256]
        return carry

    lax.fori_loop(0, 20, project_row, 0)
    for rp in range(2):
        for pair in range(2):
            row = 4 * pair + rp
            xs = [dot(split_ref[...], x_ref[6 + row + d]) for d in (0, 2)]
            ds = [dot(split_ref[...], do_ref[row + d]) for d in (0, 2)]
            for cp in range(2):
                for p in range(8):
                    at = slice(64 * cp + 8 * p, 64 * cp + 8 * p + 8)
                    xq[rp, cp, p, 16 * pair:16 * pair + 16] = jnp.concatenate([xs[0][at], xs[1][at]], axis=0).astype(BF)
                    dd = jnp.concatenate([ds[0][at], ds[1][at]], axis=0).astype(BF)
                    for g in range(GROUPS):
                        do[g, rp, cp, p, 16 * pair:16 * pair + 16] = dd[:, 128 * g:128 * g + 128]
        for cp in range(2):
            qs = dot(xq[rp, cp].reshape(256, 384), w_ref[:, :384]).astype(BF)
            for g in range(GROUPS):
                q[g, rp, cp] = qs[:, 128 * g:128 * g + 128].reshape(8, 32, 128)

    head_lane = lax.broadcasted_iota(jnp.int32, (32, 128), 1) // 32
    pick_b = [(head_lane == h).astype(F32).astype(BF) for h in range(4)]
    pick = [head_lane == h for h in range(4)]
    zero = jnp.zeros((128, 128), BF)

    def attend(step, carry):
        g, rp, cp = step // 4, (step // 2) % 2, step % 2
        tail = None
        for p in range(8):
            kvb = kv[g, rp, cp, p].reshape(160, 256)
            qp, dop = q[g, rp, cp, p], do[g, rp, cp, p]
            qbd = jnp.concatenate([qp * pick_b[h] for h in range(4)], axis=0)
            dobd = jnp.concatenate([dop * pick_b[h] for h in range(4)], axis=0)
            rhs = jnp.concatenate([jnp.concatenate([qbd, zero], axis=1), jnp.concatenate([zero, dobd], axis=1)], axis=0)
            s2 = dot(kvb, rhs, 1, 1)
            s = s2[:, :128] + bias[0 if p == 0 else (2 if p == 7 else 1)]
            dp = s2[:, 128:]
            m = jnp.max(s, axis=0, keepdims=True)
            e = jnp.exp2((s - m) * c)
            inv = 1.0 / jnp.sum(e, axis=0, keepdims=True)
            delta = jnp.sum(e * dp, axis=0, keepdims=True) * inv
            att = e * inv
            ds = att * (dp - delta)
            pd = jnp.concatenate([ds.astype(BF), att.astype(BF)], axis=1)
            dkv = dot(pd, rhs).reshape(10, 16, 256)
            head = dkv[:, :8]
            if tail is not None:
                head = head + tail
            acc_ref[g, rp, cp, :, 8 * p:8 * p + 8, :] = head
            tail = dkv[:, 8:]
            full = dot(pd[:, :128], kvb[:, :128], 0, 0)
            dq = jnp.where(pick[3], full[96:], 0.0)
            for h in range(3):
                dq = jnp.where(pick[h], full[32 * h:32 * h + 32], dq)
            dq_ref[g, rp, cp, p] = dq * scale
        acc_ref[g, rp, cp, :, 64:72, :] = tail
        acc_ref[g, rp, cp, :, 72:80, :] = jnp.zeros((10, 8, 256), F32)
        return carry

    lax.fori_loop(0, 12, attend, 0)

    dw = jnp.zeros((384, 768), F32)
    dwq = jnp.zeros((384, 384), F32)
    for rp in range(2):
        for cp in range(2):
            xs = xk[rp, cp].reshape(800, 384)
            parts = []
            for g in range(GROUPS):
                a = acc_ref[g, rp, cp].reshape(800, 256)
                parts.append((a[:, :128] * scale).astype(BF))
                parts.append(a[:, 128:].astype(BF))
            dw = dw + dot(xs, jnp.concatenate(parts, axis=1), 0, 0)
            dqs = jnp.concatenate([dq_ref[g, rp, cp].reshape(256, 128).astype(BF) for g in range(GROUPS)], axis=1)
            dwq = dwq + dot(xq[rp, cp].reshape(256, 384), dqs, 0, 0)
    dw_ref[:, :384] = dwq.astype(dw_ref.dtype)
    for g in range(GROUPS):
        dw_ref[:, 384 + 128 * g:512 + 128 * g] = dw[:, 256 * g:256 * g + 128].astype(dw_ref.dtype)
        dw_ref[:, 768 + 128 * g:896 + 128 * g] = dw[:, 256 * g + 128:256 * g + 256].astype(dw_ref.dtype)


def final_kernel(dq_ref, own_ref, above_ref, below_ref, w_ref, unplace_ref, unsplit_ref, out_ref):
    scale = 32 ** -0.5
    for rp in range(2):
        for kq in range(4):
            row = 2 * kq + rp
            dqs = jnp.concatenate(
                [jnp.concatenate([dq_ref[g, rp, cp, p, 8 * kq:8 * kq + 8] for g in range(GROUPS)], axis=1)
                 for cp in range(2) for p in range(8)], axis=0).astype(BF)
            ks, vs = [], []
            for g in range(GROUPS):
                both = []
                for cp in range(2):
                    t = own_ref[g, rp, cp, 3 + kq]
                    if kq < 3:
                        t = t + above_ref[g, rp, cp, kq].astype(F32)
                    if kq > 0:
                        t = t + below_ref[g, rp, cp, kq - 1].astype(F32)
                    both.append(t)
                both = jnp.concatenate(both, axis=0)
                ks.append((both[:, :128] * scale).astype(BF))
                vs.append(both[:, 128:].astype(BF))
            kvs = jnp.concatenate(ks + vs, axis=1)
            nq = dot(unsplit_ref[...], dqs).astype(BF)
            nkv = dot(unplace_ref[...], kvs).astype(BF)
            full = jnp.concatenate([nq, nkv], axis=1)
            out_ref[row] = dot(full, w_ref[...], 1, 1).astype(out_ref.dtype)


def halving_sum(x, axis):
    count = lax.axis_size(axis)
    index = lax.axis_index(axis)
    bits = count.bit_length() - 1
    x = x.reshape((2,) * bits + (x.shape[0] // count,) + x.shape[1:])
    for bit in range(bits):
        dim = bits - 1 - bit
        mine = (index >> bit) & 1
        keep = lax.dynamic_index_in_dim(x, mine, dim, keepdims=False)
        send = lax.dynamic_index_in_dim(x, 1 - mine, dim, keepdims=False).astype(BF)
        got = lax.ppermute(send, axis, [(i, i ^ (1 << bit)) for i in range(count)])
        x = keep.astype(F32) + got.astype(F32)
    return x


def shards(features, qkv_weight, grad_output):
    row_count, col_count, width = features.shape
    count = lax.axis_size("row")
    index = lax.axis_index("row")
    up = [(i, i + 1) for i in range(count - 1)]
    down = [(i + 1, i) for i in range(count - 1)]
    before = lax.ppermute(features[row_count - HALO:], "row", up)
    after = lax.ppermute(features[:HALO], "row", down)
    x20 = jnp.concatenate([before, features, after], axis=0)
    edge = jnp.stack([jnp.where(index == 0, 3, 0), jnp.where(index == count - 1, 7, 10)]).astype(jnp.int32)
    place, split = column_maps()
    vm = pl.BlockSpec(memory_space=pltpu.VMEM)
    dq, acc, dw = pl.pallas_call(
        grads_kernel,
        out_shape=(
            jax.ShapeDtypeStruct((GROUPS, 2, 2, 8, 32, 128), F32),
            jax.ShapeDtypeStruct((GROUPS, 2, 2, 10, 80, 256), F32),
            jax.ShapeDtypeStruct((384, 1152), F32),
        ),
        in_specs=[pl.BlockSpec(memory_space=pltpu.SMEM)] + [vm] * 5,
        out_specs=(vm, vm, vm),
        scratch_shapes=[
            pltpu.VMEM((2, 2, 10, 80, 384), BF),
            pltpu.VMEM((2, 2, 8, 32, 384), BF),
            pltpu.VMEM((GROUPS, 2, 2, 8, 10, 16, 256), BF),
            pltpu.VMEM((GROUPS, 2, 2, 8, 32, 128), BF),
            pltpu.VMEM((GROUPS, 2, 2, 8, 32, 128), BF),
            pltpu.VMEM((3, 160, 128), F32),
            pltpu.VMEM((384, 768), BF),
        ],
        compiler_params=pltpu.CompilerParams(vmem_limit_bytes=56 << 20),
        name="grads",
    )(edge, x20, grad_output, qkv_weight, place, split)
    from_above = lax.ppermute(acc[:, :, :, 7:].astype(BF), "row", up)
    from_below = lax.ppermute(acc[:, :, :, :3].astype(BF), "row", down)
    grad_features = pl.pallas_call(
        final_kernel,
        out_shape=jax.ShapeDtypeStruct(features.shape, BF),
        in_specs=[vm] * 7,
        out_specs=vm,
        compiler_params=pltpu.CompilerParams(vmem_limit_bytes=56 << 20),
        name="final",
    )(dq, acc, from_above, from_below, qkv_weight, place.T, split.T)
    summed = halving_sum(dw, "row")
    return grad_features, summed * (row_count * count * col_count) ** -0.5


def solution(mesh):
    placed = (P(("group", "row"), None, None), P(), P(("group", "row"), None, None))
    return jax.shard_map(
        shards,
        mesh=mesh,
        in_specs=placed,
        out_specs=(P(("group", "row"), None, None), P(("group", "row"), None)),
        check_vma=False,
    )
```

profile of v0, /device:TPU:9, one launch (start us, length us, event | category | flops | bytes accessed | tf_op | source)
XLA Modules:
  0.0 113.2 jit_solution(7558874556397808968)
XLA Ops:
  0.6 0.0 copy-start
  0.6 1.5 %fusion.6 = (bf16[6,128,384]{2,1,0:T(8,128)(2,1)S(1)}, bf16[6,128,384]{2,1,0:T(8,128)(2,1)S(1)}) fusion(bf16[8,128,384]{2,1,0:T(8,128)(2,1)} %param.5), kind=kLoop, calls=%fused_computation.18 | loop fusion | bytes 2359296 | tf_op jit(solution)/shard_map/slice | solution.py:190
  2.1 3.7 %collective-permute-start = (bf16[6,128,384]{2,1,0:T(8,128)(2,1)S(1)}, bf16[6,128,384]{2,1,0:T(8,128)(2,1)S(1)}, u32[]{:S(2)}, u32[]{:S(2)}) collective-permute-start(bf16[6,128,384]{2,1,0:T(8,128)(2,1)S(1)} %get-tuple-element.10), channel_id=1, source_target_pairs={{0,1},{1,2},{2,3},{3,4},{4,5},{5,6},{6,7},{7,8},{8,9},{9,10},{10,1... | collective-permute-start | bytes 1769480 | tf_op jit(solution)/shard_map/ppermute | solution.py:190
  5.8 1.9 %collective-permute-start.1 = (bf16[6,128,384]{2,1,0:T(8,128)(2,1)S(1)}, bf16[6,128,384]{2,1,0:T(8,128)(2,1)S(1)}, u32[]{:S(2)}, u32[]{:S(2)}) collective-permute-start(bf16[6,128,384]{2,1,0:T(8,128)(2,1)S(1)} %get-tuple-element.11), channel_id=1, source_target_pairs={{1,0},{2,1},{3,2},{4,3},{5,4},{6,5},{7,6},{8,7},{9,8},{10,9},{11,1... | collective-permute-start | bytes 1769480 | tf_op jit(solution)/shard_map/ppermute | solution.py:191
  7.8 0.6 pad_add_fusion.edge_ref
  8.4 10.5 %collective-permute-done = bf16[6,128,384]{2,1,0:T(8,128)(2,1)S(1)} collective-permute-done((bf16[6,128,384]{2,1,0:T(8,128)(2,1)S(1)}, bf16[6,128,384]{2,1,0:T(8,128)(2,1)S(1)}, u32[]{:S(2)}, u32[]{:S(2)}) %collective-permute-start) | collective-permute-done | bytes 589856 | tf_op jit(solution)/shard_map/ppermute | solution.py:190
  18.9 1.6 %collective-permute-done.1 = bf16[6,128,384]{2,1,0:T(8,128)(2,1)S(1)} collective-permute-done((bf16[6,128,384]{2,1,0:T(8,128)(2,1)S(1)}, bf16[6,128,384]{2,1,0:T(8,128)(2,1)S(1)}, u32[]{:S(2)}, u32[]{:S(2)}) %collective-permute-start.1) | collective-permute-done | bytes 589856 | tf_op jit(solution)/shard_map/ppermute | solution.py:191
  20.5 0.0 copy-done
  20.5 1.5 %pad_maximum_fusion.x_ref = bf16[20,128,384]{2,1,0:T(8,128)(2,1)} fusion(bf16[6,128,384]{2,1,0:T(8,128)(2,1)S(1)} %collective-permute-done.1, bf16[8,128,384]{2,1,0:T(8,128)(2,1)S(1)} %copy-done, bf16[6,128,384]{2,1,0:T(8,128)(2,1)S(1)} %collective-permute-done), kind=kLoop, calls=%fused_computation | loop fusion | flops 1966080 | bytes 3932160 | tf_op jit(solution)/shard_map/concatenate | solution.py:192
  22.0 37.1 %grads.1 = (f32[3,2,2,8,32,128]{5,4,3,2,1,0:T(8,128)}, f32[3,2,2,10,80,256]{5,4,3,2,1,0:T(8,128)}, f32[384,1152]{1,0:T(8,128)}) custom-call(s32[2]{0:T(128)} %pad_add_fusion.edge_ref, bf16[20,128,384]{2,1,0:T(8,128)(2,1)} %pad_maximum_fusion.x_ref, bf16[8,128,384]{2,1,0:T(8,128)(2,1)} %do_ref.1, bf16[384,1152]{1,0:T(8,128)(2,1)} %w_ref.3, ...), custom_call_target="tpu_custom_call" | custom-call | tf_op jit(solution)/shard_map/grads/pallas_call | solution.py:196
  59.2 1.2 %fusion = bf16[2,2,2,24,1152]{4,3,0,1,2:T(8,128)(2,1)S(1)} fusion(f32[2,2,2,2,24,1152]{5,4,3,2,1,0:T(8,128)} %bitcast.21, s32[]{:T(128)S(6)} %select_n.38), kind=kLoop, calls=%fused_computation.3 | loop fusion | bytes 884740 | tf_op jit(solution)/shard_map/convert_element_type | solution.py:178
  60.4 0.1 collective-permute-start.4
  60.5 0.0 copy-start.1
  60.5 4.6 %convert.4 = bf16[3,2,2,10,80,256]{5,4,3,2,1,0:T(8,128)(2,1)S(1)} convert(f32[3,2,2,10,80,256]{5,4,3,2,1,0:T(8,128)} %get-tuple-element.6.own_ref) | non-fusion elementwise | flops 2457600 | bytes 14745600 | tf_op jit(solution)/shard_map/convert.1
  65.1 0.0 collective-permute-done.4
  65.1 0.0 copy-done.1
  65.1 0.1 bitcast_add_fusion
  65.2 1.1 collective-permute-start.5
  66.3 0.3 fusion.5
  66.6 2.2 %collective-permute-start.3 = (bf16[3,2,2,3,80,256]{5,4,3,2,1,0:T(8,128)(2,1)S(1)}, bf16[3,2,2,3,80,256]{5,4,3,2,1,0:T(8,128)(2,1)}, u32[]{:S(2)}, u32[]{:S(2)}) collective-permute-start(bf16[3,2,2,3,80,256]{5,4,3,2,1,0:T(8,128)(2,1)S(1)} %get-tuple-element.8), channel_id=1, source_target_pairs={{1,0},{2,1},{3,2},{4,3},{5,4},{6,5},{7,6},{8,7},{9,8},{10,9},{11,1... | collective-permute-start | bytes 4423688 | tf_op jit(solution)/shard_map/ppermute | solution.py:218
  68.8 3.3 %collective-permute-start.2 = (bf16[3,2,2,3,80,256]{5,4,3,2,1,0:T(8,128)(2,1)S(1)}, bf16[3,2,2,3,80,256]{5,4,3,2,1,0:T(8,128)(2,1)}, u32[]{:S(2)}, u32[]{:S(2)}) collective-permute-start(bf16[3,2,2,3,80,256]{5,4,3,2,1,0:T(8,128)(2,1)S(1)} %get-tuple-element.9), channel_id=1, source_target_pairs={{0,1},{1,2},{2,3},{3,4},{4,5},{5,6},{6,7},{7,8},{8,9},{9,10},{10,1... | collective-permute-start | bytes 4423688 | tf_op jit(solution)/shard_map/ppermute | solution.py:217
  72.2 0.0 collective-permute-done.5
  72.3 0.7 fusion.2
  72.9 14.7 %collective-permute-start.6 = (bf16[2,24,1152]{2,1,0:T(8,128)(2,1)}, bf16[2,24,1152]{2,1,0:T(8,128)(2,1)S(1)}, u32[]{:S(2)}, u32[]{:S(2)}) collective-permute-start(bf16[2,24,1152]{2,1,0:T(8,128)(2,1)} %fusion.2), channel_id=1, source_target_pairs={{0,4},{1,5},{2,6},{3,7},{4,0},{5,1},{6,2},{7,3},{8,12},{9,13},{10,... | collective-permute-start | bytes 331784 | tf_op jit(solution)/shard_map/ppermute | solution.py:179
  87.6 2.6 %collective-permute-done.6 = bf16[2,24,1152]{2,1,0:T(8,128)(2,1)S(1)} collective-permute-done((bf16[2,24,1152]{2,1,0:T(8,128)(2,1)}, bf16[2,24,1152]{2,1,0:T(8,128)(2,1)S(1)}, u32[]{:S(2)}, u32[]{:S(2)}) %collective-permute-start.6) | collective-permute-done | bytes 110624 | tf_op jit(solution)/shard_map/ppermute | solution.py:179
  90.2 0.0 copy-start.2
  90.2 0.7 copy-done.2
  90.9 0.1 collective-permute-start.7
  91.0 3.9 %collective-permute-done.7 = bf16[24,1152]{1,0:T(8,128)(2,1)S(1)} collective-permute-done((bf16[24,1152]{1,0:T(8,128)(2,1)S(1)}, bf16[24,1152]{1,0:T(8,128)(2,1)S(1)}, u32[]{:S(2)}, u32[]{:S(2)}) %collective-permute-start.7) | collective-permute-done | bytes 55328 | tf_op jit(solution)/shard_map/ppermute | solution.py:179
  95.0 1.6 %fusion.3 = f32[24,1152]{1,0:T(8,128)} fusion(bf16[24,1152]{1,0:T(8,128)(2,1)S(1)} %collective-permute-done.7, f32[2,24,1152]{2,1,0:T(8,128)} %copy-done.2, s32[]{:T(128)S(6)} %select_n.43), kind=kLoop, calls=%fused_computation.11 | loop fusion | flops 82944 | bytes 276484 | tf_op jit(solution)/shard_map/mul | solution.py:228
  96.5 7.6 %collective-permute-done.3.below_ref = bf16[3,2,2,3,80,256]{5,4,3,2,1,0:T(8,128)(2,1)} collective-permute-done((bf16[3,2,2,3,80,256]{5,4,3,2,1,0:T(8,128)(2,1)S(1)}, bf16[3,2,2,3,80,256]{5,4,3,2,1,0:T(8,128)(2,1)}, u32[]{:S(2)}, u32[]{:S(2)}) %collective-permute-start.3) | collective-permute-done | bytes 1474592 | tf_op jit(solution)/shard_map/ppermute | solution.py:218
  104.2 0.0 collective-permute-done.2.above_ref
  104.2 9.0 %final.1 = bf16[8,128,384]{2,1,0:T(8,128)(2,1)} custom-call(f32[3,2,2,8,32,128]{5,4,3,2,1,0:T(8,128)} %get-tuple-element.5.dq_ref, f32[3,2,2,10,80,256]{5,4,3,2,1,0:T(8,128)} %get-tuple-element.6.own_ref, bf16[3,2,2,3,80,256]{5,4,3,2,1,0:T(8,128)(2,1)} %collective-permute-done.2.above_ref, bf16[3,2,2,3,80,256]{5,4,3,2,1,0:T(8,128)(2,1)} %collective-permute-done.3.below_ref, ...), custom_call_target="tpu_custom_call" | custom-call | tf_op jit(solution)/shard_map/final/pallas_call | solution.py:219
  (4 shorter events, 0.1 us)
Async XLA Ops:
  0.6 19.9 %copy-start = (bf16[8,128,384]{2,1,0:T(8,128)(2,1)S(1)}, bf16[8,128,384]{2,1,0:T(8,128)(2,1)}, u32[]{:S(2)}) copy-start(bf16[8,128,384]{2,1,0:T(8,128)(2,1)} %param.5) | copy-start | bytes 2359300
  2.1 16.8 %collective-permute-start = (bf16[6,128,384]{2,1,0:T(8,128)(2,1)S(1)}, bf16[6,128,384]{2,1,0:T(8,128)(2,1)S(1)}, u32[]{:S(2)}, u32[]{:S(2)}) collective-permute-start(bf16[6,128,384]{2,1,0:T(8,128)(2,1)S(1)} %get-tuple-element.10), channel_id=1, source_target_pairs={{0,1},{1,2},{2,3},{3,4},{4,5},{5,6},{6,7},{7,8},{8,9},{9,10},{10,1... | collective-permute-start | bytes 1769480 | tf_op jit(solution)/shard_map/ppermute | solution.py:190
  5.8 14.7 %collective-permute-start.1 = (bf16[6,128,384]{2,1,0:T(8,128)(2,1)S(1)}, bf16[6,128,384]{2,1,0:T(8,128)(2,1)S(1)}, u32[]{:S(2)}, u32[]{:S(2)}) collective-permute-start(bf16[6,128,384]{2,1,0:T(8,128)(2,1)S(1)} %get-tuple-element.11), channel_id=1, source_target_pairs={{1,0},{2,1},{3,2},{4,3},{5,4},{6,5},{7,6},{8,7},{9,8},{10,9},{11,1... | collective-permute-start | bytes 1769480 | tf_op jit(solution)/shard_map/ppermute | solution.py:191
  60.4 4.7 %collective-permute-start.4 = (bf16[2,2,2,24,1152]{4,3,0,1,2:T(8,128)(2,1)S(1)}, bf16[2,2,2,24,1152]{4,3,0,1,2:T(8,128)(2,1)S(1)}, u32[]{:S(2)}, u32[]{:S(2)}) collective-permute-start(bf16[2,2,2,24,1152]{4,3,0,1,2:T(8,128)(2,1)S(1)} %fusion), channel_id=1, source_target_pairs={{0,1},{1,0},{2,3},{3,2},{4,5},{5,4},{6,7},{7,6},{8,9},{9,8},{10,11... | collective-permute-start | bytes 1327112 | tf_op jit(solution)/shard_map/ppermute | solution.py:179
  60.5 4.6 %copy-start.1 = (f32[384,1152]{1,0:T(8,128)S(1)}, f32[384,1152]{1,0:T(8,128)}, u32[]{:S(2)}) copy-start(f32[384,1152]{1,0:T(8,128)} %get-tuple-element.7) | copy-start | bytes 5308420
  65.2 7.0 %collective-permute-start.5 = (bf16[2,2,24,1152]{3,2,0,1:T(8,128)(2,1)S(1)}, bf16[2,2,24,1152]{3,2,0,1:T(8,128)(2,1)S(1)}, u32[]{:S(2)}, u32[]{:S(2)}) collective-permute-start(bf16[2,2,24,1152]{3,2,0,1:T(8,128)(2,1)S(1)} %fusion.1), channel_id=1, source_target_pairs={{0,2},{1,3},{2,0},{3,1},{4,6},{5,7},{6,4},{7,5},{8,10},{9,11},{10,... | collective-permute-start | bytes 663560 | tf_op jit(solution)/shard_map/ppermute | solution.py:179
  66.6 37.5 %collective-permute-start.3 = (bf16[3,2,2,3,80,256]{5,4,3,2,1,0:T(8,128)(2,1)S(1)}, bf16[3,2,2,3,80,256]{5,4,3,2,1,0:T(8,128)(2,1)}, u32[]{:S(2)}, u32[]{:S(2)}) collective-permute-start(bf16[3,2,2,3,80,256]{5,4,3,2,1,0:T(8,128)(2,1)S(1)} %get-tuple-element.8), channel_id=1, source_target_pairs={{1,0},{2,1},{3,2},{4,3},{5,4},{6,5},{7,6},{8,7},{9,8},{10,9},{11,1... | collective-permute-start | bytes 4423688 | tf_op jit(solution)/shard_map/ppermute | solution.py:218
  68.8 35.3 %collective-permute-start.2 = (bf16[3,2,2,3,80,256]{5,4,3,2,1,0:T(8,128)(2,1)S(1)}, bf16[3,2,2,3,80,256]{5,4,3,2,1,0:T(8,128)(2,1)}, u32[]{:S(2)}, u32[]{:S(2)}) collective-permute-start(bf16[3,2,2,3,80,256]{5,4,3,2,1,0:T(8,128)(2,1)S(1)} %get-tuple-element.9), channel_id=1, source_target_pairs={{0,1},{1,2},{2,3},{3,4},{4,5},{5,6},{6,7},{7,8},{8,9},{9,10},{10,1... | collective-permute-start | bytes 4423688 | tf_op jit(solution)/shard_map/ppermute | solution.py:217
  72.9 17.3 %collective-permute-start.6 = (bf16[2,24,1152]{2,1,0:T(8,128)(2,1)}, bf16[2,24,1152]{2,1,0:T(8,128)(2,1)S(1)}, u32[]{:S(2)}, u32[]{:S(2)}) collective-permute-start(bf16[2,24,1152]{2,1,0:T(8,128)(2,1)} %fusion.2), channel_id=1, source_target_pairs={{0,4},{1,5},{2,6},{3,7},{4,0},{5,1},{6,2},{7,3},{8,12},{9,13},{10,... | collective-permute-start | bytes 331784 | tf_op jit(solution)/shard_map/ppermute | solution.py:179
  90.2 0.7 copy-start.2
  90.9 4.0 %collective-permute-start.7 = (bf16[24,1152]{1,0:T(8,128)(2,1)S(1)}, bf16[24,1152]{1,0:T(8,128)(2,1)S(1)}, u32[]{:S(2)}, u32[]{:S(2)}) collective-permute-start(bf16[24,1152]{1,0:T(8,128)(2,1)S(1)} %fusion.4), channel_id=1, source_target_pairs={{0,8},{1,9},{2,10},{3,11},{4,12},{5,13},{6,14},{7,15},{8,0},{9,1},... | collective-permute-start | bytes 165896 | tf_op jit(solution)/shard_map/ppermute | solution.py:179
where the time goes:
time: 114 us; the launch traced here: 113 us
  Pallas kernels  46.2 us (41%)
  starting transfers between devices  27.1 us (24%)
  waiting for transfers between devices  26.3 us (23%)
  other arithmetic  8.47 us (7%)
  local copies, waits for them, and re-layouts  4.37 us (4%)
    pallas_call x1, Pallas kernels, shards(): pl.pallas_call(grads_kernel, out_shape=(jax.ShapeDtypeStruct((GROUPS, 2,...  37.1 us
    ppermute x4, starting transfers between devices, halving_sum(): got = lax.ppermute(send, axis, [(i, i ^ 1 << bit) for i in range(count)])  15.9 us
    ppermute x1, waiting for transfers between devices, shards(): before = lax.ppermute(features[row_count - HALO:], 'row', up)  10.5 us
    pallas_call x1, Pallas kernels, shards(): pl.pallas_call(final_kernel, out_shape=jax.ShapeDtypeStruct(features.shap...  9.05 us
    ppermute x1, waiting for transfers between devices, shards(): from_below = lax.ppermute(acc[:, :, :, :3].astype(BF), 'row', down)  7.64 us
    ppermute x4, waiting for transfers between devices, halving_sum(): got = lax.ppermute(send, axis, [(i, i ^ 1 << bit) for i in range(count)])  6.5 us
    another operation x1, other arithmetic  4.6 us
    ppermute x1, starting transfers between devices, shards(): before = lax.ppermute(features[row_count - HALO:], 'row', up)  3.71 us
  transfers between devices with their start and end apart: 8, of which 5 were waited for; matrix products, arithmetic and copies ran while one was open for 7% of the time, Pallas kernels for 0%

commit v1 on v0

v1 whole, which is shorter than its diff:
```python
import jax
import jax.numpy as jnp
import numpy as np
from jax import lax
from jax.experimental import pallas as pl
from jax.experimental.pallas import tpu as pltpu
from jax.sharding import PartitionSpec as P

HEADS = 12
WINDOW = 7
DILATION = 2
HALO = 6
GROUPS = 3
SLOTS = 4
BF = jnp.bfloat16
F32 = jnp.float32
SCALE = 32 ** -0.5
C = SCALE * 1.4426950408889634
VMEM_BYTES = 40 << 20


def dot(a, b, ca=1, cb=0):
    return lax.dot_general(a, b, (((ca,), (cb,)), ((), ())), preferred_element_type=F32)


def column_maps():
    place = np.zeros((160, 128), np.float32)
    split = np.zeros((128, 128), np.float32)
    for col in range(128):
        place[80 * (col % 2) + col // 2 + 3, col] = 1
        split[64 * (col % 2) + col // 2, col] = 1
    return jnp.asarray(place, BF), jnp.asarray(split, BF)


def gather_kv_weight(w_ref, wkv):
    for g in range(GROUPS):
        wkv[:, 256 * g:256 * g + 128] = w_ref[:, 384 + 128 * g:384 + 128 * g + 128]
        wkv[:, 256 * g + 128:256 * g + 256] = w_ref[:, 768 + 128 * g:768 + 128 * g + 128]


def project_keys(x, place_ref, wkv, xk, kv, k):
    placed = dot(place_ref[...], x).astype(BF)
    xk[0, k] = placed[:80]
    xk[1, k] = placed[80:]
    both = dot(placed, wkv[...])
    for cp in range(2):
        for p in range(8):
            block = both[80 * cp + 8 * p:80 * cp + 8 * p + 16].astype(BF)
            for g in range(GROUPS):
                kv[g, cp, p, k] = block[:, 256 * g:256 * g + 256]


def to_patches(pair_rows, split_ref, store):
    parts = [None if row is None else dot(split_ref[...], row) for row in pair_rows]
    for cp in range(2):
        for p in range(8):
            at = slice(64 * cp + 8 * p, 64 * cp + 8 * p + 8)
            known = [part for part in parts if part is not None][0][at]
            halves = [jnp.zeros_like(known) if part is None else part[at] for part in parts]
            store(cp, p, jnp.concatenate(halves, axis=0).astype(BF))


def pack_kernel(edge_ref, x_ref, g_ref, x0_ref, x1_ref, fg_ref, near_ref, xs, gs, sem):
    odd = edge_ref[2]
    mine, other = pl.ds(odd, 3), pl.ds(1 - odd, 3)
    loads = [pltpu.make_async_copy(x_ref, xs, sem.at[0]), pltpu.make_async_copy(g_ref, gs, sem.at[1])]
    for copy in loads:
        copy.start()
    loads[0].wait()
    copies = [
        pltpu.make_async_copy(xs.at[mine, 0], x0_ref, sem.at[2]),
        pltpu.make_async_copy(xs.at[other], near_ref.at[0], sem.at[3]),
        pltpu.make_async_copy(xs.at[mine, 1], x1_ref, sem.at[4]),
        pltpu.make_async_copy(gs.at[other], near_ref.at[1], sem.at[5]),
        pltpu.make_async_copy(gs.at[mine], fg_ref, sem.at[6]),
    ]
    for copy in copies[:3]:
        copy.start()
    loads[1].wait()
    for copy in copies[3:]:
        copy.start()
    for copy in copies:
        copy.wait()


def own_kernel(x_ref, do_ref, w_ref, place_ref, split_ref, q_ref, g_ref, xq_ref, kv_ref, xk_ref, wkv):
    gather_kv_weight(w_ref, wkv)
    for rp in range(2):
        for k in range(4):
            project_keys(x_ref[k, rp], place_ref, wkv, xk_ref.at[rp], kv_ref.at[rp], k)
        for pair in range(2):
            at = slice(16 * pair, 16 * pair + 16)

            def store_x(cp, p, block, at=at, rp=rp):
                xq_ref[rp, cp, p, at] = block

            def store_g(cp, p, block, at=at, rp=rp):
                for g in range(GROUPS):
                    g_ref[rp, g, cp, p, at] = block[:, 128 * g:128 * g + 128]

            to_patches([x_ref[2 * pair + d, rp] for d in range(2)], split_ref, store_x)
            to_patches([do_ref[2 * pair + d, rp] for d in range(2)], split_ref, store_g)
        for cp in range(2):
            qs = dot(xq_ref[rp, cp].reshape(256, 384), w_ref[:, :384]).astype(BF)
            for g in range(GROUPS):
                q_ref[rp, g, cp] = qs[:, 128 * g:128 * g + 128].reshape(8, 32, 128)


def window_bias(bias, key_rows, row_ok):
    shape = (16 * key_rows, 128)
    key = lax.broadcasted_iota(jnp.int32, shape, 0)
    lane = lax.broadcasted_iota(jnp.int32, shape, 1)
    krow, kcol = key // 16, key % 16
    qrow, dcol = (lane % 32) // 8, key % 16 - lane % 8
    ok = row_ok(krow, qrow) & (dcol >= 0) & (dcol <= 6)
    for which, extra in enumerate((kcol >= 3, kcol >= 0, kcol < 11)):
        bias[which] = jnp.where(ok & extra, 0.0, -1e30).astype(F32)


def head_masks():
    head_lane = lax.broadcasted_iota(jnp.int32, (32, 128), 1) // 32
    return [head_lane == h for h in range(4)], [(head_lane == h).astype(F32).astype(BF) for h in range(4)]


def pack_heads(rhs, slot, qp, gp, pick_b):
    for h in range(4):
        rhs[slot, 32 * h:32 * h + 32, :128] = qp * pick_b[h]
        rhs[slot, 128 + 32 * h:160 + 32 * h, 128:] = gp * pick_b[h]


def clear_off_diagonal(rhs):
    for slot in range(rhs.shape[0]):
        rhs[slot, :128, 128:] = jnp.zeros((128, 128), BF)
        rhs[slot, 128:, :128] = jnp.zeros((128, 128), BF)


def edge_kind(p):
    return 0 if p == 0 else (2 if p == 7 else 1)


def attend_kernel(rp, edge_ref, near_ref, far_ref, q, do, xq, kv, xk, w_ref, place_ref, *refs):
    if rp == 0:
        dw_in = None
    else:
        dw_in, *refs = refs
    dq_ref, own_ref, stat_ref, dw_ref, xh, kvh, acc, bias, wkv, sc, pd, rhs, tail = refs
    odd = edge_ref[2]
    gather_kv_weight(w_ref, wkv)
    window_bias(bias, 10, lambda krow, qrow: (krow >= qrow) & (krow <= qrow + 6) & (krow >= edge_ref[0]) & (krow < edge_ref[1]))

    def project_pair(k, carry):
        project_keys(near_ref[0, k, rp], place_ref, wkv, xh, kvh, k + 3 - 3 * odd)
        project_keys(far_ref[k], place_ref, wkv, xh, kvh, k + 3 * odd)
        return carry

    lax.fori_loop(0, 3, project_pair, 0)
    pick, pick_b = head_masks()
    clear_off_diagonal(rhs)

    def attend(step, carry):
        g, cp = step // 2, step % 2

        def keys(p):
            return jnp.concatenate([
                kvh[g, cp, p, :3].reshape(48, 256),
                kv[0, g, cp, p].reshape(64, 256),
                kvh[g, cp, p, 3:].reshape(48, 256)], axis=0)

        def score(p):
            slot = p % SLOTS
            pack_heads(rhs, slot, q[0, g, cp, p], do[0, g, cp, p], pick_b)
            sc[p % 2] = dot(keys(p), rhs[slot], 1, 1)

        def soften(p):
            slot = p % 2
            s = sc[slot, :, :128] + bias[edge_kind(p)]
            m = jnp.max(s, axis=0, keepdims=True)
            e = jnp.exp2((s - m) * C)
            dp = sc[slot, :, 128:]
            total = jnp.sum(e, axis=0, keepdims=True)
            inv = 1.0 / total
            delta = jnp.sum(e * dp, axis=0, keepdims=True) * inv
            att = e * inv
            pd[slot, :, :128] = (att * (dp - delta)).astype(BF)
            pd[slot, :, 128:] = att.astype(BF)
            stat_ref[0, g, cp, p:p + 1] = m * C + jnp.log2(total)
            stat_ref[1, g, cp, p:p + 1] = delta

        def add_to(at, value):
            acc[g, cp, :3, at, :] = value[:3]
            own_ref[g, cp, :, at, :] = value[3:7]
            acc[g, cp, 3:, at, :] = value[7:]

        def spread(p):
            slot = p % 2
            dkv = dot(pd[slot], rhs[p % SLOTS]).reshape(10, 16, 256)
            head = dkv[:, :8]
            if p > 0:
                head = head + tail[(p + 1) % 2]
            add_to(slice(8 * p, 8 * p + 8), head)
            if p < 7:
                tail[slot] = dkv[:, 8:]
            else:
                add_to(slice(64, 72), dkv[:, 8:])
            full = dot(pd[slot, :, :128], keys(p)[:, :128], 0, 0)
            dq = jnp.where(pick[3], full[96:], 0.0)
            for h in range(3):
                dq = jnp.where(pick[h], full[32 * h:32 * h + 32], dq)
            dq_ref[g, cp, p] = (dq * SCALE).astype(BF)

        for t in range(8 + 2):
            if t < 8:
                score(t)
            if 0 <= t - 1 < 8:
                soften(t - 1)
            if 0 <= t - 2 < 8:
                spread(t - 2)
        add_to(slice(72, 80), jnp.zeros((10, 8, 256), F32))
        return carry

    lax.fori_loop(0, 6, attend, 0)

    dw = jnp.zeros((384, 768), F32)
    dwq = jnp.zeros((384, 384), F32)
    for cp in range(2):
        for xs, ref, n in ((xh[cp], acc, 480), (xk[0, cp], own_ref, 320)):
            parts = []
            for g in range(GROUPS):
                a = ref[g, cp].reshape(n, 256)
                parts.append((a[:, :128] * SCALE).astype(BF))
                parts.append(a[:, 128:].astype(BF))
            dw = dw + dot(xs.reshape(n, 384), jnp.concatenate(parts, axis=1), 0, 0)
        dqs = jnp.concatenate([dq_ref[g, cp].reshape(256, 128) for g in range(GROUPS)], axis=1)
        dwq = dwq + dot(xq[0, cp].reshape(256, 384), dqs, 0, 0)

    def put(at, value):
        dw_ref[:, at:at + value.shape[1]] = value if dw_in is None else value + dw_in[:, at:at + value.shape[1]]

    put(0, dwq)
    for g in range(GROUPS):
        put(384 + 128 * g, dw[:, 256 * g:256 * g + 128])
        put(768 + 128 * g, dw[:, 256 * g + 128:256 * g + 256])


def cross_kernel(rp, edge_ref, near_ref, far_ref, far_g_ref, near_stat, far_stat, kv, own_ref, w_ref, split_ref,
                 dkvs, xq, q, do, bias_a, bias_b, sc, pd, rhs, acc, tail, stats):
    odd = edge_ref[2]
    stats[1 - odd] = near_stat[...]
    stats[odd] = far_stat[...]
    window_bias(bias_a, 3, lambda krow, qrow: krow <= qrow - 1)
    window_bias(bias_b, 3, lambda krow, qrow: krow >= qrow)
    pick, pick_b = head_masks()
    clear_off_diagonal(rhs)
    sides = ((0, bias_a), (1, bias_b))

    def side_patches(side, x_row, d_row):
        lines = [None, 0, 1, 2] if side == 0 else [0, 1, 2, None]
        for pair in range(2):
            rows = lines[2 * pair:2 * pair + 2]
            at = slice(16 * pair, 16 * pair + 16)

            def store_x(cp, p, block, at=at):
                xq[cp, p, at] = block

            def store_g(cp, p, block, at=at):
                for g in range(GROUPS):
                    do[side, g, cp, p, at] = block[:, 128 * g:128 * g + 128]

            to_patches([None if r is None else x_row(r) for r in rows], split_ref, store_x)
            to_patches([None if r is None else d_row(r) for r in rows], split_ref, store_g)
        for cp in range(2):
            qs = dot(xq[cp].reshape(256, 384), w_ref[:, :384]).astype(BF)
            for g in range(GROUPS):
                q[side, g, cp] = qs[:, 128 * g:128 * g + 128].reshape(8, 32, 128)

    for parity in range(2):
        @pl.when(odd == parity)
        def _(parity=parity):
            side_patches(1 - parity, lambda r: near_ref[0, r, rp], lambda r: near_ref[1, r, rp])
            side_patches(parity, lambda r: far_ref[r], lambda r: far_g_ref[r, rp])

    def attend(step, carry):
        g, cp = step // 2, step % 2

        def score(p):
            for side, bias in sides:
                slot = 2 * (p % SLOTS) + side
                pack_heads(rhs, slot, q[side, g, cp, p], do[side, g, cp, p], pick_b)
                sc[2 * (p % 2) + side] = dot(kv[0, g, cp, p, side:side + 3].reshape(48, 256), rhs[slot], 1, 1)

        def soften(p):
            for side, bias in sides:
                slot = 2 * (p % 2) + side
                s = (sc[slot, :, :128] + bias[edge_kind(p)]) * C
                att = jnp.exp2(s - stats[side, 0, g, cp, p:p + 1])
                ds = att * (sc[slot, :, 128:] - stats[side, 1, g, cp, p:p + 1])
                pd[slot, :, :128] = ds.astype(BF)
                pd[slot, :, 128:] = att.astype(BF)

        def spread(p):
            up, down = (dot(pd[2 * (p % 2) + side], rhs[2 * (p % SLOTS) + side]).reshape(3, 16, 256) for side in range(2))
            dkv = jnp.concatenate([up[:1], up[1:] + down[:2], down[2:]], axis=0)
            head = dkv[:, :8] + own_ref[g, cp, :, 8 * p:8 * p + 8, :]
            if p > 0:
                head = head + tail[(p + 1) % 2]
            acc[:, 8 * p:8 * p + 8, :] = head
            if p < 7:
                tail[p % 2] = dkv[:, 8:]
            else:
                acc[:, 64:72, :] = dkv[:, 8:] + own_ref[g, cp, :, 64:72, :]

        for t in range(8 + 2):
            if t < 8:
                score(t)
            if 0 <= t - 1 < 8:
                soften(t - 1)
            if 0 <= t - 2 < 8:
                spread(t - 2)
        acc[:, 72:80, :] = jnp.zeros((4, 8, 256), F32)
        dkvs[g, cp, :, :, :128] = (acc[:, :, :128] * SCALE).astype(BF)
        dkvs[g, cp, :, :, 128:] = acc[:, :, 128:].astype(BF)
        return carry

    lax.fori_loop(0, 6, attend, 0)


def final_kernel(dq0_ref, dq1_ref, dkv0_ref, dkv1_ref, w_ref, unplace_ref, unsplit_ref, out_ref):
    for rp, (dq_ref, dkvs) in enumerate(((dq0_ref, dkv0_ref), (dq1_ref, dkv1_ref))):
        for pair in range(2):
            quads = [jnp.concatenate([dq_ref[g, cp, p, 16 * pair:16 * pair + 16] for g in range(GROUPS)], axis=1).astype(F32)
                     for cp in range(2) for p in range(8)]
            for sub in range(2):
                kq = 2 * pair + sub
                dqs = jnp.concatenate([t[8 * sub:8 * sub + 8] for t in quads], axis=0).astype(BF)
                parts = [jnp.concatenate([dkvs[g, 0, kq], dkvs[g, 1, kq]], axis=0) for g in range(GROUPS)]
                both = jnp.concatenate([t[:, :128] for t in parts] + [t[:, 128:] for t in parts], axis=1)
                nq = dot(unsplit_ref[...], dqs).astype(BF)
                nkv = dot(unplace_ref[...], both).astype(BF)
                out_ref[2 * kq + rp] = dot(jnp.concatenate([nq, nkv], axis=1), w_ref[...], 1, 1).astype(BF)


def after(value, *others):
    return lax.optimization_barrier((value,) + others)[0]


def exchange(x, axis, dim, bit_count, low, behind):
    count = lax.axis_size(axis)
    span = 1 << bit_count
    mine = (lax.axis_index(axis) >> low) & (span - 1)
    total = lax.dynamic_index_in_dim(x, mine, dim, keepdims=False).astype(F32)
    sent = [lax.ppermute(lax.dynamic_index_in_dim(x, mine ^ turn, dim, keepdims=False).astype(BF), axis,
                         [(i, i ^ (turn << low)) for i in range(count)]) for turn in range(1, span)]
    for block in lax.optimization_barrier((behind, *sent))[1:]:
        total = total + block.astype(F32)
    return total


def block(shape, *at):
    at = at + (0,) * (len(shape) - len(at))
    return pl.BlockSpec(shape, lambda i: at)


def whole(x):
    return block(x.shape)


SMEM = pl.BlockSpec(memory_space=pltpu.SMEM)
ANY = pl.BlockSpec(memory_space=pl.ANY)


def call(kernel, name, us, outs, out_specs, scratch, args, in_specs, aliases={}):
    return pl.pallas_call(
        kernel,
        grid=(1,),
        out_shape=[jax.ShapeDtypeStruct(s, t) for s, t in outs],
        in_specs=in_specs,
        out_specs=out_specs,
        scratch_shapes=[pltpu.VMEM(s, t) for s, t in scratch],
        compiler_params=pltpu.CompilerParams(vmem_limit_bytes=VMEM_BYTES),
        cost_estimate=pl.CostEstimate(flops=int(us * 1e9), bytes_accessed=1 << 20, transcendentals=0),
        input_output_aliases=aliases,
        name=name,
    )(*args)


def pack_call(edge, x4, g4):
    rows = x4.shape[2:]
    return pl.pallas_call(
        pack_kernel,
        out_shape=[jax.ShapeDtypeStruct(s + rows, BF) for s in ((3,), (3,), (3, 2), (2, 3, 2))],
        in_specs=[SMEM, ANY, ANY],
        out_specs=[ANY] * 4,
        scratch_shapes=[pltpu.VMEM(x4.shape, BF), pltpu.VMEM(g4.shape, BF), pltpu.SemaphoreType.DMA((7,))],
        name="pack",
    )(edge, x4, g4)


def own_call(x4, g4, w, place, split):
    outs = [((2, 3, 2, 8, 32, 128), BF), ((2, 3, 2, 8, 32, 128), BF), ((2, 2, 8, 32, 384), BF),
            ((2, 3, 2, 8, 4, 16, 256), BF), ((2, 2, 4, 80, 384), BF)]
    args = (x4, g4, w, place, split)
    return call(own_kernel, "own", 4, outs, [block(s) for s, _ in outs], [((384, 768), BF)], args, [whole(a) for a in args])


def attend_call(rp, edge, near, far, q, do, xq, kv, xk, w, place, dw):
    def kernel(*refs):
        attend_kernel(rp, *refs)

    outs = [((3, 2, 8, 32, 128), BF), ((3, 2, 4, 80, 256), F32), ((2, 3, 2, 8, 128), F32), ((384, 1152), F32)]
    args = [edge, near, far, q, do, xq, kv, xk, w, place]
    specs = [SMEM, whole(near), whole(far)] + [block((1,) + a.shape[1:], rp) for a in (q, do, xq, kv, xk)] + [whole(w), whole(place)]
    if rp == 1:
        args.append(dw)
        specs.append(whole(dw))
    return call(kernel, "attend", 12, outs, [block(s) for s, _ in outs], [
        ((2, 6, 80, 384), BF), ((3, 2, 8, 6, 16, 256), BF), ((3, 2, 6, 80, 256), F32), ((3, 160, 128), F32),
        ((384, 768), BF), ((2, 160, 256), F32), ((2, 160, 256), BF), ((SLOTS, 256, 256), BF), ((2, 10, 8, 256), F32),
    ], args, specs)


def cross_call(rp, edge, near, far, far_g, stat_near, stat_far, kv, own, w, split):
    def kernel(*refs):
        cross_kernel(rp, *refs)

    args = [edge, near, far, far_g, stat_near, stat_far, kv, own, w, split]
    specs = [SMEM] + [whole(a) for a in args[1:6]] + [block((1,) + kv.shape[1:], rp)] + [whole(a) for a in args[7:]]
    return call(kernel, "cross", 9, [((3, 2, 4, 80, 256), BF)], [block((3, 2, 4, 80, 256))], [
        ((2, 8, 32, 384), BF), ((2, 3, 2, 8, 32, 128), BF), ((2, 3, 2, 8, 32, 128), BF),
        ((3, 48, 128), F32), ((3, 48, 128), F32), ((4, 48, 256), F32), ((4, 48, 256), BF),
        ((2 * SLOTS, 256, 256), BF), ((4, 80, 256), F32), ((2, 4, 8, 256), F32), ((2, 2, 3, 2, 8, 128), F32),
    ], args, specs)[0]


def final_call(shape, *args):
    return call(final_kernel, "final", 4, [(shape, BF)], [block(shape)], [], args, [whole(a) for a in args])[0]


def shards(features, qkv_weight, grad_output):
    row_count, col_count, width = features.shape
    count = lax.axis_size("row")
    index = lax.axis_index("row")
    odd = index & 1
    near = [(i, i ^ 1) for i in range(count)]
    far = [(i, i + 1) for i in range(1, count - 1, 2)] + [(i + 1, i) for i in range(1, count - 1, 2)]
    place, split = column_maps()
    edge = jnp.stack([jnp.where(index == 0, 3, 0), jnp.where(index == count - 1, 7, 10), odd]).astype(jnp.int32)
    x4, g4 = (a.reshape(row_count // 2, 2, col_count, width) for a in (features, grad_output))
    send_x0, send_x1, send_g, send_near = pack_call(edge, x4, g4)

    far_x0 = lax.ppermute(send_x0, "row", far)
    near_xg = lax.ppermute(send_near, "row", near)
    q, do, xq, kv, xk = own_call(x4, g4, qkv_weight, place, split)
    far_x1 = lax.ppermute(after(send_x1, far_x0, xk), "row", far)
    dq0, own0, stat0, dw0 = attend_call(0, edge, near_xg, far_x0, q, do, xq, kv, xk, qkv_weight, place, None)
    far_x1 = after(far_x1, dw0)
    far_g = lax.ppermute(after(send_g, far_x1), "row", far)
    stat0_near = lax.ppermute(stat0, "row", near)
    stat0_far = lax.ppermute(stat0, "row", far)
    dq1, own1, stat1, dw1 = attend_call(1, edge, near_xg, far_x1, q, do, xq, kv, xk, qkv_weight, place, dw0)
    far_g, stat0_near, stat0_far, _ = lax.optimization_barrier((far_g, stat0_near, stat0_far, dq1))
    stat1_near = lax.ppermute(stat1, "row", near)
    stat1_far = lax.ppermute(stat1, "row", far)
    bits = count.bit_length() - 1
    rows = width // count
    dkv0 = cross_call(0, edge, near_xg, far_x0, far_g, stat0_near, stat0_far, kv, own0, qkv_weight, split)
    stat1_near, stat1_far, _ = lax.optimization_barrier((stat1_near, stat1_far, dkv0))
    total = exchange(dw1.reshape(count // 2, 2, rows, 3 * width), "row", 1, 1, 0, dkv0)
    dkv1 = cross_call(1, edge, near_xg, far_x1, far_g, stat1_near, stat1_far, kv, own1, qkv_weight, split)
    total = exchange(total.reshape(count // 4, 2, rows, 3 * width), "row", 1, 1, 1, dkv1)
    grad_features = final_call(features.shape, dq0, dq1, dkv0, dkv1, qkv_weight, place.T, split.T)
    low = 2
    while low < bits:
        step = min(2, bits - low)
        total = exchange(total.reshape(count >> (low + step), 1 << step, rows, 3 * width), "row", 1, step, low, grad_features)
        low += step
    grad_weight = total.reshape(rows, 3 * width) * (row_count * count * col_count) ** -0.5
    return grad_features, grad_weight


def solution(mesh):
    placed = (P(("group", "row"), None, None), P(), P(("group", "row"), None, None))
    return jax.shard_map(
        shards,
        mesh=mesh,
        in_specs=placed,
        out_specs=(P(("group", "row"), None, None), P(("group", "row"), None)),
        check_vma=False,
    )
```

time: 114 us -> 85.3 us (0.75)
  the two profiles are of different devices: /device:TPU:9 before, /device:TPU:0 now
where the time goes in v1:
time: 85.3 us; the launch traced here: 84.8 us
  Pallas kernels  51.8 us (61%)
  starting transfers between devices  24.7 us (29%)
  local copies, waits for them, and re-layouts  5.14 us (6%)
  other arithmetic  1.42 us (2%)
  between operations  0.96 us (1%)
    pallas_call x6, Pallas kernels, call(): pl.pallas_call(kernel, grid=(1,), out_shape=[jax.ShapeDtypeStruct(s, t) f...  48.5 us
    ppermute x5, starting transfers between devices, exchange(): lax.ppermute(lax.dynamic_index_in_dim(x, mine ^ turn, dim, keepdims=False...  9.82 us
    ppermute x1, starting transfers between devices, shards(): stat0_near = lax.ppermute(stat0, 'row', near)  6.5 us
    unnamed x30, local copies, waits for them, and re-layouts  5.01 us
    ppermute x1, starting transfers between devices, shards(): stat1_near = lax.ppermute(stat1, 'row', near)  4.38 us
    pallas_call x1, Pallas kernels, pack_call(): pl.pallas_call(pack_kernel, out_shape=[jax.ShapeDtypeStruct(s + rows, BF)...  3.25 us
  transfers between devices with their start and end apart: 13, of which 1 were waited for; matrix products, arithmetic and copies ran while one was open for 0% of the time, Pallas kernels for 57%

profile of v1, /device:TPU:0, one launch (start us, length us, event | category | flops | bytes accessed | tf_op | source)
XLA Modules:
  0.0 84.8 jit_solution(8768036091384330991)
XLA Ops:
  0.6 0.6 pad_add_fusion.edge_ref.refs_0_
  1.3 3.3 %pack.1 = (bf16[3,128,384]{2,1,0:T(8,128)(2,1)}, bf16[3,128,384]{2,1,0:T(8,128)(2,1)}, bf16[3,2,128,384]{3,2,1,0:T(8,128)(2,1)}, bf16[2,3,2,128,384]{4,3,2,1,0:T(8,128)(2,1)}) custom-call(s32[3]{0:T(128)} %pad_add_fusion.edge_ref.refs_0_, bf16[4,2,128,384]{3,2,1,0:T(8,128)(2,1)} %bitcast.23, bf16[4,2,128,384]{3,2,1,0:T(8,128)(2,1)} %bitcast.25), custom_call_target="tpu_custom_call" | custom-call | tf_op jit(solution)/shard_map/pack/pallas_call | solution.py:388
  4.5 0.5 collective-permute-start
  5.0 0.7 collective-permute-start.1
  5.7 0.0 copy-start
  5.8 1.1 %copy-done = bf16[8,128,384]{2,1,0:T(8,128)(2,1)S(1)} copy-done((bf16[8,128,384]{2,1,0:T(8,128)(2,1)S(1)}, bf16[8,128,384]{2,1,0:T(8,128)(2,1)}, u32[]{:S(2)}) %copy-start) | copy-done | bytes 786456
  6.9 1.1 %copy-done.1 = bf16[8,128,384]{2,1,0:T(8,128)(2,1)S(1)} copy-done((bf16[8,128,384]{2,1,0:T(8,128)(2,1)S(1)}, bf16[8,128,384]{2,1,0:T(8,128)(2,1)}, u32[]{:S(2)}) %copy-start.1) | copy-done | bytes 786456
  8.0 1.2 %copy-done.3 = bf16[384,1152]{1,0:T(8,128)(2,1)S(1)} copy-done((bf16[384,1152]{1,0:T(8,128)(2,1)S(1)}, bf16[384,1152]{1,0:T(8,128)(2,1)}, u32[]{:S(2)}) %copy-start.3) | copy-done | bytes 884760
  9.2 0.8 copy-done.6
  10.0 0.8 copy-done.9
  10.7 3.1 %own.1 = (bf16[2,3,2,8,32,128]{5,4,3,2,1,0:T(8,128)(2,1)S(1)}, bf16[2,3,2,8,32,128]{5,4,3,2,1,0:T(8,128)(2,1)S(1)}, bf16[2,2,8,32,384]{4,3,2,1,0:T(8,128)(2,1)S(...) custom-call(bf16[4,2,128,384]{3,2,1,0:T(8,128)(2,1)S(1)} %bitcast.24, ...), custom_call_target="tpu_custom_call" | custom-call | flops 4000000000 | bytes 1048576 | tf_op jit(solution)/shard_map/own/pallas_call | solution.py:372
  13.8 0.0 collective-permute-done.1.refs_2_
  13.9 0.7 collective-permute-start.2
  14.6 0.0 collective-permute-done.refs_1_
  14.6 0.0 copy-start.13
  14.6 11.6 %attend.2 = (bf16[3,2,8,32,128]{4,3,2,1,0:T(8,128)(2,1)S(1)}, f32[3,2,4,80,256]{4,3,2,1,0:T(8,128)S(1)}, f32[2,3,2,8,128]{4,3,2,1,0:T(8,128)S(1)}, f32[384,1152]{1,0:T(8,128)S(1)}) custom-call(s32[3]{0:T(128)S(1)} %copy-done.2, bf16[2,3,2,128,384]{4,3,2,1,0:T(8,128)(2,1)S(1)} %collective-permute-done.refs_1_, ...), custom_call_target="tpu_custom_call" | custom-call | flops 12000000000 | bytes 1048576 | tf_op jit(solution)/shard_map/attend/pallas_call | solution.py:372
  26.2 0.0 copy-done.11
  26.2 6.5 %collective-permute-start.4 = (f32[2,3,2,8,128]{4,3,2,1,0:T(8,128)S(1)}, f32[2,3,2,8,128]{4,3,2,1,0:T(8,128)S(1)}, u32[]{:S(2)}, u32[]{:S(2)}) collective-permute-start(f32[2,3,2,8,128]{4,3,2,1,0:T(8,128)S(1)} %get-tuple-element.47), channel_id=1, source_target_pairs={{0,1},{1,0},{2,3},{3,2},{4,5},{5,4},{6,7},{7,6},{8,9},{9,8},{10,11... | collective-permute-start | bytes 147464 | tf_op jit(solution)/shard_map/ppermute | solution.py:457
  32.7 0.7 collective-permute-start.5
  33.3 0.0 collective-permute-done.2.refs_2_
  33.4 0.0 copy-start.10
  33.4 0.8 collective-permute-start.3
  34.2 12.5 %attend.3 = (bf16[3,2,8,32,128]{4,3,2,1,0:T(8,128)(2,1)S(1)}, f32[3,2,4,80,256]{4,3,2,1,0:T(8,128)S(1)}, f32[2,3,2,8,128]{4,3,2,1,0:T(8,128)S(1)}, f32[384,1152]{1,0:T(8,128)S(1)}) custom-call(s32[3]{0:T(128)S(1)} %copy-done.2, bf16[2,3,2,128,384]{4,3,2,1,0:T(8,128)(2,1)S(1)} %collective-permute-done.refs_1_, ...), custom_call_target="tpu_custom_call" | custom-call | flops 12000000000 | bytes 1048576 | tf_op jit(solution)/shard_map/attend/pallas_call | solution.py:372
  46.8 4.4 %collective-permute-start.6 = (f32[2,3,2,8,128]{4,3,2,1,0:T(8,128)S(1)}, f32[2,3,2,8,128]{4,3,2,1,0:T(8,128)S(1)}, u32[]{:S(2)}, u32[]{:S(2)}) collective-permute-start(f32[2,3,2,8,128]{4,3,2,1,0:T(8,128)S(1)} %get-tuple-element.52), channel_id=1, source_target_pairs={{0,1},{1,0},{2,3},{3,2},{4,5},{5,4},{6,7},{7,6},{8,9},{9,8},{10,11... | collective-permute-start | bytes 147464 | tf_op jit(solution)/shard_map/ppermute | solution.py:461
  51.2 0.7 collective-permute-start.7
  51.8 0.1 fusion
  51.9 0.0 collective-permute-done.4.refs_4_
  51.9 4.0 %collective-permute-start.8 = (bf16[8,24,1152]{2,1,0:T(8,128)(2,1)S(1)}, bf16[8,24,1152]{2,1,0:T(8,128)(2,1)S(1)}, u32[]{:S(2)}, u32[]{:S(2)}) collective-permute-start(bf16[8,24,1152]{2,1,0:T(8,128)(2,1)S(1)} %fusion), channel_id=1, source_target_pairs={{0,1},{1,0},{2,3},{3,2},{4,5},{5,4},{6,7},{7,6},{8,9},{9,8},{10,11... | collective-permute-start | bytes 1327112 | tf_op jit(solution)/shard_map/ppermute | solution.py:351
  55.9 0.0 collective-permute-done.5.refs_5_
  55.9 0.0 collective-permute-done.3.refs_3_
  55.9 0.0 copy-done.10
  55.9 8.9 %cross.2.dkv0_ref = bf16[3,2,4,80,256]{4,3,2,1,0:T(8,128)(2,1)S(1)} custom-call(s32[3]{0:T(128)S(1)} %copy-done.2, bf16[2,3,2,128,384]{4,3,2,1,0:T(8,128)(2,1)S(1)} %collective-permute-done.refs_1_, bf16[3,128,384]{2,1,0:T(8,128)(2,1)S(1)} %collective-permute-done.1.refs_2_, bf16[3,2,128,384]{3,2,1,0:T(8,128)(2,1)S(1)} %collective-permute-done.3.refs_3_, ...), custom_call_target="tpu_custom_call" | custom-call | flops 8999999488 | bytes 1048576 | tf_op jit(solution)/shard_map/cross/pallas_call | solution.py:372
  64.8 0.0 collective-permute-done.8
  64.8 0.1 bitcast_add_fusion
  64.9 1.4 %collective-permute-start.9 = (bf16[4,24,1152]{2,1,0:T(8,128)(2,1)S(1)}, bf16[4,24,1152]{2,1,0:T(8,128)(2,1)S(1)}, u32[]{:S(2)}, u32[]{:S(2)}) collective-permute-start(bf16[4,24,1152]{2,1,0:T(8,128)(2,1)S(1)} %fusion.1), channel_id=1, source_target_pairs={{0,2},{1,3},{2,0},{3,1},{4,6},{5,7},{6,4},{7,5},{8,10},{9,11},{10,... | collective-permute-start | bytes 663560 | tf_op jit(solution)/shard_map/ppermute | solution.py:351
  66.3 0.0 collective-permute-done.6.refs_4_
  66.3 0.0 collective-permute-done.7.refs_5_
  66.3 0.0 copy-start.8
  66.3 8.7 %cross.3.dkv1_ref = bf16[3,2,4,80,256]{4,3,2,1,0:T(8,128)(2,1)S(1)} custom-call(s32[3]{0:T(128)S(1)} %copy-done.2, bf16[2,3,2,128,384]{4,3,2,1,0:T(8,128)(2,1)S(1)} %collective-permute-done.refs_1_, bf16[3,128,384]{2,1,0:T(8,128)(2,1)S(1)} %collective-permute-done.2.refs_2_, bf16[3,2,128,384]{3,2,1,0:T(8,128)(2,1)S(1)} %collective-permute-done.3.refs_3_, ...), custom_call_target="tpu_custom_call" | custom-call | flops 8999999488 | bytes 1048576 | tf_op jit(solution)/shard_map/cross/pallas_call | solution.py:372
  75.0 0.0 collective-permute-done.9
  75.1 1.6 %collective-permute-start.10 = (bf16[1,24,1152]{2,1,0:T(8,128)(2,1)S(1)}, bf16[1,24,1152]{2,1,0:T(8,128)(2,1)S(1)}, u32[]{:S(2)}, u32[]{:S(2)}) collective-permute-start(bf16[1,24,1152]{2,1,0:T(8,128)(2,1)S(1)} %get-tuple-element.64), channel_id=1, source_target_pairs={{0,4},{1,5},{2,6},{3,7},{4,0},{5,1},{6,2},{7,3},{8,12},{9,13},{10,... | collective-permute-start | bytes 165896 | tf_op jit(solution)/shard_map/ppermute | solution.py:351
  76.8 1.3 %collective-permute-start.11 = (bf16[1,24,1152]{2,1,0:T(8,128)(2,1)S(1)}, bf16[1,24,1152]{2,1,0:T(8,128)(2,1)S(1)}, u32[]{:S(2)}, u32[]{:S(2)}) collective-permute-start(bf16[1,24,1152]{2,1,0:T(8,128)(2,1)S(1)} %get-tuple-element.63), channel_id=1, source_target_pairs={{0,8},{1,9},{2,10},{3,11},{4,12},{5,13},{6,14},{7,15},{8,0},{9,1},... | collective-permute-start | bytes 165896 | tf_op jit(solution)/shard_map/ppermute | solution.py:351
  78.1 1.5 %collective-permute-start.12 = (bf16[1,24,1152]{2,1,0:T(8,128)(2,1)S(1)}, bf16[1,24,1152]{2,1,0:T(8,128)(2,1)S(1)}, u32[]{:S(2)}, u32[]{:S(2)}) collective-permute-start(bf16[1,24,1152]{2,1,0:T(8,128)(2,1)S(1)} %get-tuple-element.62), channel_id=1, source_target_pairs={{0,12},{1,13},{2,14},{3,15},{4,8},{5,9},{6,10},{7,11},{8,4},{9,5},... | collective-permute-start | bytes 165896 | tf_op jit(solution)/shard_map/ppermute | solution.py:351
  79.6 3.8 %final.1 = bf16[8,128,384]{2,1,0:T(8,128)(2,1)} custom-call(bf16[3,2,8,32,128]{4,3,2,1,0:T(8,128)(2,1)S(1)} %get-tuple-element.39.dq0_ref, bf16[3,2,8,32,128]{4,3,2,1,0:T(8,128)(2,1)S(1)} %get-tuple-element.44.dq1_ref, bf16[3,2,4,80,256]{4,3,2,1,0:T(8,128)(2,1)S(1)} %cross.2.dkv0_ref, bf16[3,2,4,80,256]{4,3,2,1,0:T(8,128)(2,1)S(1)} %cross.3.dkv1_ref, ...), custom_call_target="tpu_custom_call" | custom-call | flops 4000000000 | bytes 1048576 | tf_op jit(solution)/shard_map/final/pallas_call | solution.py:372
  83.3 0.0 collective-permute-done.10
  83.3 0.0 collective-permute-done.11
  83.3 0.8 collective-permute-done.12
  84.1 0.7 multiply_bitcast_fusion
  (22 shorter events, 0.2 us)
Async XLA Ops:
  4.5 10.0 %collective-permute-start = (bf16[2,3,2,128,384]{4,3,2,1,0:T(8,128)(2,1)}, bf16[2,3,2,128,384]{4,3,2,1,0:T(8,128)(2,1)S(1)}, u32[]{:S(2)}, u32[]{:S(2)}) collective-permute-start(bf16[2,3,2,128,384]{4,3,2,1,0:T(8,128)(2,1)} %get-tuple-element.32), channel_id=1, source_target_pairs={{0,1},{1,0},{2,3},{3,2},{4,5},{5,4},{6,7},{7,6},{8,9},{9,8},{10,11... | collective-permute-start | bytes 3538952 | tf_op jit(solution)/shard_map/ppermute | solution.py:451
  5.0 8.8 %collective-permute-start.1 = (bf16[3,128,384]{2,1,0:T(8,128)(2,1)}, bf16[3,128,384]{2,1,0:T(8,128)(2,1)S(1)}, u32[]{:S(2)}, u32[]{:S(2)}) collective-permute-start(bf16[3,128,384]{2,1,0:T(8,128)(2,1)} %get-tuple-element.33), channel_id=1, source_target_pairs={{1,2},{3,4},{5,6},{7,8},{9,10},{11,12},{13,14},{2,1},{4,3},{6,5},{... | collective-permute-start | bytes 884744 | tf_op jit(solution)/shard_map/ppermute | solution.py:450
  5.7 1.1 %copy-start = (bf16[8,128,384]{2,1,0:T(8,128)(2,1)S(1)}, bf16[8,128,384]{2,1,0:T(8,128)(2,1)}, u32[]{:S(2)}) copy-start(bf16[8,128,384]{2,1,0:T(8,128)(2,1)} %param.5) | copy-start | bytes 2359300
  6.9 1.1 %copy-start.1 = (bf16[8,128,384]{2,1,0:T(8,128)(2,1)S(1)}, bf16[8,128,384]{2,1,0:T(8,128)(2,1)}, u32[]{:S(2)}) copy-start(bf16[8,128,384]{2,1,0:T(8,128)(2,1)} %param.7) | copy-start | bytes 2359300
  8.0 1.2 %copy-start.3 = (bf16[384,1152]{1,0:T(8,128)(2,1)S(1)}, bf16[384,1152]{1,0:T(8,128)(2,1)}, u32[]{:S(2)}) copy-start(bf16[384,1152]{1,0:T(8,128)(2,1)} %w_ref.3) | copy-start | bytes 2654212
  9.2 0.8 copy-start.6
  10.0 0.8 copy-start.9
  10.7 3.1 %copy-start.14 = (bf16[3,128,384]{2,1,0:T(8,128)(2,1)S(1)}, bf16[3,128,384]{2,1,0:T(8,128)(2,1)}, u32[]{:S(2)}) copy-start(bf16[3,128,384]{2,1,0:T(8,128)(2,1)} %get-tuple-element.41) | copy-start | bytes 884740
  10.7 3.8 %copy-start.2 = (s32[3]{0:T(128)S(1)}, s32[3]{0:T(128)}, u32[]{:S(2)}) copy-start(s32[3]{0:T(128)} %pad_add_fusion.edge_ref.refs_0_) | copy-start | bytes 40
  10.7 3.9 %copy-start.4 = (bf16[384,1152]{1,0:T(8,128)(2,1)S(1)}, bf16[384,1152]{1,0:T(8,128)(2,1)}, u32[]{:S(2)}) copy-start(bf16[384,1152]{1,0:T(8,128)(2,1)} %w_ref.3) | copy-start | bytes 2654212
  10.7 3.9 %copy-start.7 = (bf16[160,128]{1,0:T(8,128)(2,1)S(1)}, bf16[160,128]{1,0:T(8,128)(2,1)}, u32[]{:S(2)}) copy-start(bf16[160,128]{1,0:T(8,128)(2,1)} %constant.47.clone.place_ref.refs_9_) | copy-start | bytes 122884
  13.8 12.3 %copy-start.11 = (bf16[2,3,2,8,4,16,256]{6,5,4,3,2,1,0:T(8,128)(2,1)}, bf16[2,3,2,8,4,16,256]{6,5,4,3,2,1,0:T(8,128)(2,1)S(1)}, u32[]{:S(2)}) copy-start(bf16[2,3,2,8,4,16,256]{6,5,4,3,2,1,0:T(8,128)(2,1)S(1)} %get-tuple-element.37.refs_6_) | copy-start | bytes 9437188
  13.9 19.5 %collective-permute-start.2 = (bf16[3,128,384]{2,1,0:T(8,128)(2,1)S(1)}, bf16[3,128,384]{2,1,0:T(8,128)(2,1)S(1)}, u32[]{:S(2)}, u32[]{:S(2)}) collective-permute-start(bf16[3,128,384]{2,1,0:T(8,128)(2,1)S(1)} %copy-done.14), channel_id=1, source_target_pairs={{1,2},{3,4},{5,6},{7,8},{9,10},{11,12},{13,14},{2,1},{4,3},{6,5},{... | collective-permute-start | bytes 884744 | tf_op jit(solution)/shard_map/ppermute | solution.py:453
  14.6 18.8 %copy-start.13 = (bf16[3,2,128,384]{3,2,1,0:T(8,128)(2,1)S(1)}, bf16[3,2,128,384]{3,2,1,0:T(8,128)(2,1)}, u32[]{:S(2)}) copy-start(bf16[3,2,128,384]{3,2,1,0:T(8,128)(2,1)} %get-tuple-element.46) | copy-start | bytes 1769476
  26.2 25.7 %collective-permute-start.4 = (f32[2,3,2,8,128]{4,3,2,1,0:T(8,128)S(1)}, f32[2,3,2,8,128]{4,3,2,1,0:T(8,128)S(1)}, u32[]{:S(2)}, u32[]{:S(2)}) collective-permute-start(f32[2,3,2,8,128]{4,3,2,1,0:T(8,128)S(1)} %get-tuple-element.47), channel_id=1, source_target_pairs={{0,1},{1,0},{2,3},{3,2},{4,5},{5,4},{6,7},{7,6},{8,9},{9,8},{10,11... | collective-permute-start | bytes 147464 | tf_op jit(solution)/shard_map/ppermute | solution.py:457
  32.7 23.2 %collective-permute-start.5 = (f32[2,3,2,8,128]{4,3,2,1,0:T(8,128)S(1)}, f32[2,3,2,8,128]{4,3,2,1,0:T(8,128)S(1)}, u32[]{:S(2)}, u32[]{:S(2)}) collective-permute-start(f32[2,3,2,8,128]{4,3,2,1,0:T(8,128)S(1)} %get-tuple-element.47), channel_id=1, source_target_pairs={{1,2},{3,4},{5,6},{7,8},{9,10},{11,12},{13,14},{2,1},{4,3},{6,5},{... | collective-permute-start | bytes 147464 | tf_op jit(solution)/shard_map/ppermute | solution.py:458
  33.4 22.5 %copy-start.10 = (bf16[128,128]{1,0:T(8,128)(2,1)S(1)}, bf16[128,128]{1,0:T(8,128)(2,1)}, u32[]{:S(2)}) copy-start(bf16[128,128]{1,0:T(8,128)(2,1)} %constant.48.clone.split_ref.refs_9_) | copy-start | bytes 98308
  33.4 22.5 %copy-start.12 = (bf16[2,3,2,8,4,16,256]{6,5,4,3,2,1,0:T(8,128)(2,1)S(1)}, bf16[2,3,2,8,4,16,256]{6,5,4,3,2,1,0:T(8,128)(2,1)}, u32[]{:S(2)}) copy-start(bf16[2,3,2,8,4,16,256]{6,5,4,3,2,1,0:T(8,128)(2,1)} %copy-done.11) | copy-start | bytes 9437188
  33.4 22.5 %collective-permute-start.3 = (bf16[3,2,128,384]{3,2,1,0:T(8,128)(2,1)S(1)}, bf16[3,2,128,384]{3,2,1,0:T(8,128)(2,1)S(1)}, u32[]{:S(2)}, u32[]{:S(2)}) collective-permute-start(bf16[3,2,128,384]{3,2,1,0:T(8,128)(2,1)S(1)} %copy-done.13), channel_id=1, source_target_pairs={{1,2},{3,4},{5,6},{7,8},{9,10},{11,12},{13,14},{2,1},{4,3},{6,5},{... | collective-permute-start | bytes 1769480 | tf_op jit(solution)/shard_map/ppermute | solution.py:456
  46.8 19.5 %collective-permute-start.6 = (f32[2,3,2,8,128]{4,3,2,1,0:T(8,128)S(1)}, f32[2,3,2,8,128]{4,3,2,1,0:T(8,128)S(1)}, u32[]{:S(2)}, u32[]{:S(2)}) collective-permute-start(f32[2,3,2,8,128]{4,3,2,1,0:T(8,128)S(1)} %get-tuple-element.52), channel_id=1, source_target_pairs={{0,1},{1,0},{2,3},{3,2},{4,5},{5,4},{6,7},{7,6},{8,9},{9,8},{10,11... | collective-permute-start | bytes 147464 | tf_op jit(solution)/shard_map/ppermute | solution.py:461
  51.2 15.2 %collective-permute-start.7 = (f32[2,3,2,8,128]{4,3,2,1,0:T(8,128)S(1)}, f32[2,3,2,8,128]{4,3,2,1,0:T(8,128)S(1)}, u32[]{:S(2)}, u32[]{:S(2)}) collective-permute-start(f32[2,3,2,8,128]{4,3,2,1,0:T(8,128)S(1)} %get-tuple-element.52), channel_id=1, source_target_pairs={{1,2},{3,4},{5,6},{7,8},{9,10},{11,12},{13,14},{2,1},{4,3},{6,5},{... | collective-permute-start | bytes 147464 | tf_op jit(solution)/shard_map/ppermute | solution.py:462
  51.9 12.9 %collective-permute-start.8 = (bf16[8,24,1152]{2,1,0:T(8,128)(2,1)S(1)}, bf16[8,24,1152]{2,1,0:T(8,128)(2,1)S(1)}, u32[]{:S(2)}, u32[]{:S(2)}) collective-permute-start(bf16[8,24,1152]{2,1,0:T(8,128)(2,1)S(1)} %fusion), channel_id=1, source_target_pairs={{0,1},{1,0},{2,3},{3,2},{4,5},{5,4},{6,7},{7,6},{8,9},{9,8},{10,11... | collective-permute-start | bytes 1327112 | tf_op jit(solution)/shard_map/ppermute | solution.py:351
  64.9 10.1 %collective-permute-start.9 = (bf16[4,24,1152]{2,1,0:T(8,128)(2,1)S(1)}, bf16[4,24,1152]{2,1,0:T(8,128)(2,1)S(1)}, u32[]{:S(2)}, u32[]{:S(2)}) collective-permute-start(bf16[4,24,1152]{2,1,0:T(8,128)(2,1)S(1)} %fusion.1), channel_id=1, source_target_pairs={{0,2},{1,3},{2,0},{3,1},{4,6},{5,7},{6,4},{7,5},{8,10},{9,11},{10,... | collective-permute-start | bytes 663560 | tf_op jit(solution)/shard_map/ppermute | solution.py:351
  66.3 13.3 %copy-start.5 = (bf16[128,160]{1,0:T(8,128)(2,1)S(1)}, bf16[128,160]{1,0:T(8,128)(2,1)}, u32[]{:S(2)}) copy-start(bf16[128,160]{1,0:T(8,128)(2,1)} %constant.51.unplace_ref) | copy-start | bytes 122884
  66.3 13.3 %copy-start.8 = (bf16[128,128]{1,0:T(8,128)(2,1)S(1)}, bf16[128,128]{1,0:T(8,128)(2,1)}, u32[]{:S(2)}) copy-start(bf16[128,128]{1,0:T(8,128)(2,1)} %constant.52.unsplit_ref) | copy-start | bytes 98308
  75.1 8.2 %collective-permute-start.10 = (bf16[1,24,1152]{2,1,0:T(8,128)(2,1)S(1)}, bf16[1,24,1152]{2,1,0:T(8,128)(2,1)S(1)}, u32[]{:S(2)}, u32[]{:S(2)}) collective-permute-start(bf16[1,24,1152]{2,1,0:T(8,128)(2,1)S(1)} %get-tuple-element.64), channel_id=1, source_target_pairs={{0,4},{1,5},{2,6},{3,7},{4,0},{5,1},{6,2},{7,3},{8,12},{9,13},{10,... | collective-permute-start | bytes 165896 | tf_op jit(solution)/shard_map/ppermute | solution.py:351
  76.8 6.6 %collective-permute-start.11 = (bf16[1,24,1152]{2,1,0:T(8,128)(2,1)S(1)}, bf16[1,24,1152]{2,1,0:T(8,128)(2,1)S(1)}, u32[]{:S(2)}, u32[]{:S(2)}) collective-permute-start(bf16[1,24,1152]{2,1,0:T(8,128)(2,1)S(1)} %get-tuple-element.63), channel_id=1, source_target_pairs={{0,8},{1,9},{2,10},{3,11},{4,12},{5,13},{6,14},{7,15},{8,0},{9,1},... | collective-permute-start | bytes 165896 | tf_op jit(solution)/shard_map/ppermute | solution.py:351
  78.1 6.1 %collective-permute-start.12 = (bf16[1,24,1152]{2,1,0:T(8,128)(2,1)S(1)}, bf16[1,24,1152]{2,1,0:T(8,128)(2,1)S(1)}, u32[]{:S(2)}, u32[]{:S(2)}) collective-permute-start(bf16[1,24,1152]{2,1,0:T(8,128)(2,1)S(1)} %get-tuple-element.62), channel_id=1, source_target_pairs={{0,12},{1,13},{2,14},{3,15},{4,8},{5,9},{6,10},{7,11},{8,4},{9,5},... | collective-permute-start | bytes 165896 | tf_op jit(solution)/shard_map/ppermute | solution.py:351

commit v2 on v1

--- a/solution.py
+++ b/solution.py
@@ -11,7 +11,10 @@
 DILATION = 2
 HALO = 6
 GROUPS = 3
-SLOTS = 4
+UNITS = 16
+LAG = 3
+SLOTS = 2 * LAG + 1
+CROSS_UNITS = 16
 BF = jnp.bfloat16
 F32 = jnp.float32
 SCALE = 32 ** -0.5
@@ -158,25 +161,29 @@
     clear_off_diagonal(rhs)
 
     def attend(step, carry):
-        g, cp = step // 2, step % 2
-
-        def keys(p):
+        def place_of(u):
+            index = step * (UNITS // 8) + u // 8
+            return index // 2, (index % 2 if UNITS == 8 else u // 8), u % 8
+
+        def keys(u):
+            g, cp, p = place_of(u)
             return jnp.concatenate([
                 kvh[g, cp, p, :3].reshape(48, 256),
                 kv[0, g, cp, p].reshape(64, 256),
                 kvh[g, cp, p, 3:].reshape(48, 256)], axis=0)
 
-        def score(p):
-            slot = p % SLOTS
-            pack_heads(rhs, slot, q[0, g, cp, p], do[0, g, cp, p], pick_b)
-            sc[p % 2] = dot(keys(p), rhs[slot], 1, 1)
-
-        def soften(p):
-            slot = p % 2
-            s = sc[slot, :, :128] + bias[edge_kind(p)]
+        def score(u):
+            g, cp, p = place_of(u)
+            pack_heads(rhs, u % SLOTS, q[0, g, cp, p], do[0, g, cp, p], pick_b)
+            sc[u % (LAG + 1)] = dot(keys(u), rhs[u % SLOTS], 1, 1)
+
+        def soften(u):
+            g, cp, p = place_of(u)
+            now, slot = u % (LAG + 1), u % (LAG + 1)
+            s = sc[now, :, :128] + bias[edge_kind(p)]
             m = jnp.max(s, axis=0, keepdims=True)
             e = jnp.exp2((s - m) * C)
-            dp = sc[slot, :, 128:]
+            dp = sc[now, :, 128:]
             total = jnp.sum(e, axis=0, keepdims=True)
             inv = 1.0 / total
             delta = jnp.sum(e * dp, axis=0, keepdims=True) * inv
@@ -186,39 +193,41 @@
             stat_ref[0, g, cp, p:p + 1] = m * C + jnp.log2(total)
             stat_ref[1, g, cp, p:p + 1] = delta
 
-        def add_to(at, value):
-            acc[g, cp, :3, at, :] = value[:3]
-            own_ref[g, cp, :, at, :] = value[3:7]
-            acc[g, cp, 3:, at, :] = value[7:]
-
-        def spread(p):
-            slot = p % 2
-            dkv = dot(pd[slot], rhs[p % SLOTS]).reshape(10, 16, 256)
+        def spread(u):
+            g, cp, p = place_of(u)
+            slot = u % (LAG + 1)
+
+            def add_to(at, value):
+                acc[g, cp, :3, at, :] = value[:3]
+                own_ref[g, cp, :, at, :] = value[3:7]
+                acc[g, cp, 3:, at, :] = value[7:]
+
+            dkv = dot(pd[slot], rhs[u % SLOTS]).reshape(10, 16, 256)
             head = dkv[:, :8]
             if p > 0:
                 head = head + tail[(p + 1) % 2]
             add_to(slice(8 * p, 8 * p + 8), head)
             if p < 7:
-                tail[slot] = dkv[:, 8:]
+                tail[p % 2] = dkv[:, 8:]
             else:
                 add_to(slice(64, 72), dkv[:, 8:])
-            full = dot(pd[slot, :, :128], keys(p)[:, :128], 0, 0)
+                add_to(slice(72, 80), jnp.zeros((10, 8, 256), F32))
+            full = dot(pd[slot, :, :128], keys(u)[:, :128], 0, 0)
             dq = jnp.where(pick[3], full[96:], 0.0)
             for h in range(3):
                 dq = jnp.where(pick[h], full[32 * h:32 * h + 32], dq)
             dq_ref[g, cp, p] = (dq * SCALE).astype(BF)
 
-        for t in range(8 + 2):
-            if t < 8:
+        for t in range(UNITS + 2 * LAG):
+            if t < UNITS:
                 score(t)
-            if 0 <= t - 1 < 8:
-                soften(t - 1)
-            if 0 <= t - 2 < 8:
-                spread(t - 2)
-        add_to(slice(72, 80), jnp.zeros((10, 8, 256), F32))
+            if 0 <= t - LAG < UNITS:
+                soften(t - LAG)
+            if 0 <= t - 2 * LAG < UNITS:
+                spread(t - 2 * LAG)
         return carry
 
-    lax.fori_loop(0, 6, attend, 0)
+    lax.fori_loop(0, 48 // UNITS, attend, 0)
 
     dw = jnp.zeros((384, 768), F32)
     dwq = jnp.zeros((384, 384), F32)
@@ -243,15 +252,19 @@
 
 
 def cross_kernel(rp, edge_ref, near_ref, far_ref, far_g_ref, near_stat, far_stat, kv, own_ref, w_ref, split_ref,
-                 dkvs, xq, q, do, bias_a, bias_b, sc, pd, rhs, acc, tail, stats):
+                 dkvs, xq, q, do, bias, sc, pd, rhs, acc, tail, stats):
     odd = edge_ref[2]
-    stats[1 - odd] = near_stat[...]
-    stats[odd] = far_stat[...]
-    window_bias(bias_a, 3, lambda krow, qrow: krow <= qrow - 1)
-    window_bias(bias_b, 3, lambda krow, qrow: krow >= qrow)
+    stats[:, :, :, :, :128] = jnp.where(odd == 1, near_stat[...], far_stat[...])
+    stats[:, :, :, :, 128:] = jnp.where(odd == 1, far_stat[...], near_stat[...])
+    key = lax.broadcasted_iota(jnp.int32, (64, 256), 0)
+    lane = lax.broadcasted_iota(jnp.int32, (64, 256), 1)
+    krow, kcol, qrow = key // 16, key % 16, (lane % 32) // 8
+    dcol = kcol - lane % 8
+    ok = ((lane < 128) & (krow < qrow)) | ((lane >= 128) & (krow > qrow))
+    ok = ok & (dcol >= 0) & (dcol <= 6)
+    for which, extra in enumerate((kcol >= 3, kcol >= 0, kcol < 11)):
+        bias[which] = jnp.where(ok & extra, 0.0, -1e30).astype(F32)
     pick, pick_b = head_masks()
-    clear_off_diagonal(rhs)
-    sides = ((0, bias_a), (1, bias_b))
 
     def side_patches(side, x_row, d_row):
         lines = [None, 0, 1, 2] if side == 0 else [0, 1, 2, None]
@@ -280,48 +293,58 @@
             side_patches(parity, lambda r: far_ref[r], lambda r: far_g_ref[r, rp])
 
     def attend(step, carry):
-        g, cp = step // 2, step % 2
-
-        def score(p):
-            for side, bias in sides:
-                slot = 2 * (p % SLOTS) + side
-                pack_heads(rhs, slot, q[side, g, cp, p], do[side, g, cp, p], pick_b)
-                sc[2 * (p % 2) + side] = dot(kv[0, g, cp, p, side:side + 3].reshape(48, 256), rhs[slot], 1, 1)
-
-        def soften(p):
-            for side, bias in sides:
-                slot = 2 * (p % 2) + side
-                s = (sc[slot, :, :128] + bias[edge_kind(p)]) * C
-                att = jnp.exp2(s - stats[side, 0, g, cp, p:p + 1])
-                ds = att * (sc[slot, :, 128:] - stats[side, 1, g, cp, p:p + 1])
-                pd[slot, :, :128] = ds.astype(BF)
-                pd[slot, :, 128:] = att.astype(BF)
-
-        def spread(p):
-            up, down = (dot(pd[2 * (p % 2) + side], rhs[2 * (p % SLOTS) + side]).reshape(3, 16, 256) for side in range(2))
-            dkv = jnp.concatenate([up[:1], up[1:] + down[:2], down[2:]], axis=0)
-            head = dkv[:, :8] + own_ref[g, cp, :, 8 * p:8 * p + 8, :]
-            if p > 0:
-                head = head + tail[(p + 1) % 2]
-            acc[:, 8 * p:8 * p + 8, :] = head
-            if p < 7:
-                tail[p % 2] = dkv[:, 8:]
-            else:
-                acc[:, 64:72, :] = dkv[:, 8:] + own_ref[g, cp, :, 64:72, :]
-
-        for t in range(8 + 2):
-            if t < 8:
+        def place_of(u):
+            index = step * (CROSS_UNITS // 8) + u // 8
+            return index // 2, (index % 2 if CROSS_UNITS == 8 else u // 8), u % 8
+
+        def score(u):
+            g, cp, p = place_of(u)
+            slot = u % SLOTS
+            for side in range(2):
+                for h in range(4):
+                    at = slice(128 * side + 32 * h, 128 * side + 32 * h + 32)
+                    rhs[slot, 0, at] = q[side, g, cp, p] * pick_b[h]
+                    rhs[slot, 1, at] = do[side, g, cp, p] * pick_b[h]
+            keys = kv[0, g, cp, p].reshape(64, 256)
+            for part in range(2):
+                sc[u % (LAG + 1), part] = dot(keys[:, 128 * part:128 * part + 128], rhs[slot, part], 1, 1)
+
+        def soften(u):
+            g, cp, p = place_of(u)
+            now = u % (LAG + 1)
+            s = (sc[now, 0] + bias[edge_kind(p)]) * C
+            att = jnp.exp2(s - stats[0, g, cp, p:p + 1])
+            pd[now, 0] = (att * (sc[now, 1] - stats[1, g, cp, p:p + 1])).astype(BF)
+            pd[now, 1] = att.astype(BF)
+
+        def spread(u):
+            g, cp, p = place_of(u)
+            for part in range(2):
+                lanes = slice(128 * part, 128 * part + 128)
+                value = dot(pd[u % (LAG + 1), part], rhs[u % SLOTS, part]).reshape(4, 16, 128)
+                head = value[:, :8] + own_ref[g, cp, :, 8 * p:8 * p + 8, lanes]
+                if p > 0:
+                    head = head + tail[(p + 1) % 2, :, :, lanes]
+                acc[:, 8 * p:8 * p + 8, lanes] = head
+                if p < 7:
+                    tail[p % 2, :, :, lanes] = value[:, 8:]
+                else:
+                    acc[:, 64:72, lanes] = value[:, 8:] + own_ref[g, cp, :, 64:72, lanes]
+            if p == 7:
+                acc[:, 72:80, :] = jnp.zeros((4, 8, 256), F32)
+                dkvs[g, cp, :, :, :128] = (acc[:, :, :128] * SCALE).astype(BF)
+                dkvs[g, cp, :, :, 128:] = acc[:, :, 128:].astype(BF)
+
+        for t in range(CROSS_UNITS + 2 * LAG):
+            if t < CROSS_UNITS:
                 score(t)
-            if 0 <= t - 1 < 8:
-                soften(t - 1)
-            if 0 <= t - 2 < 8:
-                spread(t - 2)
-        acc[:, 72:80, :] = jnp.zeros((4, 8, 256), F32)
-        dkvs[g, cp, :, :, :128] = (acc[:, :, :128] * SCALE).astype(BF)
-        dkvs[g, cp, :, :, 128:] = acc[:, :, 128:].astype(BF)
+            if 0 <= t - LAG < CROSS_UNITS:
+                soften(t - LAG)
+            if 0 <= t - 2 * LAG < CROSS_UNITS:
+                spread(t - 2 * LAG)
         return carry
 
-    lax.fori_loop(0, 6, attend, 0)
+    lax.fori_loop(0, 48 // CROSS_UNITS, attend, 0)
 
 
 def final_kernel(dq0_ref, dq1_ref, dkv0_ref, dkv1_ref, w_ref, unplace_ref, unsplit_ref, out_ref):
@@ -414,7 +437,7 @@
         specs.append(whole(dw))
     return call(kernel, "attend", 12, outs, [block(s) for s, _ in outs], [
         ((2, 6, 80, 384), BF), ((3, 2, 8, 6, 16, 256), BF), ((3, 2, 6, 80, 256), F32), ((3, 160, 128), F32),
-        ((384, 768), BF), ((2, 160, 256), F32), ((2, 160, 256), BF), ((SLOTS, 256, 256), BF), ((2, 10, 8, 256), F32),
+        ((384, 768), BF), ((LAG + 1, 160, 256), F32), ((LAG + 1, 160, 256), BF), ((SLOTS, 256, 256), BF), ((2, 10, 8, 256), F32),
     ], args, specs)
 
 
@@ -426,8 +449,8 @@
     specs = [SMEM] + [whole(a) for a in args[1:6]] + [block((1,) + kv.shape[1:], rp)] + [whole(a) for a in args[7:]]
     return call(kernel, "cross", 9, [((3, 2, 4, 80, 256), BF)], [block((3, 2, 4, 80, 256))], [
         ((2, 8, 32, 384), BF), ((2, 3, 2, 8, 32, 128), BF), ((2, 3, 2, 8, 32, 128), BF),
-        ((3, 48, 128), F32), ((3, 48, 128), F32), ((4, 48, 256), F32), ((4, 48, 256), BF),
-        ((2 * SLOTS, 256, 256), BF), ((4, 80, 256), F32), ((2, 4, 8, 256), F32), ((2, 2, 3, 2, 8, 128), F32),
+        ((3, 64, 256), F32), ((LAG + 1, 2, 64, 256), F32), ((LAG + 1, 2, 64, 256), BF), ((SLOTS, 2, 256, 128), BF),
+        ((4, 80, 256), F32), ((2, 4, 8, 256), F32), ((2, 3, 2, 8, 256), F32),
     ], args, specs)[0]
 
 

time: 85.3 us -> 76.4 us (0.90)
  Pallas kernels: 51.8 us -> 41.3 us
  waiting for transfers between devices: 0.82 us -> 2.21 us
    pallas_call x6, Pallas kernels: 48.5 us -> 38 us  [call(): pl.pallas_call(kernel, grid=(1,), out_shape=[jax.ShapeDtypeStruct(s, t) f...]
    ppermute x5, waiting for transfers between devices: 0.8 us -> 2.19 us  [exchange(): lax.ppermute(lax.dynamic_index_in_dim(x, mine ^ turn, dim, keepdims=False...]
  transfers between devices with their start and end apart: 13 -> 13, of which waited for: 1 -> 3; matrix products, arithmetic and copies ran while one was open for 0% -> 0% of each run, Pallas kernels for 57% -> 50%
where the time goes in v2:
time: 76.4 us; the launch traced here: 75.8 us
  Pallas kernels  41.3 us (54%)
  starting transfers between devices  24.8 us (32%)
  local copies, waits for them, and re-layouts  5.14 us (7%)
  waiting for transfers between devices  2.21 us (3%)
  other arithmetic  1.42 us (2%)
  between operations  0.95 us (1%)
    pallas_call x6, Pallas kernels, call(): pl.pallas_call(kernel, grid=(1,), out_shape=[jax.ShapeDtypeStruct(s, t) f...  38 us
    ppermute x5, starting transfers between devices, exchange(): lax.ppermute(lax.dynamic_index_in_dim(x, mine ^ turn, dim, keepdims=False...  9.95 us
    ppermute x1, starting transfers between devices, shards(): stat0_near = lax.ppermute(stat0, 'row', near)  6.5 us
    unnamed x30, local copies, waits for them, and re-layouts  5.01 us
    ppermute x1, starting transfers between devices, shards(): stat1_near = lax.ppermute(stat1, 'row', near)  4.38 us
    pallas_call x1, Pallas kernels, pack_call(): pl.pallas_call(pack_kernel, out_shape=[jax.ShapeDtypeStruct(s + rows, BF)...  3.25 us
    ppermute x5, waiting for transfers between devices, exchange(): lax.ppermute(lax.dynamic_index_in_dim(x, mine ^ turn, dim, keepdims=False...  2.19 us
  transfers between devices with their start and end apart: 13, of which 3 were waited for; matrix products, arithmetic and copies ran while one was open for 0% of the time, Pallas kernels for 50%

profile of v2, /device:TPU:0, one launch (start us, length us, event | category | flops | bytes accessed | tf_op | source)
XLA Modules:
  0.0 75.8 jit_solution(18169645815250141514)
XLA Ops:
  0.6 0.6 pad_add_fusion.edge_ref.refs_0_
  1.3 3.3 %pack.1 = (bf16[3,128,384]{2,1,0:T(8,128)(2,1)}, bf16[3,128,384]{2,1,0:T(8,128)(2,1)}, bf16[3,2,128,384]{3,2,1,0:T(8,128)(2,1)}, bf16[2,3,2,128,384]{4,3,2,1,0:T(8,128)(2,1)}) custom-call(s32[3]{0:T(128)} %pad_add_fusion.edge_ref.refs_0_, bf16[4,2,128,384]{3,2,1,0:T(8,128)(2,1)} %bitcast.23, bf16[4,2,128,384]{3,2,1,0:T(8,128)(2,1)} %bitcast.25), custom_call_target="tpu_custom_call" | custom-call | tf_op jit(solution)/shard_map/pack/pallas_call | solution.py:411
  4.5 0.5 collective-permute-start
  5.0 0.7 collective-permute-start.1
  5.7 0.0 copy-start
  5.8 1.1 %copy-done = bf16[8,128,384]{2,1,0:T(8,128)(2,1)S(1)} copy-done((bf16[8,128,384]{2,1,0:T(8,128)(2,1)S(1)}, bf16[8,128,384]{2,1,0:T(8,128)(2,1)}, u32[]{:S(2)}) %copy-start) | copy-done | bytes 786456
  6.9 1.1 %copy-done.1 = bf16[8,128,384]{2,1,0:T(8,128)(2,1)S(1)} copy-done((bf16[8,128,384]{2,1,0:T(8,128)(2,1)S(1)}, bf16[8,128,384]{2,1,0:T(8,128)(2,1)}, u32[]{:S(2)}) %copy-start.1) | copy-done | bytes 786456
  8.0 1.2 %copy-done.3 = bf16[384,1152]{1,0:T(8,128)(2,1)S(1)} copy-done((bf16[384,1152]{1,0:T(8,128)(2,1)S(1)}, bf16[384,1152]{1,0:T(8,128)(2,1)}, u32[]{:S(2)}) %copy-start.3) | copy-done | bytes 884760
  9.2 0.8 %copy-done.6 = bf16[160,128]{1,0:T(8,128)(2,1)S(1)} copy-done((bf16[160,128]{1,0:T(8,128)(2,1)S(1)}, bf16[160,128]{1,0:T(8,128)(2,1)}, u32[]{:S(2)}) %copy-start.6) | copy-done | bytes 40984
  10.0 0.8 copy-done.9
  10.7 3.1 %own.1 = (bf16[2,3,2,8,32,128]{5,4,3,2,1,0:T(8,128)(2,1)S(1)}, bf16[2,3,2,8,32,128]{5,4,3,2,1,0:T(8,128)(2,1)S(1)}, bf16[2,2,8,32,384]{4,3,2,1,0:T(8,128)(2,1)S(...) custom-call(bf16[4,2,128,384]{3,2,1,0:T(8,128)(2,1)S(1)} %bitcast.24, ...), custom_call_target="tpu_custom_call" | custom-call | flops 4000000000 | bytes 1048576 | tf_op jit(solution)/shard_map/own/pallas_call | solution.py:395
  13.8 0.0 collective-permute-done.1.refs_2_
  13.9 0.0 copy-done.14
  13.9 0.7 collective-permute-start.2
  14.6 0.0 collective-permute-done.refs_1_
  14.6 0.0 copy-start.13
  14.6 9.5 %attend.2 = (bf16[3,2,8,32,128]{4,3,2,1,0:T(8,128)(2,1)S(1)}, f32[3,2,4,80,256]{4,3,2,1,0:T(8,128)S(1)}, f32[2,3,2,8,128]{4,3,2,1,0:T(8,128)S(1)}, f32[384,1152]{1,0:T(8,128)S(1)}) custom-call(s32[3]{0:T(128)S(1)} %copy-done.2, bf16[2,3,2,128,384]{4,3,2,1,0:T(8,128)(2,1)S(1)} %collective-permute-done.refs_1_, ...), custom_call_target="tpu_custom_call" | custom-call | flops 12000000000 | bytes 1048576 | tf_op jit(solution)/shard_map/attend/pallas_call | solution.py:395
  24.1 6.5 %collective-permute-start.4 = (f32[2,3,2,8,128]{4,3,2,1,0:T(8,128)S(1)}, f32[2,3,2,8,128]{4,3,2,1,0:T(8,128)S(1)}, u32[]{:S(2)}, u32[]{:S(2)}) collective-permute-start(f32[2,3,2,8,128]{4,3,2,1,0:T(8,128)S(1)} %get-tuple-element.47), channel_id=1, source_target_pairs={{0,1},{1,0},{2,3},{3,2},{4,5},{5,4},{6,7},{7,6},{8,9},{9,8},{10,11... | collective-permute-start | bytes 147464 | tf_op jit(solution)/shard_map/ppermute | solution.py:480
  30.6 0.7 collective-permute-start.5
  31.3 0.0 collective-permute-done.2.refs_2_
  31.3 0.0 copy-start.10
  31.3 0.8 %collective-permute-start.3 = (bf16[3,2,128,384]{3,2,1,0:T(8,128)(2,1)S(1)}, bf16[3,2,128,384]{3,2,1,0:T(8,128)(2,1)S(1)}, u32[]{:S(2)}, u32[]{:S(2)}) collective-permute-start(bf16[3,2,128,384]{3,2,1,0:T(8,128)(2,1)S(1)} %copy-done.13), channel_id=1, source_target_pairs={{1,2},{3,4},{5,6},{7,8},{9,10},{11,12},{13,14},{2,1},{4,3},{6,5},{... | collective-permute-start | bytes 1769480 | tf_op jit(solution)/shard_map/ppermute | solution.py:479
  32.1 10.4 %attend.3 = (bf16[3,2,8,32,128]{4,3,2,1,0:T(8,128)(2,1)S(1)}, f32[3,2,4,80,256]{4,3,2,1,0:T(8,128)S(1)}, f32[2,3,2,8,128]{4,3,2,1,0:T(8,128)S(1)}, f32[384,1152]{1,0:T(8,128)S(1)}) custom-call(s32[3]{0:T(128)S(1)} %copy-done.2, bf16[2,3,2,128,384]{4,3,2,1,0:T(8,128)(2,1)S(1)} %collective-permute-done.refs_1_, ...), custom_call_target="tpu_custom_call" | custom-call | flops 12000000000 | bytes 1048576 | tf_op jit(solution)/shard_map/attend/pallas_call | solution.py:395
  42.6 4.4 %collective-permute-start.6 = (f32[2,3,2,8,128]{4,3,2,1,0:T(8,128)S(1)}, f32[2,3,2,8,128]{4,3,2,1,0:T(8,128)S(1)}, u32[]{:S(2)}, u32[]{:S(2)}) collective-permute-start(f32[2,3,2,8,128]{4,3,2,1,0:T(8,128)S(1)} %get-tuple-element.52), channel_id=1, source_target_pairs={{0,1},{1,0},{2,3},{3,2},{4,5},{5,4},{6,7},{7,6},{8,9},{9,8},{10,11... | collective-permute-start | bytes 147464 | tf_op jit(solution)/shard_map/ppermute | solution.py:484
  47.0 0.7 collective-permute-start.7
  47.6 0.1 fusion
  47.7 0.0 collective-permute-done.4.refs_4_
  47.7 4.0 %collective-permute-start.8 = (bf16[8,24,1152]{2,1,0:T(8,128)(2,1)S(1)}, bf16[8,24,1152]{2,1,0:T(8,128)(2,1)S(1)}, u32[]{:S(2)}, u32[]{:S(2)}) collective-permute-start(bf16[8,24,1152]{2,1,0:T(8,128)(2,1)S(1)} %fusion), channel_id=1, source_target_pairs={{0,1},{1,0},{2,3},{3,2},{4,5},{5,4},{6,7},{7,6},{8,9},{9,8},{10,11... | collective-permute-start | bytes 1327112 | tf_op jit(solution)/shard_map/ppermute | solution.py:374
  51.7 0.0 collective-permute-done.5.refs_5_
  51.7 0.0 collective-permute-done.3.refs_3_
  51.7 0.0 copy-done.12
  51.7 5.7 %cross.2.dkv0_ref = bf16[3,2,4,80,256]{4,3,2,1,0:T(8,128)(2,1)S(1)} custom-call(s32[3]{0:T(128)S(1)} %copy-done.2, bf16[2,3,2,128,384]{4,3,2,1,0:T(8,128)(2,1)S(1)} %collective-permute-done.refs_1_, bf16[3,128,384]{2,1,0:T(8,128)(2,1)S(1)} %collective-permute-done.1.refs_2_, bf16[3,2,128,384]{3,2,1,0:T(8,128)(2,1)S(1)} %collective-permute-done.3.refs_3_, ...), custom_call_target="tpu_custom_call" | custom-call | flops 8999999488 | bytes 1048576 | tf_op jit(solution)/shard_map/cross/pallas_call | solution.py:395
  57.4 0.0 collective-permute-done.8
  57.4 0.1 bitcast_add_fusion
  57.6 1.4 %collective-permute-start.9 = (bf16[4,24,1152]{2,1,0:T(8,128)(2,1)S(1)}, bf16[4,24,1152]{2,1,0:T(8,128)(2,1)S(1)}, u32[]{:S(2)}, u32[]{:S(2)}) collective-permute-start(bf16[4,24,1152]{2,1,0:T(8,128)(2,1)S(1)} %fusion.1), channel_id=1, source_target_pairs={{0,2},{1,3},{2,0},{3,1},{4,6},{5,7},{6,4},{7,5},{8,10},{9,11},{10,... | collective-permute-start | bytes 663560 | tf_op jit(solution)/shard_map/ppermute | solution.py:374
  59.0 0.0 collective-permute-done.6.refs_4_
  59.0 0.0 collective-permute-done.7.refs_5_
  59.0 0.0 copy-start.8
  59.0 5.6 %cross.3.dkv1_ref = bf16[3,2,4,80,256]{4,3,2,1,0:T(8,128)(2,1)S(1)} custom-call(s32[3]{0:T(128)S(1)} %copy-done.2, bf16[2,3,2,128,384]{4,3,2,1,0:T(8,128)(2,1)S(1)} %collective-permute-done.refs_1_, bf16[3,128,384]{2,1,0:T(8,128)(2,1)S(1)} %collective-permute-done.2.refs_2_, bf16[3,2,128,384]{3,2,1,0:T(8,128)(2,1)S(1)} %collective-permute-done.3.refs_3_, ...), custom_call_target="tpu_custom_call" | custom-call | flops 8999999488 | bytes 1048576 | tf_op jit(solution)/shard_map/cross/pallas_call | solution.py:395
  64.6 0.4 collective-permute-done.9
  65.1 2.1 %collective-permute-start.10 = (bf16[1,24,1152]{2,1,0:T(8,128)(2,1)S(1)}, bf16[1,24,1152]{2,1,0:T(8,128)(2,1)S(1)}, u32[]{:S(2)}, u32[]{:S(2)}) collective-permute-start(bf16[1,24,1152]{2,1,0:T(8,128)(2,1)S(1)} %get-tuple-element.64), channel_id=1, source_target_pairs={{0,4},{1,5},{2,6},{3,7},{4,0},{5,1},{6,2},{7,3},{8,12},{9,13},{10,... | collective-permute-start | bytes 165896 | tf_op jit(solution)/shard_map/ppermute | solution.py:374
  67.2 2.0 %collective-permute-start.11 = (bf16[1,24,1152]{2,1,0:T(8,128)(2,1)S(1)}, bf16[1,24,1152]{2,1,0:T(8,128)(2,1)S(1)}, u32[]{:S(2)}, u32[]{:S(2)}) collective-permute-start(bf16[1,24,1152]{2,1,0:T(8,128)(2,1)S(1)} %get-tuple-element.63), channel_id=1, source_target_pairs={{0,8},{1,9},{2,10},{3,11},{4,12},{5,13},{6,14},{7,15},{8,0},{9,1},... | collective-permute-start | bytes 165896 | tf_op jit(solution)/shard_map/ppermute | solution.py:374
  69.2 0.5 collective-permute-start.12
  69.7 3.8 %final.1 = bf16[8,128,384]{2,1,0:T(8,128)(2,1)} custom-call(bf16[3,2,8,32,128]{4,3,2,1,0:T(8,128)(2,1)S(1)} %get-tuple-element.39.dq0_ref, bf16[3,2,8,32,128]{4,3,2,1,0:T(8,128)(2,1)S(1)} %get-tuple-element.44.dq1_ref, bf16[3,2,4,80,256]{4,3,2,1,0:T(8,128)(2,1)S(1)} %cross.2.dkv0_ref, bf16[3,2,4,80,256]{4,3,2,1,0:T(8,128)(2,1)S(1)} %cross.3.dkv1_ref, ...), custom_call_target="tpu_custom_call" | custom-call | flops 4000000000 | bytes 1048576 | tf_op jit(solution)/shard_map/final/pallas_call | solution.py:395
  73.4 0.0 collective-permute-done.10
  73.4 0.3 collective-permute-done.11
  73.8 1.4 %collective-permute-done.12 = bf16[1,24,1152]{2,1,0:T(8,128)(2,1)S(1)} collective-permute-done((bf16[1,24,1152]{2,1,0:T(8,128)(2,1)S(1)}, bf16[1,24,1152]{2,1,0:T(8,128)(2,1)S(1)}, u32[]{:S(2)}, u32[]{:S(2)}) %collective-permute-start.12) | collective-permute-done | bytes 55328 | tf_op jit(solution)/shard_map/ppermute | solution.py:374
  75.2 0.7 multiply_bitcast_fusion
  (22 shorter events, 0.2 us)
Async XLA Ops:
  4.5 10.0 %collective-permute-start = (bf16[2,3,2,128,384]{4,3,2,1,0:T(8,128)(2,1)}, bf16[2,3,2,128,384]{4,3,2,1,0:T(8,128)(2,1)S(1)}, u32[]{:S(2)}, u32[]{:S(2)}) collective-permute-start(bf16[2,3,2,128,384]{4,3,2,1,0:T(8,128)(2,1)} %get-tuple-element.32), channel_id=1, source_target_pairs={{0,1},{1,0},{2,3},{3,2},{4,5},{5,4},{6,7},{7,6},{8,9},{9,8},{10,11... | collective-permute-start | bytes 3538952 | tf_op jit(solution)/shard_map/ppermute | solution.py:474
  5.0 8.8 %collective-permute-start.1 = (bf16[3,128,384]{2,1,0:T(8,128)(2,1)}, bf16[3,128,384]{2,1,0:T(8,128)(2,1)S(1)}, u32[]{:S(2)}, u32[]{:S(2)}) collective-permute-start(bf16[3,128,384]{2,1,0:T(8,128)(2,1)} %get-tuple-element.33), channel_id=1, source_target_pairs={{1,2},{3,4},{5,6},{7,8},{9,10},{11,12},{13,14},{2,1},{4,3},{6,5},{... | collective-permute-start | bytes 884744 | tf_op jit(solution)/shard_map/ppermute | solution.py:473
  5.7 1.1 %copy-start = (bf16[8,128,384]{2,1,0:T(8,128)(2,1)S(1)}, bf16[8,128,384]{2,1,0:T(8,128)(2,1)}, u32[]{:S(2)}) copy-start(bf16[8,128,384]{2,1,0:T(8,128)(2,1)} %param.5) | copy-start | bytes 2359300
  6.9 1.1 %copy-start.1 = (bf16[8,128,384]{2,1,0:T(8,128)(2,1)S(1)}, bf16[8,128,384]{2,1,0:T(8,128)(2,1)}, u32[]{:S(2)}) copy-start(bf16[8,128,384]{2,1,0:T(8,128)(2,1)} %param.7) | copy-start | bytes 2359300
  8.0 1.2 %copy-start.3 = (bf16[384,1152]{1,0:T(8,128)(2,1)S(1)}, bf16[384,1152]{1,0:T(8,128)(2,1)}, u32[]{:S(2)}) copy-start(bf16[384,1152]{1,0:T(8,128)(2,1)} %w_ref.3) | copy-start | bytes 2654212
  9.2 0.8 %copy-start.6 = (bf16[160,128]{1,0:T(8,128)(2,1)S(1)}, bf16[160,128]{1,0:T(8,128)(2,1)}, u32[]{:S(2)}) copy-start(bf16[160,128]{1,0:T(8,128)(2,1)} %constant.47.clone.place_ref.refs_9_) | copy-start | bytes 122884
  10.0 0.8 copy-start.9
  10.7 3.1 %copy-start.14 = (bf16[3,128,384]{2,1,0:T(8,128)(2,1)S(1)}, bf16[3,128,384]{2,1,0:T(8,128)(2,1)}, u32[]{:S(2)}) copy-start(bf16[3,128,384]{2,1,0:T(8,128)(2,1)} %get-tuple-element.41) | copy-start | bytes 884740
  10.7 3.8 %copy-start.2 = (s32[3]{0:T(128)S(1)}, s32[3]{0:T(128)}, u32[]{:S(2)}) copy-start(s32[3]{0:T(128)} %pad_add_fusion.edge_ref.refs_0_) | copy-start | bytes 40
  10.7 3.9 %copy-start.4 = (bf16[384,1152]{1,0:T(8,128)(2,1)S(1)}, bf16[384,1152]{1,0:T(8,128)(2,1)}, u32[]{:S(2)}) copy-start(bf16[384,1152]{1,0:T(8,128)(2,1)} %w_ref.3) | copy-start | bytes 2654212
  10.7 3.9 %copy-start.7 = (bf16[160,128]{1,0:T(8,128)(2,1)S(1)}, bf16[160,128]{1,0:T(8,128)(2,1)}, u32[]{:S(2)}) copy-start(bf16[160,128]{1,0:T(8,128)(2,1)} %constant.47.clone.place_ref.refs_9_) | copy-start | bytes 122884
  13.8 10.3 %copy-start.11 = (bf16[2,3,2,8,4,16,256]{6,5,4,3,2,1,0:T(8,128)(2,1)}, bf16[2,3,2,8,4,16,256]{6,5,4,3,2,1,0:T(8,128)(2,1)S(1)}, u32[]{:S(2)}) copy-start(bf16[2,3,2,8,4,16,256]{6,5,4,3,2,1,0:T(8,128)(2,1)S(1)} %get-tuple-element.37.refs_6_) | copy-start | bytes 9437188
  13.9 17.4 %collective-permute-start.2 = (bf16[3,128,384]{2,1,0:T(8,128)(2,1)S(1)}, bf16[3,128,384]{2,1,0:T(8,128)(2,1)S(1)}, u32[]{:S(2)}, u32[]{:S(2)}) collective-permute-start(bf16[3,128,384]{2,1,0:T(8,128)(2,1)S(1)} %copy-done.14), channel_id=1, source_target_pairs={{1,2},{3,4},{5,6},{7,8},{9,10},{11,12},{13,14},{2,1},{4,3},{6,5},{... | collective-permute-start | bytes 884744 | tf_op jit(solution)/shard_map/ppermute | solution.py:476
  14.6 16.7 %copy-start.13 = (bf16[3,2,128,384]{3,2,1,0:T(8,128)(2,1)S(1)}, bf16[3,2,128,384]{3,2,1,0:T(8,128)(2,1)}, u32[]{:S(2)}) copy-start(bf16[3,2,128,384]{3,2,1,0:T(8,128)(2,1)} %get-tuple-element.46) | copy-start | bytes 1769476
  24.1 23.6 %collective-permute-start.4 = (f32[2,3,2,8,128]{4,3,2,1,0:T(8,128)S(1)}, f32[2,3,2,8,128]{4,3,2,1,0:T(8,128)S(1)}, u32[]{:S(2)}, u32[]{:S(2)}) collective-permute-start(f32[2,3,2,8,128]{4,3,2,1,0:T(8,128)S(1)} %get-tuple-element.47), channel_id=1, source_target_pairs={{0,1},{1,0},{2,3},{3,2},{4,5},{5,4},{6,7},{7,6},{8,9},{9,8},{10,11... | collective-permute-start | bytes 147464 | tf_op jit(solution)/shard_map/ppermute | solution.py:480
  30.6 21.1 %collective-permute-start.5 = (f32[2,3,2,8,128]{4,3,2,1,0:T(8,128)S(1)}, f32[2,3,2,8,128]{4,3,2,1,0:T(8,128)S(1)}, u32[]{:S(2)}, u32[]{:S(2)}) collective-permute-start(f32[2,3,2,8,128]{4,3,2,1,0:T(8,128)S(1)} %get-tuple-element.47), channel_id=1, source_target_pairs={{1,2},{3,4},{5,6},{7,8},{9,10},{11,12},{13,14},{2,1},{4,3},{6,5},{... | collective-permute-start | bytes 147464 | tf_op jit(solution)/shard_map/ppermute | solution.py:481
  31.3 20.4 %copy-start.10 = (bf16[128,128]{1,0:T(8,128)(2,1)S(1)}, bf16[128,128]{1,0:T(8,128)(2,1)}, u32[]{:S(2)}) copy-start(bf16[128,128]{1,0:T(8,128)(2,1)} %constant.48.clone.split_ref.refs_9_) | copy-start | bytes 98308
  31.3 20.4 %copy-start.12 = (bf16[2,3,2,8,4,16,256]{6,5,4,3,2,1,0:T(8,128)(2,1)S(1)}, bf16[2,3,2,8,4,16,256]{6,5,4,3,2,1,0:T(8,128)(2,1)}, u32[]{:S(2)}) copy-start(bf16[2,3,2,8,4,16,256]{6,5,4,3,2,1,0:T(8,128)(2,1)} %copy-done.11) | copy-start | bytes 9437188
  31.3 20.4 %collective-permute-start.3 = (bf16[3,2,128,384]{3,2,1,0:T(8,128)(2,1)S(1)}, bf16[3,2,128,384]{3,2,1,0:T(8,128)(2,1)S(1)}, u32[]{:S(2)}, u32[]{:S(2)}) collective-permute-start(bf16[3,2,128,384]{3,2,1,0:T(8,128)(2,1)S(1)} %copy-done.13), channel_id=1, source_target_pairs={{1,2},{3,4},{5,6},{7,8},{9,10},{11,12},{13,14},{2,1},{4,3},{6,5},{... | collective-permute-start | bytes 1769480 | tf_op jit(solution)/shard_map/ppermute | solution.py:479
  42.6 16.4 %collective-permute-start.6 = (f32[2,3,2,8,128]{4,3,2,1,0:T(8,128)S(1)}, f32[2,3,2,8,128]{4,3,2,1,0:T(8,128)S(1)}, u32[]{:S(2)}, u32[]{:S(2)}) collective-permute-start(f32[2,3,2,8,128]{4,3,2,1,0:T(8,128)S(1)} %get-tuple-element.52), channel_id=1, source_target_pairs={{0,1},{1,0},{2,3},{3,2},{4,5},{5,4},{6,7},{7,6},{8,9},{9,8},{10,11... | collective-permute-start | bytes 147464 | tf_op jit(solution)/shard_map/ppermute | solution.py:484
  47.0 12.0 %collective-permute-start.7 = (f32[2,3,2,8,128]{4,3,2,1,0:T(8,128)S(1)}, f32[2,3,2,8,128]{4,3,2,1,0:T(8,128)S(1)}, u32[]{:S(2)}, u32[]{:S(2)}) collective-permute-start(f32[2,3,2,8,128]{4,3,2,1,0:T(8,128)S(1)} %get-tuple-element.52), channel_id=1, source_target_pairs={{1,2},{3,4},{5,6},{7,8},{9,10},{11,12},{13,14},{2,1},{4,3},{6,5},{... | collective-permute-start | bytes 147464 | tf_op jit(solution)/shard_map/ppermute | solution.py:485
  47.7 9.7 %collective-permute-start.8 = (bf16[8,24,1152]{2,1,0:T(8,128)(2,1)S(1)}, bf16[8,24,1152]{2,1,0:T(8,128)(2,1)S(1)}, u32[]{:S(2)}, u32[]{:S(2)}) collective-permute-start(bf16[8,24,1152]{2,1,0:T(8,128)(2,1)S(1)} %fusion), channel_id=1, source_target_pairs={{0,1},{1,0},{2,3},{3,2},{4,5},{5,4},{6,7},{7,6},{8,9},{9,8},{10,11... | collective-permute-start | bytes 1327112 | tf_op jit(solution)/shard_map/ppermute | solution.py:374
  57.6 7.4 %collective-permute-start.9 = (bf16[4,24,1152]{2,1,0:T(8,128)(2,1)S(1)}, bf16[4,24,1152]{2,1,0:T(8,128)(2,1)S(1)}, u32[]{:S(2)}, u32[]{:S(2)}) collective-permute-start(bf16[4,24,1152]{2,1,0:T(8,128)(2,1)S(1)} %fusion.1), channel_id=1, source_target_pairs={{0,2},{1,3},{2,0},{3,1},{4,6},{5,7},{6,4},{7,5},{8,10},{9,11},{10,... | collective-permute-start | bytes 663560 | tf_op jit(solution)/shard_map/ppermute | solution.py:374
  59.0 10.7 %copy-start.5 = (bf16[128,160]{1,0:T(8,128)(2,1)S(1)}, bf16[128,160]{1,0:T(8,128)(2,1)}, u32[]{:S(2)}) copy-start(bf16[128,160]{1,0:T(8,128)(2,1)} %constant.51.unplace_ref) | copy-start | bytes 122884
  59.0 10.7 %copy-start.8 = (bf16[128,128]{1,0:T(8,128)(2,1)S(1)}, bf16[128,128]{1,0:T(8,128)(2,1)}, u32[]{:S(2)}) copy-start(bf16[128,128]{1,0:T(8,128)(2,1)} %constant.52.unsplit_ref) | copy-start | bytes 98308
  65.1 8.3 %collective-permute-start.10 = (bf16[1,24,1152]{2,1,0:T(8,128)(2,1)S(1)}, bf16[1,24,1152]{2,1,0:T(8,128)(2,1)S(1)}, u32[]{:S(2)}, u32[]{:S(2)}) collective-permute-start(bf16[1,24,1152]{2,1,0:T(8,128)(2,1)S(1)} %get-tuple-element.64), channel_id=1, source_target_pairs={{0,4},{1,5},{2,6},{3,7},{4,0},{5,1},{6,2},{7,3},{8,12},{9,13},{10,... | collective-permute-start | bytes 165896 | tf_op jit(solution)/shard_map/ppermute | solution.py:374
  67.2 6.6 %collective-permute-start.11 = (bf16[1,24,1152]{2,1,0:T(8,128)(2,1)S(1)}, bf16[1,24,1152]{2,1,0:T(8,128)(2,1)S(1)}, u32[]{:S(2)}, u32[]{:S(2)}) collective-permute-start(bf16[1,24,1152]{2,1,0:T(8,128)(2,1)S(1)} %get-tuple-element.63), channel_id=1, source_target_pairs={{0,8},{1,9},{2,10},{3,11},{4,12},{5,13},{6,14},{7,15},{8,0},{9,1},... | collective-permute-start | bytes 165896 | tf_op jit(solution)/shard_map/ppermute | solution.py:374
  69.2 6.0 %collective-permute-start.12 = (bf16[1,24,1152]{2,1,0:T(8,128)(2,1)S(1)}, bf16[1,24,1152]{2,1,0:T(8,128)(2,1)S(1)}, u32[]{:S(2)}, u32[]{:S(2)}) collective-permute-start(bf16[1,24,1152]{2,1,0:T(8,128)(2,1)S(1)} %get-tuple-element.62), channel_id=1, source_target_pairs={{0,12},{1,13},{2,14},{3,15},{4,8},{5,9},{6,10},{7,11},{8,4},{9,5},... | collective-permute-start | bytes 165896 | tf_op jit(solution)/shard_map/ppermute | solution.py:374

commit v3 on v2

--- a/solution.py
+++ b/solution.py
@@ -11,10 +11,10 @@
 DILATION = 2
 HALO = 6
 GROUPS = 3
-UNITS = 16
+UNITS = 48
 LAG = 3
 SLOTS = 2 * LAG + 1
-CROSS_UNITS = 16
+CROSS_UNITS = 48
 BF = jnp.bfloat16
 F32 = jnp.float32
 SCALE = 32 ** -0.5
@@ -63,30 +63,46 @@
             store(cp, p, jnp.concatenate(halves, axis=0).astype(BF))
 
 
-def pack_kernel(edge_ref, x_ref, g_ref, x0_ref, x1_ref, fg_ref, near_ref, xs, gs, sem):
-    odd = edge_ref[2]
+def first_kernel(x_ref, x0_ref, xs, sem):
+    odd = lax.axis_index("row") & 1
+    load = pltpu.make_async_copy(x_ref.at[pl.ds(odd, 3), 0], xs, sem.at[0])
+    load.start()
+    load.wait()
+    store = pltpu.make_async_copy(xs, x0_ref, sem.at[1])
+    store.start()
+    store.wait()
+
+
+def pack_kernel(first_ref, x_ref, g_ref, x1_ref, fg_ref, near_ref, xs, gs, sem):
+    odd = lax.axis_index("row") & 1
     mine, other = pl.ds(odd, 3), pl.ds(1 - odd, 3)
     loads = [pltpu.make_async_copy(x_ref, xs, sem.at[0]), pltpu.make_async_copy(g_ref, gs, sem.at[1])]
     for copy in loads:
         copy.start()
     loads[0].wait()
     copies = [
-        pltpu.make_async_copy(xs.at[mine, 0], x0_ref, sem.at[2]),
-        pltpu.make_async_copy(xs.at[other], near_ref.at[0], sem.at[3]),
-        pltpu.make_async_copy(xs.at[mine, 1], x1_ref, sem.at[4]),
-        pltpu.make_async_copy(gs.at[other], near_ref.at[1], sem.at[5]),
-        pltpu.make_async_copy(gs.at[mine], fg_ref, sem.at[6]),
+        pltpu.make_async_copy(xs.at[other], near_ref.at[0], sem.at[2]),
+        pltpu.make_async_copy(xs.at[mine, 1], x1_ref, sem.at[3]),
+        pltpu.make_async_copy(gs.at[other], near_ref.at[1], sem.at[4]),
+        pltpu.make_async_copy(gs.at[mine], fg_ref, sem.at[5]),
     ]
-    for copy in copies[:3]:
+    for copy in copies[:2]:
         copy.start()
     loads[1].wait()
-    for copy in copies[3:]:
+    for copy in copies[2:]:
         copy.start()
     for copy in copies:
         copy.wait()
 
 
-def own_kernel(x_ref, do_ref, w_ref, place_ref, split_ref, q_ref, g_ref, xq_ref, kv_ref, xk_ref, wkv):
+def own_kernel(*refs):
+    sources, (q_ref, g_ref, xq_ref, kv_ref, xk_ref, wkv), held, sem = refs[:5], refs[5:11], refs[11:16], refs[16]
+    loads = [pltpu.make_async_copy(source, room, sem.at[n]) for n, (source, room) in enumerate(zip(sources, held))]
+    for copy in loads:
+        copy.start()
+    for copy in loads:
+        copy.wait()
+    x_ref, do_ref, w_ref, place_ref, split_ref = held
     gather_kv_weight(w_ref, wkv)
     for rp in range(2):
         for k in range(4):
@@ -141,40 +157,40 @@
     return 0 if p == 0 else (2 if p == 7 else 1)
 
 
-def attend_kernel(rp, edge_ref, near_ref, far_ref, q, do, xq, kv, xk, w_ref, place_ref, *refs):
+def attend_kernel(rp, near_ref, far_ref, q, do, xq, kv, xk, w_ref, place_ref, *refs):
     if rp == 0:
-        dw_in = None
-    else:
-        dw_in, *refs = refs
+        send_ref, gs_ref, *refs = refs
+        gs_ref[:768] = send_ref[...].reshape(768, 384)
     dq_ref, own_ref, stat_ref, dw_ref, xh, kvh, acc, bias, wkv, sc, pd, rhs, tail = refs
-    odd = edge_ref[2]
+    index = lax.axis_index("row")
+    odd = index & 1
+    low = jnp.where(index == 0, 3, 0)
+    high = jnp.where(index == lax.axis_size("row") - 1, 7, 10)
     gather_kv_weight(w_ref, wkv)
-    window_bias(bias, 10, lambda krow, qrow: (krow >= qrow) & (krow <= qrow + 6) & (krow >= edge_ref[0]) & (krow < edge_ref[1]))
-
-    def project_pair(k, carry):
+    window_bias(bias, 10, lambda krow, qrow: (krow >= qrow) & (krow <= qrow + 6) & (krow >= low) & (krow < high))
+
+    for k in range(3):
         project_keys(near_ref[0, k, rp], place_ref, wkv, xh, kvh, k + 3 - 3 * odd)
+    for k in range(3):
         project_keys(far_ref[k], place_ref, wkv, xh, kvh, k + 3 * odd)
-        return carry
-
-    lax.fori_loop(0, 3, project_pair, 0)
     pick, pick_b = head_masks()
     clear_off_diagonal(rhs)
 
     def attend(step, carry):
         def place_of(u):
             index = step * (UNITS // 8) + u // 8
-            return index // 2, (index % 2 if UNITS == 8 else u // 8), u % 8
+            return index // 2, (u // 8) % 2, u % 8
 
         def keys(u):
             g, cp, p = place_of(u)
             return jnp.concatenate([
                 kvh[g, cp, p, :3].reshape(48, 256),
-                kv[0, g, cp, p].reshape(64, 256),
+                kv[rp, g, cp, p].reshape(64, 256),
                 kvh[g, cp, p, 3:].reshape(48, 256)], axis=0)
 
         def score(u):
             g, cp, p = place_of(u)
-            pack_heads(rhs, u % SLOTS, q[0, g, cp, p], do[0, g, cp, p], pick_b)
+            pack_heads(rhs, u % SLOTS, q[rp, g, cp, p], do[rp, g, cp, p], pick_b)
             sc[u % (LAG + 1)] = dot(keys(u), rhs[u % SLOTS], 1, 1)
 
         def soften(u):
@@ -227,12 +243,21 @@
                 spread(t - 2 * LAG)
         return carry
 
-    lax.fori_loop(0, 48 // UNITS, attend, 0)
+    if UNITS == 48:
+        attend(0, 0)
+    else:
+        lax.fori_loop(0, 48 // UNITS, attend, 0)
+    if rp == 0:
+        rest = stat_ref[...].reshape(96, 128)
+        for part in range(3):
+            piece = rest.astype(BF)
+            gs_ref[768:, 128 * part:128 * part + 128] = piece
+            rest = rest - piece.astype(F32)
 
     dw = jnp.zeros((384, 768), F32)
     dwq = jnp.zeros((384, 384), F32)
     for cp in range(2):
-        for xs, ref, n in ((xh[cp], acc, 480), (xk[0, cp], own_ref, 320)):
+        for xs, ref, n in ((xh[cp], acc, 480), (xk[rp, cp], own_ref, 320)):
             parts = []
             for g in range(GROUPS):
                 a = ref[g, cp].reshape(n, 256)
@@ -240,22 +265,24 @@
                 parts.append(a[:, 128:].astype(BF))
             dw = dw + dot(xs.reshape(n, 384), jnp.concatenate(parts, axis=1), 0, 0)
         dqs = jnp.concatenate([dq_ref[g, cp].reshape(256, 128) for g in range(GROUPS)], axis=1)
-        dwq = dwq + dot(xq[0, cp].reshape(256, 384), dqs, 0, 0)
-
-    def put(at, value):
-        dw_ref[:, at:at + value.shape[1]] = value if dw_in is None else value + dw_in[:, at:at + value.shape[1]]
-
-    put(0, dwq)
+        dwq = dwq + dot(xq[rp, cp].reshape(256, 384), dqs, 0, 0)
+
+    dw_ref[:, :384] = dwq
     for g in range(GROUPS):
-        put(384 + 128 * g, dw[:, 256 * g:256 * g + 128])
-        put(768 + 128 * g, dw[:, 256 * g + 128:256 * g + 256])
-
-
-def cross_kernel(rp, edge_ref, near_ref, far_ref, far_g_ref, near_stat, far_stat, kv, own_ref, w_ref, split_ref,
+        dw_ref[:, 384 + 128 * g:512 + 128 * g] = dw[:, 256 * g:256 * g + 128]
+        dw_ref[:, 768 + 128 * g:896 + 128 * g] = dw[:, 256 * g + 128:256 * g + 256]
+
+
+def cross_kernel(rp, near_ref, far_ref, far_gs_ref, near_stat, far_stat, kv, own_ref, w_ref, split_ref,
                  dkvs, xq, q, do, bias, sc, pd, rhs, acc, tail, stats):
-    odd = edge_ref[2]
-    stats[:, :, :, :, :128] = jnp.where(odd == 1, near_stat[...], far_stat[...])
-    stats[:, :, :, :, 128:] = jnp.where(odd == 1, far_stat[...], near_stat[...])
+    odd = lax.axis_index("row") & 1
+    if far_stat is None:
+        parts = far_gs_ref[768:].astype(F32)
+        far_rows = (parts[:, :128] + parts[:, 128:256] + parts[:, 256:]).reshape(near_stat.shape)
+    else:
+        far_rows = far_stat[...]
+    stats[:, :, :, :, :128] = jnp.where(odd == 1, near_stat[...], far_rows)
+    stats[:, :, :, :, 128:] = jnp.where(odd == 1, far_rows, near_stat[...])
     key = lax.broadcasted_iota(jnp.int32, (64, 256), 0)
     lane = lax.broadcasted_iota(jnp.int32, (64, 256), 1)
     krow, kcol, qrow = key // 16, key % 16, (lane % 32) // 8
@@ -290,12 +317,12 @@
         @pl.when(odd == parity)
         def _(parity=parity):
             side_patches(1 - parity, lambda r: near_ref[0, r, rp], lambda r: near_ref[1, r, rp])
-            side_patches(parity, lambda r: far_ref[r], lambda r: far_g_ref[r, rp])
+            side_patches(parity, lambda r: far_ref[r], lambda r: far_gs_ref[256 * r + 128 * rp:256 * r + 128 * rp + 128])
 
     def attend(step, carry):
         def place_of(u):
             index = step * (CROSS_UNITS // 8) + u // 8
-            return index // 2, (index % 2 if CROSS_UNITS == 8 else u // 8), u % 8
+            return index // 2, (u // 8) % 2, u % 8
 
         def score(u):
             g, cp, p = place_of(u)
@@ -305,7 +332,7 @@
                     at = slice(128 * side + 32 * h, 128 * side + 32 * h + 32)
                     rhs[slot, 0, at] = q[side, g, cp, p] * pick_b[h]
                     rhs[slot, 1, at] = do[side, g, cp, p] * pick_b[h]
-            keys = kv[0, g, cp, p].reshape(64, 256)
+            keys = kv[rp, g, cp, p].reshape(64, 256)
             for part in range(2):
                 sc[u % (LAG + 1), part] = dot(keys[:, 128 * part:128 * part + 128], rhs[slot, part], 1, 1)
 
@@ -344,7 +371,10 @@
                 spread(t - 2 * LAG)
         return carry
 
-    lax.fori_loop(0, 48 // CROSS_UNITS, attend, 0)
+    if CROSS_UNITS == 48:
+        attend(0, 0)
+    else:
+        lax.fori_loop(0, 48 // CROSS_UNITS, attend, 0)
 
 
 def final_kernel(dq0_ref, dq1_ref, dkv0_ref, dkv1_ref, w_ref, unplace_ref, unsplit_ref, out_ref):
@@ -378,117 +408,112 @@
     return total
 
 
-def block(shape, *at):
-    at = at + (0,) * (len(shape) - len(at))
-    return pl.BlockSpec(shape, lambda i: at)
-
-
-def whole(x):
-    return block(x.shape)
-
-
-SMEM = pl.BlockSpec(memory_space=pltpu.SMEM)
+VM = pl.BlockSpec(memory_space=pltpu.VMEM)
 ANY = pl.BlockSpec(memory_space=pl.ANY)
 
 
-def call(kernel, name, us, outs, out_specs, scratch, args, in_specs, aliases={}):
+def call(kernel, name, us, outs, scratch, args):
     return pl.pallas_call(
         kernel,
-        grid=(1,),
         out_shape=[jax.ShapeDtypeStruct(s, t) for s, t in outs],
-        in_specs=in_specs,
-        out_specs=out_specs,
+        in_specs=[VM] * len(args),
+        out_specs=[VM] * len(outs),
         scratch_shapes=[pltpu.VMEM(s, t) for s, t in scratch],
         compiler_params=pltpu.CompilerParams(vmem_limit_bytes=VMEM_BYTES),
         cost_estimate=pl.CostEstimate(flops=int(us * 1e9), bytes_accessed=1 << 20, transcendentals=0),
-        input_output_aliases=aliases,
         name=name,
     )(*args)
 
 
-def pack_call(edge, x4, g4):
-    rows = x4.shape[2:]
+def raw_call(kernel, name, outs, scratch, args):
     return pl.pallas_call(
-        pack_kernel,
-        out_shape=[jax.ShapeDtypeStruct(s + rows, BF) for s in ((3,), (3,), (3, 2), (2, 3, 2))],
-        in_specs=[SMEM, ANY, ANY],
-        out_specs=[ANY] * 4,
-        scratch_shapes=[pltpu.VMEM(x4.shape, BF), pltpu.VMEM(g4.shape, BF), pltpu.SemaphoreType.DMA((7,))],
-        name="pack",
-    )(edge, x4, g4)
-
-
-def own_call(x4, g4, w, place, split):
-    outs = [((2, 3, 2, 8, 32, 128), BF), ((2, 3, 2, 8, 32, 128), BF), ((2, 2, 8, 32, 384), BF),
-            ((2, 3, 2, 8, 4, 16, 256), BF), ((2, 2, 4, 80, 384), BF)]
-    args = (x4, g4, w, place, split)
-    return call(own_kernel, "own", 4, outs, [block(s) for s, _ in outs], [((384, 768), BF)], args, [whole(a) for a in args])
-
-
-def attend_call(rp, edge, near, far, q, do, xq, kv, xk, w, place, dw):
+        kernel,
+        out_shape=[jax.ShapeDtypeStruct(s, BF) for s in outs],
+        in_specs=[ANY] * len(args),
+        out_specs=[ANY] * len(outs),
+        scratch_shapes=[pltpu.VMEM(s, BF) for s in scratch] + [pltpu.SemaphoreType.DMA((6,))],
+        name=name,
+    )(*args)
+
+
+def own_call(*args):
+    outs = [(2, 3, 2, 8, 32, 128), (2, 3, 2, 8, 32, 128), (2, 2, 8, 32, 384), (2, 3, 2, 8, 4, 16, 256), (2, 2, 4, 80, 384)]
+    return pl.pallas_call(
+        own_kernel,
+        out_shape=[jax.ShapeDtypeStruct(s, BF) for s in outs],
+        in_specs=[ANY] * len(args),
+        out_specs=[VM] * len(outs),
+        scratch_shapes=[pltpu.VMEM((384, 768), BF)] + [pltpu.VMEM(a.shape, BF) for a in args] + [pltpu.SemaphoreType.DMA((5,))],
+        compiler_params=pltpu.CompilerParams(vmem_limit_bytes=VMEM_BYTES),
+        cost_estimate=pl.CostEstimate(flops=4000000000, bytes_accessed=1 << 20, transcendentals=0),
+        name="own",
+    )(*args)
+
+
+def attend_call(rp, *args):
     def kernel(*refs):
         attend_kernel(rp, *refs)
 
     outs = [((3, 2, 8, 32, 128), BF), ((3, 2, 4, 80, 256), F32), ((2, 3, 2, 8, 128), F32), ((384, 1152), F32)]
-    args = [edge, near, far, q, do, xq, kv, xk, w, place]
-    specs = [SMEM, whole(near), whole(far)] + [block((1,) + a.shape[1:], rp) for a in (q, do, xq, kv, xk)] + [whole(w), whole(place)]
-    if rp == 1:
-        args.append(dw)
-        specs.append(whole(dw))
-    return call(kernel, "attend", 12, outs, [block(s) for s, _ in outs], [
+    if rp == 0:
+        outs = [((864, 384), BF)] + outs
+    return call(kernel, "attend", 10, outs, [
         ((2, 6, 80, 384), BF), ((3, 2, 8, 6, 16, 256), BF), ((3, 2, 6, 80, 256), F32), ((3, 160, 128), F32),
         ((384, 768), BF), ((LAG + 1, 160, 256), F32), ((LAG + 1, 160, 256), BF), ((SLOTS, 256, 256), BF), ((2, 10, 8, 256), F32),
-    ], args, specs)
-
-
-def cross_call(rp, edge, near, far, far_g, stat_near, stat_far, kv, own, w, split):
+    ], args)
+
+
+def cross_call(rp, near, far, far_gs, stat_near, stat_far, kv, own, w, split):
+    args = [near, far, far_gs, stat_near, stat_far, kv, own, w, split]
+    if rp == 0:
+        del args[4]
+
     def kernel(*refs):
+        refs = list(refs)
+        if rp == 0:
+            refs.insert(4, None)
         cross_kernel(rp, *refs)
 
-    args = [edge, near, far, far_g, stat_near, stat_far, kv, own, w, split]
-    specs = [SMEM] + [whole(a) for a in args[1:6]] + [block((1,) + kv.shape[1:], rp)] + [whole(a) for a in args[7:]]
-    return call(kernel, "cross", 9, [((3, 2, 4, 80, 256), BF)], [block((3, 2, 4, 80, 256))], [
+    return call(kernel, "cross", 6, [((3, 2, 4, 80, 256), BF)], [
         ((2, 8, 32, 384), BF), ((2, 3, 2, 8, 32, 128), BF), ((2, 3, 2, 8, 32, 128), BF),
         ((3, 64, 256), F32), ((LAG + 1, 2, 64, 256), F32), ((LAG + 1, 2, 64, 256), BF), ((SLOTS, 2, 256, 128), BF),
         ((4, 80, 256), F32), ((2, 4, 8, 256), F32), ((2, 3, 2, 8, 256), F32),
-    ], args, specs)[0]
+    ], args)[0]
 
 
 def final_call(shape, *args):
-    return call(final_kernel, "final", 4, [(shape, BF)], [block(shape)], [], args, [whole(a) for a in args])[0]
+    return call(final_kernel, "final", 4, [(shape, BF)], [], args)[0]
 
 
 def shards(features, qkv_weight, grad_output):
     row_count, col_count, width = features.shape
     count = lax.axis_size("row")
-    index = lax.axis_index("row")
-    odd = index & 1
     near = [(i, i ^ 1) for i in range(count)]
     far = [(i, i + 1) for i in range(1, count - 1, 2)] + [(i + 1, i) for i in range(1, count - 1, 2)]
     place, split = column_maps()
-    edge = jnp.stack([jnp.where(index == 0, 3, 0), jnp.where(index == count - 1, 7, 10), odd]).astype(jnp.int32)
     x4, g4 = (a.reshape(row_count // 2, 2, col_count, width) for a in (features, grad_output))
-    send_x0, send_x1, send_g, send_near = pack_call(edge, x4, g4)
-
+    rim = (col_count, width)
+    send_x0 = raw_call(first_kernel, "first", [(3,) + rim], [(3,) + rim], (x4,))[0]
     far_x0 = lax.ppermute(send_x0, "row", far)
+    send_x1, send_g, send_near = raw_call(pack_kernel, "pack", [(3,) + rim, (3, 2) + rim, (2, 3, 2) + rim],
+                                          [x4.shape, g4.shape], (send_x0, x4, g4))
     near_xg = lax.ppermute(send_near, "row", near)
     q, do, xq, kv, xk = own_call(x4, g4, qkv_weight, place, split)
     far_x1 = lax.ppermute(after(send_x1, far_x0, xk), "row", far)
-    dq0, own0, stat0, dw0 = attend_call(0, edge, near_xg, far_x0, q, do, xq, kv, xk, qkv_weight, place, None)
+    gs, dq0, own0, stat0, dw0 = attend_call(0, near_xg, far_x0, q, do, xq, kv, xk, qkv_weight, place, send_g)
     far_x1 = after(far_x1, dw0)
-    far_g = lax.ppermute(after(send_g, far_x1), "row", far)
+    far_gs = lax.ppermute(after(gs, far_x1), "row", far)
     stat0_near = lax.ppermute(stat0, "row", near)
-    stat0_far = lax.ppermute(stat0, "row", far)
-    dq1, own1, stat1, dw1 = attend_call(1, edge, near_xg, far_x1, q, do, xq, kv, xk, qkv_weight, place, dw0)
-    far_g, stat0_near, stat0_far, _ = lax.optimization_barrier((far_g, stat0_near, stat0_far, dq1))
+    dq1, own1, stat1, dw1 = attend_call(1, near_xg, far_x1, q, do, xq, kv, xk, qkv_weight, place)
+    far_gs, stat0_near, _ = lax.optimization_barrier((far_gs, stat0_near, dq1))
     stat1_near = lax.ppermute(stat1, "row", near)
     stat1_far = lax.ppermute(stat1, "row", far)
     bits = count.bit_length() - 1
     rows = width // count
-    dkv0 = cross_call(0, edge, near_xg, far_x0, far_g, stat0_near, stat0_far, kv, own0, qkv_weight, split)
+    dkv0 = cross_call(0, near_xg, far_x0, far_gs, stat0_near, None, kv, own0, qkv_weight, split)
     stat1_near, stat1_far, _ = lax.optimization_barrier((stat1_near, stat1_far, dkv0))
-    total = exchange(dw1.reshape(count // 2, 2, rows, 3 * width), "row", 1, 1, 0, dkv0)
-    dkv1 = cross_call(1, edge, near_xg, far_x1, far_g, stat1_near, stat1_far, kv, own1, qkv_weight, split)
+    total = exchange((dw0 + dw1).reshape(count // 2, 2, rows, 3 * width), "row", 1, 1, 0, dkv0)
+    dkv1 = cross_call(1, near_xg, far_x1, far_gs, stat1_near, stat1_far, kv, own1, qkv_weight, split)
     total = exchange(total.reshape(count // 4, 2, rows, 3 * width), "row", 1, 1, 1, dkv1)
     grad_features = final_call(features.shape, dq0, dq1, dkv0, dkv1, qkv_weight, place.T, split.T)
     low = 2

time: 76.4 us -> 69.8 us (0.914)
  Pallas kernels: 41.3 us -> 37.3 us
  local copies, waits for them, and re-layouts: 5.14 us -> 1.34 us
  starting transfers between devices: 24.8 us -> 27.2 us
    ppermute x1, starting transfers between devices: 4.38 us -> 11.6 us  [shards(): stat1_near = lax.ppermute(stat1, 'row', near)]
    ppermute x1, starting transfers between devices: 6.5 us -> 2.31 us  [shards(): stat0_near = lax.ppermute(stat0, 'row', near)]
    pallas_call x7 -> x8, Pallas kernels: 41.3 us -> 37.3 us  [the longest x5 29.4 us: call(): pl.pallas_call(kernel, out_shape=[jax.ShapeDtypeStruct(s, t) for s, t in...]
    unnamed x30 -> x22, local copies, waits for them, and re-layouts: 5.01 us -> 1.21 us
    ppermute x5, waiting for transfers between devices: 2.19 us -> 0.99 us  [exchange(): lax.ppermute(lax.dynamic_index_in_dim(x, mine ^ turn, dim, keepdims=False...]
  transfers between devices with their start and end apart: 13 -> 12, of which waited for: 3 -> 2; matrix products, arithmetic and copies ran while one was open for 0% -> 0% of each run, Pallas kernels for 50% -> 47%
where the time goes in v3:
time: 69.8 us; the launch traced here: 69.5 us
  Pallas kernels  37.3 us (53%)
  starting transfers between devices  27.2 us (39%)
  waiting for transfers between devices  1.74 us (2%)
  local copies, waits for them, and re-layouts  1.34 us (2%)
  other arithmetic  0.98 us (1%)
  between operations  0.95 us (1%)
    pallas_call x5, Pallas kernels, call(): pl.pallas_call(kernel, out_shape=[jax.ShapeDtypeStruct(s, t) for s, t in...  29.4 us
    ppermute x1, starting transfers between devices, shards(): stat1_near = lax.ppermute(stat1, 'row', near)  11.6 us
    ppermute x5, starting transfers between devices, exchange(): lax.ppermute(lax.dynamic_index_in_dim(x, mine ^ turn, dim, keepdims=False...  9.85 us
    pallas_call x2, Pallas kernels, raw_call(): pl.pallas_call(kernel, out_shape=[jax.ShapeDtypeStruct(s, BF) for s in ou...  4.37 us
    pallas_call x1, Pallas kernels, own_call(): pl.pallas_call(own_kernel, out_shape=[jax.ShapeDtypeStruct(s, BF) for s i...  3.51 us
    ppermute x1, starting transfers between devices, shards(): stat0_near = lax.ppermute(stat0, 'row', near)  2.31 us
  transfers between devices with their start and end apart: 12, of which 2 were waited for; matrix products, arithmetic and copies ran while one was open for 0% of the time, Pallas kernels for 47%

profile of v3, /device:TPU:0, one launch (start us, length us, event | category | flops | bytes accessed | tf_op | source)
XLA Modules:
  0.0 69.5 jit_solution(6914959551382704730)
XLA Ops:
  0.6 0.0 copy-start.6
  0.6 0.0 copy-start.8
  0.7 0.0 copy-start
  0.7 0.0 copy-start.1
  0.7 1.8 %first.1.first_ref = bf16[3,128,384]{2,1,0:T(8,128)(2,1)} custom-call(bf16[4,2,128,384]{3,2,1,0:T(8,128)(2,1)} %bitcast.18), custom_call_target="tpu_custom_call" | custom-call | tf_op jit(solution)/shard_map/first/pallas_call | solution.py:429
  2.5 0.0 copy-start.9
  2.5 2.5 %pack.1 = (bf16[3,128,384]{2,1,0:T(8,128)(2,1)}, bf16[3,2,128,384]{3,2,1,0:T(8,128)(2,1)}, bf16[2,3,2,128,384]{4,3,2,1,0:T(8,128)(2,1)}) custom-call(bf16[3,128,384]{2,1,0:T(8,128)(2,1)} %first.1.first_ref, bf16[4,2,128,384]{3,2,1,0:T(8,128)(2,1)} %bitcast.19, bf16[4,2,128,384]{3,2,1,0:T(8,128)(2,1)} %bitcast.21), custom_call_target="tpu_custom_call" | custom-call | tf_op jit(solution)/shard_map/pack/pallas_call | solution.py:429
  5.1 0.5 collective-permute-start
  5.6 0.0 copy-done.9
  5.6 0.7 collective-permute-start.1
  6.3 0.0 copy-done.6
  6.3 0.0 copy-done.8
  6.3 0.0 copy-done
  6.3 0.0 copy-done.1
  6.4 0.0 copy-start.2
  6.4 1.2 %copy-done.2 = bf16[384,1152]{1,0:T(8,128)(2,1)S(1)} copy-done((bf16[384,1152]{1,0:T(8,128)(2,1)S(1)}, bf16[384,1152]{1,0:T(8,128)(2,1)}, u32[]{:S(2)}) %copy-start.2) | copy-done | bytes 884760
  7.5 3.5 %own.1 = (bf16[2,3,2,8,32,128]{5,4,3,2,1,0:T(8,128)(2,1)S(1)}, bf16[2,3,2,8,32,128]{5,4,3,2,1,0:T(8,128)(2,1)S(1)}, bf16[2,2,8,32,384]{4,3,2,1,0:T(8,128)(2,1)S(...) custom-call(bf16[4,2,128,384]{3,2,1,0:T(8,128)(2,1)S(1)} %bitcast.20, ...), custom_call_target="tpu_custom_call" | custom-call | flops 4000000000 | bytes 1048576 | tf_op jit(solution)/shard_map/own/pallas_call | solution.py:441
  11.0 0.0 collective-permute-done.1.refs_1_
  11.1 0.7 collective-permute-start.2
  11.8 0.0 collective-permute-done.refs_0_
  11.8 7.9 %attend.2 = (bf16[864,384]{1,0:T(8,128)(2,1)S(1)}, bf16[3,2,8,32,128]{4,3,2,1,0:T(8,128)(2,1)S(1)}, f32[3,2,4,80,256]{4,3,2,1,0:T(8,128)S(1)}, f32[2,3,2,8,128]{4,3,2,1,0:T(8,128)S(1)}, f32[384,1152]{1,0:T(8,128)S(1)}) custom-call(bf16[2,3,2,128,384]{4,3,2,1,0:T(8,128)(2,1)S(1)} %collective-permute-done.refs_0_, ...), custom_call_target="tpu_custom_call" | custom-call | flops 10000000000 | bytes 1048576 | tf_op jit(solution)/shard_map/attend/pallas_call | solution.py:416
  19.6 0.0 collective-permute-done.2.refs_1_
  19.7 0.9 %collective-permute-start.3 = (bf16[864,384]{1,0:T(8,128)(2,1)S(1)}, bf16[864,384]{1,0:T(8,128)(2,1)S(1)}, u32[]{:S(2)}, u32[]{:S(2)}) collective-permute-start(bf16[864,384]{1,0:T(8,128)(2,1)S(1)} %get-tuple-element.45), channel_id=1, source_target_pairs={{1,2},{3,4},{5,6},{7,8},{9,10},{11,12},{13,14},{2,1},{4,3},{6,5},{... | collective-permute-start | bytes 1990664 | tf_op jit(solution)/shard_map/ppermute | solution.py:505
  20.6 7.7 %attend.3 = (bf16[3,2,8,32,128]{4,3,2,1,0:T(8,128)(2,1)S(1)}, f32[3,2,4,80,256]{4,3,2,1,0:T(8,128)S(1)}, f32[2,3,2,8,128]{4,3,2,1,0:T(8,128)S(1)}, f32[384,1152]{1,0:T(8,128)S(1)}) custom-call(bf16[2,3,2,128,384]{4,3,2,1,0:T(8,128)(2,1)S(1)} %collective-permute-done.refs_0_, bf16[3,128,384]{2,1,0:T(8,128)(2,1)S(1)} %collective-permute-done.2.refs_1_, ...), custom_call_target="tpu_custom_call" | custom-call | flops 10000000000 | bytes 1048576 | tf_op jit(solution)/shard_map/attend/pallas_call | solution.py:416
  28.3 11.6 %collective-permute-start.5 = (f32[2,3,2,8,128]{4,3,2,1,0:T(8,128)S(1)}, f32[2,3,2,8,128]{4,3,2,1,0:T(8,128)S(1)}, u32[]{:S(2)}, u32[]{:S(2)}) collective-permute-start(f32[2,3,2,8,128]{4,3,2,1,0:T(8,128)S(1)} %get-tuple-element.50), channel_id=1, source_target_pairs={{0,1},{1,0},{2,3},{3,2},{4,5},{5,4},{6,7},{7,6},{8,9},{9,8},{10,11... | collective-permute-start | bytes 147464 | tf_op jit(solution)/shard_map/ppermute | solution.py:509
  39.9 0.7 collective-permute-start.6
  40.6 0.2 add.45
  40.8 2.3 %collective-permute-start.4 = (f32[2,3,2,8,128]{4,3,2,1,0:T(8,128)S(1)}, f32[2,3,2,8,128]{4,3,2,1,0:T(8,128)S(1)}, u32[]{:S(2)}, u32[]{:S(2)}) collective-permute-start(f32[2,3,2,8,128]{4,3,2,1,0:T(8,128)S(1)} %get-tuple-element.46), channel_id=1, source_target_pairs={{0,1},{1,0},{2,3},{3,2},{4,5},{5,4},{6,7},{7,6},{8,9},{9,8},{10,11... | collective-permute-start | bytes 147464 | tf_op jit(solution)/shard_map/ppermute | solution.py:506
  43.1 0.1 collective-permute-start.7
  43.2 0.7 %collective-permute-done.4.refs_3_ = f32[2,3,2,8,128]{4,3,2,1,0:T(8,128)S(1)} collective-permute-done((f32[2,3,2,8,128]{4,3,2,1,0:T(8,128)S(1)}, f32[2,3,2,8,128]{4,3,2,1,0:T(8,128)S(1)}, u32[]{:S(2)}, u32[]{:S(2)}) %collective-permute-start.4) | collective-permute-done | bytes 49184 | tf_op jit(solution)/shard_map/ppermute | solution.py:506
  44.0 0.0 collective-permute-done.3.refs_2_
  44.0 5.2 %cross.2.dkv0_ref = bf16[3,2,4,80,256]{4,3,2,1,0:T(8,128)(2,1)S(1)} custom-call(bf16[2,3,2,128,384]{4,3,2,1,0:T(8,128)(2,1)S(1)} %collective-permute-done.refs_0_, bf16[3,128,384]{2,1,0:T(8,128)(2,1)S(1)} %collective-permute-done.1.refs_1_, bf16[864,384]{1,0:T(8,128)(2,1)S(1)} %collective-permute-done.3.refs_2_, ...), custom_call_target="tpu_custom_call" | custom-call | flops 6000000000 | bytes 1048576 | tf_op jit(solution)/shard_map/cross/pallas_call | solution.py:416
  49.1 0.0 collective-permute-done.7
  49.2 0.1 bitcast_add_fusion
  49.3 5.5 %collective-permute-start.8 = (bf16[4,24,1152]{2,1,0:T(8,128)(2,1)S(1)}, bf16[4,24,1152]{2,1,0:T(8,128)(2,1)S(1)}, u32[]{:S(2)}, u32[]{:S(2)}) collective-permute-start(bf16[4,24,1152]{2,1,0:T(8,128)(2,1)S(1)} %fusion.1), channel_id=1, source_target_pairs={{0,2},{1,3},{2,0},{3,1},{4,6},{5,7},{6,4},{7,5},{8,10},{9,11},{10,... | collective-permute-start | bytes 663560 | tf_op jit(solution)/shard_map/ppermute | solution.py:404
  54.7 0.0 collective-permute-done.5.refs_3_
  54.7 0.0 collective-permute-done.6.refs_4_
  54.8 0.0 copy-start.7
  54.8 4.9 %cross.3.dkv1_ref = bf16[3,2,4,80,256]{4,3,2,1,0:T(8,128)(2,1)S(1)} custom-call(bf16[2,3,2,128,384]{4,3,2,1,0:T(8,128)(2,1)S(1)} %collective-permute-done.refs_0_, bf16[3,128,384]{2,1,0:T(8,128)(2,1)S(1)} %collective-permute-done.2.refs_1_, bf16[864,384]{1,0:T(8,128)(2,1)S(1)} %collective-permute-done.3.refs_2_, ...), custom_call_target="tpu_custom_call" | custom-call | flops 6000000000 | bytes 1048576 | tf_op jit(solution)/shard_map/cross/pallas_call | solution.py:416
  59.7 0.0 collective-permute-done.8
  59.8 2.9 %collective-permute-start.10 = (bf16[1,24,1152]{2,1,0:T(8,128)(2,1)S(1)}, bf16[1,24,1152]{2,1,0:T(8,128)(2,1)S(1)}, u32[]{:S(2)}, u32[]{:S(2)}) collective-permute-start(bf16[1,24,1152]{2,1,0:T(8,128)(2,1)S(1)} %get-tuple-element.61), channel_id=1, source_target_pairs={{0,8},{1,9},{2,10},{3,11},{4,12},{5,13},{6,14},{7,15},{8,0},{9,1},... | collective-permute-start | bytes 165896 | tf_op jit(solution)/shard_map/ppermute | solution.py:404
  62.8 1.3 %collective-permute-start.11 = (bf16[1,24,1152]{2,1,0:T(8,128)(2,1)S(1)}, bf16[1,24,1152]{2,1,0:T(8,128)(2,1)S(1)}, u32[]{:S(2)}, u32[]{:S(2)}) collective-permute-start(bf16[1,24,1152]{2,1,0:T(8,128)(2,1)S(1)} %get-tuple-element.60), channel_id=1, source_target_pairs={{0,12},{1,13},{2,14},{3,15},{4,8},{5,9},{6,10},{7,11},{8,4},{9,5},... | collective-permute-start | bytes 165896 | tf_op jit(solution)/shard_map/ppermute | solution.py:404
  64.1 0.0 collective-permute-start.9
  64.1 3.8 %final.1 = bf16[8,128,384]{2,1,0:T(8,128)(2,1)} custom-call(bf16[3,2,8,32,128]{4,3,2,1,0:T(8,128)(2,1)S(1)} %get-tuple-element.38.dq0_ref, bf16[3,2,8,32,128]{4,3,2,1,0:T(8,128)(2,1)S(1)} %get-tuple-element.43.dq1_ref, bf16[3,2,4,80,256]{4,3,2,1,0:T(8,128)(2,1)S(1)} %cross.2.dkv0_ref, bf16[3,2,4,80,256]{4,3,2,1,0:T(8,128)(2,1)S(1)} %cross.3.dkv1_ref, ...), custom_call_target="tpu_custom_call" | custom-call | flops 4000000000 | bytes 1048576 | tf_op jit(solution)/shard_map/final/pallas_call | solution.py:416
  67.9 0.0 collective-permute-done.10
  67.9 0.9 %collective-permute-done.11 = bf16[1,24,1152]{2,1,0:T(8,128)(2,1)S(1)} collective-permute-done((bf16[1,24,1152]{2,1,0:T(8,128)(2,1)S(1)}, bf16[1,24,1152]{2,1,0:T(8,128)(2,1)S(1)}, u32[]{:S(2)}, u32[]{:S(2)}) %collective-permute-start.11) | collective-permute-done | bytes 55328 | tf_op jit(solution)/shard_map/ppermute | solution.py:404
  68.8 0.0 collective-permute-done.9
  68.9 0.7 multiply_bitcast_fusion
  (13 shorter events, 0.2 us)
Async XLA Ops:
  0.6 5.7 %copy-start.6 = (bf16[160,128]{1,0:T(8,128)(2,1)S(1)}, bf16[160,128]{1,0:T(8,128)(2,1)}, u32[]{:S(2)}) copy-start(bf16[160,128]{1,0:T(8,128)(2,1)} %constant.41.clone.refs_3_.refs_8_) | copy-start | bytes 122884
  0.6 5.7 %copy-start.8 = (bf16[128,128]{1,0:T(8,128)(2,1)S(1)}, bf16[128,128]{1,0:T(8,128)(2,1)}, u32[]{:S(2)}) copy-start(bf16[128,128]{1,0:T(8,128)(2,1)} %constant.42.clone.refs_4_.refs_7_.refs_8_) | copy-start | bytes 98308
  0.7 5.7 %copy-start = (bf16[8,128,384]{2,1,0:T(8,128)(2,1)S(1)}, bf16[8,128,384]{2,1,0:T(8,128)(2,1)}, u32[]{:S(2)}) copy-start(bf16[8,128,384]{2,1,0:T(8,128)(2,1)} %param.5) | copy-start | bytes 2359300
  0.7 5.7 %copy-start.1 = (bf16[8,128,384]{2,1,0:T(8,128)(2,1)S(1)}, bf16[8,128,384]{2,1,0:T(8,128)(2,1)}, u32[]{:S(2)}) copy-start(bf16[8,128,384]{2,1,0:T(8,128)(2,1)} %param.7) | copy-start | bytes 2359300
  2.5 3.1 %copy-start.9 = (bf16[3,128,384]{2,1,0:T(8,128)(2,1)S(1)}, bf16[3,128,384]{2,1,0:T(8,128)(2,1)}, u32[]{:S(2)}) copy-start(bf16[3,128,384]{2,1,0:T(8,128)(2,1)} %first.1.first_ref) | copy-start | bytes 884740
  5.1 6.7 %collective-permute-start = (bf16[2,3,2,128,384]{4,3,2,1,0:T(8,128)(2,1)}, bf16[2,3,2,128,384]{4,3,2,1,0:T(8,128)(2,1)S(1)}, u32[]{:S(2)}, u32[]{:S(2)}) collective-permute-start(bf16[2,3,2,128,384]{4,3,2,1,0:T(8,128)(2,1)} %get-tuple-element.31), channel_id=1, source_target_pairs={{0,1},{1,0},{2,3},{3,2},{4,5},{5,4},{6,7},{7,6},{8,9},{9,8},{10,11... | collective-permute-start | bytes 3538952 | tf_op jit(solution)/shard_map/ppermute | solution.py:500
  5.6 5.5 %collective-permute-start.1 = (bf16[3,128,384]{2,1,0:T(8,128)(2,1)S(1)}, bf16[3,128,384]{2,1,0:T(8,128)(2,1)S(1)}, u32[]{:S(2)}, u32[]{:S(2)}) collective-permute-start(bf16[3,128,384]{2,1,0:T(8,128)(2,1)S(1)} %copy-done.9), channel_id=1, source_target_pairs={{1,2},{3,4},{5,6},{7,8},{9,10},{11,12},{13,14},{2,1},{4,3},{6,5},{... | collective-permute-start | bytes 884744 | tf_op jit(solution)/shard_map/ppermute | solution.py:497
  6.4 1.2 %copy-start.2 = (bf16[384,1152]{1,0:T(8,128)(2,1)S(1)}, bf16[384,1152]{1,0:T(8,128)(2,1)}, u32[]{:S(2)}) copy-start(bf16[384,1152]{1,0:T(8,128)(2,1)} %w_ref.1) | copy-start | bytes 2654212
  7.5 3.5 %copy-start.10 = (bf16[3,128,384]{2,1,0:T(8,128)(2,1)S(1)}, bf16[3,128,384]{2,1,0:T(8,128)(2,1)}, u32[]{:S(2)}) copy-start(bf16[3,128,384]{2,1,0:T(8,128)(2,1)} %get-tuple-element.40) | copy-start | bytes 884740
  7.5 4.2 %copy-start.3 = (bf16[384,1152]{1,0:T(8,128)(2,1)S(1)}, bf16[384,1152]{1,0:T(8,128)(2,1)}, u32[]{:S(2)}) copy-start(bf16[384,1152]{1,0:T(8,128)(2,1)} %w_ref.1) | copy-start | bytes 2654212
  7.5 4.3 %copy-start.4 = (bf16[3,2,128,384]{3,2,1,0:T(8,128)(2,1)S(1)}, bf16[3,2,128,384]{3,2,1,0:T(8,128)(2,1)}, u32[]{:S(2)}) copy-start(bf16[3,2,128,384]{3,2,1,0:T(8,128)(2,1)} %get-tuple-element.37.refs_9_) | copy-start | bytes 1769476
  11.1 8.6 %collective-permute-start.2 = (bf16[3,128,384]{2,1,0:T(8,128)(2,1)S(1)}, bf16[3,128,384]{2,1,0:T(8,128)(2,1)S(1)}, u32[]{:S(2)}, u32[]{:S(2)}) collective-permute-start(bf16[3,128,384]{2,1,0:T(8,128)(2,1)S(1)} %copy-done.10), channel_id=1, source_target_pairs={{1,2},{3,4},{5,6},{7,8},{9,10},{11,12},{13,14},{2,1},{4,3},{6,5},{... | collective-permute-start | bytes 884744 | tf_op jit(solution)/shard_map/ppermute | solution.py:502
  19.7 24.3 %collective-permute-start.3 = (bf16[864,384]{1,0:T(8,128)(2,1)S(1)}, bf16[864,384]{1,0:T(8,128)(2,1)S(1)}, u32[]{:S(2)}, u32[]{:S(2)}) collective-permute-start(bf16[864,384]{1,0:T(8,128)(2,1)S(1)} %get-tuple-element.45), channel_id=1, source_target_pairs={{1,2},{3,4},{5,6},{7,8},{9,10},{11,12},{13,14},{2,1},{4,3},{6,5},{... | collective-permute-start | bytes 1990664 | tf_op jit(solution)/shard_map/ppermute | solution.py:505
  28.3 26.5 %collective-permute-start.5 = (f32[2,3,2,8,128]{4,3,2,1,0:T(8,128)S(1)}, f32[2,3,2,8,128]{4,3,2,1,0:T(8,128)S(1)}, u32[]{:S(2)}, u32[]{:S(2)}) collective-permute-start(f32[2,3,2,8,128]{4,3,2,1,0:T(8,128)S(1)} %get-tuple-element.50), channel_id=1, source_target_pairs={{0,1},{1,0},{2,3},{3,2},{4,5},{5,4},{6,7},{7,6},{8,9},{9,8},{10,11... | collective-permute-start | bytes 147464 | tf_op jit(solution)/shard_map/ppermute | solution.py:509
  39.9 14.8 %collective-permute-start.6 = (f32[2,3,2,8,128]{4,3,2,1,0:T(8,128)S(1)}, f32[2,3,2,8,128]{4,3,2,1,0:T(8,128)S(1)}, u32[]{:S(2)}, u32[]{:S(2)}) collective-permute-start(f32[2,3,2,8,128]{4,3,2,1,0:T(8,128)S(1)} %get-tuple-element.50), channel_id=1, source_target_pairs={{1,2},{3,4},{5,6},{7,8},{9,10},{11,12},{13,14},{2,1},{4,3},{6,5},{... | collective-permute-start | bytes 147464 | tf_op jit(solution)/shard_map/ppermute | solution.py:510
  40.8 3.2 %collective-permute-start.4 = (f32[2,3,2,8,128]{4,3,2,1,0:T(8,128)S(1)}, f32[2,3,2,8,128]{4,3,2,1,0:T(8,128)S(1)}, u32[]{:S(2)}, u32[]{:S(2)}) collective-permute-start(f32[2,3,2,8,128]{4,3,2,1,0:T(8,128)S(1)} %get-tuple-element.46), channel_id=1, source_target_pairs={{0,1},{1,0},{2,3},{3,2},{4,5},{5,4},{6,7},{7,6},{8,9},{9,8},{10,11... | collective-permute-start | bytes 147464 | tf_op jit(solution)/shard_map/ppermute | solution.py:506
  43.1 6.0 %collective-permute-start.7 = (bf16[8,24,1152]{2,1,0:T(8,128)(2,1)S(1)}, bf16[8,24,1152]{2,1,0:T(8,128)(2,1)S(1)}, u32[]{:S(2)}, u32[]{:S(2)}) collective-permute-start(bf16[8,24,1152]{2,1,0:T(8,128)(2,1)S(1)} %fusion), channel_id=1, source_target_pairs={{0,1},{1,0},{2,3},{3,2},{4,5},{5,4},{6,7},{7,6},{8,9},{9,8},{10,11... | collective-permute-start | bytes 1327112 | tf_op jit(solution)/shard_map/ppermute | solution.py:404
  49.3 10.4 %collective-permute-start.8 = (bf16[4,24,1152]{2,1,0:T(8,128)(2,1)S(1)}, bf16[4,24,1152]{2,1,0:T(8,128)(2,1)S(1)}, u32[]{:S(2)}, u32[]{:S(2)}) collective-permute-start(bf16[4,24,1152]{2,1,0:T(8,128)(2,1)S(1)} %fusion.1), channel_id=1, source_target_pairs={{0,2},{1,3},{2,0},{3,1},{4,6},{5,7},{6,4},{7,5},{8,10},{9,11},{10,... | collective-permute-start | bytes 663560 | tf_op jit(solution)/shard_map/ppermute | solution.py:404
  54.7 9.4 %copy-start.5 = (bf16[128,160]{1,0:T(8,128)(2,1)S(1)}, bf16[128,160]{1,0:T(8,128)(2,1)}, u32[]{:S(2)}) copy-start(bf16[128,160]{1,0:T(8,128)(2,1)} %constant.45.unplace_ref) | copy-start | bytes 122884
  54.8 9.4 %copy-start.7 = (bf16[128,128]{1,0:T(8,128)(2,1)S(1)}, bf16[128,128]{1,0:T(8,128)(2,1)}, u32[]{:S(2)}) copy-start(bf16[128,128]{1,0:T(8,128)(2,1)} %constant.46.unsplit_ref) | copy-start | bytes 98308
  59.8 8.1 %collective-permute-start.10 = (bf16[1,24,1152]{2,1,0:T(8,128)(2,1)S(1)}, bf16[1,24,1152]{2,1,0:T(8,128)(2,1)S(1)}, u32[]{:S(2)}, u32[]{:S(2)}) collective-permute-start(bf16[1,24,1152]{2,1,0:T(8,128)(2,1)S(1)} %get-tuple-element.61), channel_id=1, source_target_pairs={{0,8},{1,9},{2,10},{3,11},{4,12},{5,13},{6,14},{7,15},{8,0},{9,1},... | collective-permute-start | bytes 165896 | tf_op jit(solution)/shard_map/ppermute | solution.py:404
  62.8 6.1 %collective-permute-start.11 = (bf16[1,24,1152]{2,1,0:T(8,128)(2,1)S(1)}, bf16[1,24,1152]{2,1,0:T(8,128)(2,1)S(1)}, u32[]{:S(2)}, u32[]{:S(2)}) collective-permute-start(bf16[1,24,1152]{2,1,0:T(8,128)(2,1)S(1)} %get-tuple-element.60), channel_id=1, source_target_pairs={{0,12},{1,13},{2,14},{3,15},{4,8},{5,9},{6,10},{7,11},{8,4},{9,5},... | collective-permute-start | bytes 165896 | tf_op jit(solution)/shard_map/ppermute | solution.py:404
  64.1 4.7 %collective-permute-start.9 = (bf16[1,24,1152]{2,1,0:T(8,128)(2,1)S(1)}, bf16[1,24,1152]{2,1,0:T(8,128)(2,1)S(1)}, u32[]{:S(2)}, u32[]{:S(2)}) collective-permute-start(bf16[1,24,1152]{2,1,0:T(8,128)(2,1)S(1)} %get-tuple-element.62), channel_id=1, source_target_pairs={{0,4},{1,5},{2,6},{3,7},{4,0},{5,1},{6,2},{7,3},{8,12},{9,13},{10,... | collective-permute-start | bytes 165896 | tf_op jit(solution)/shard_map/ppermute | solution.py:404

commit v4 on v3

--- a/solution.py
+++ b/solution.py
@@ -63,35 +63,24 @@
             store(cp, p, jnp.concatenate(halves, axis=0).astype(BF))
 
 
-def first_kernel(x_ref, x0_ref, xs, sem):
-    odd = lax.axis_index("row") & 1
-    load = pltpu.make_async_copy(x_ref.at[pl.ds(odd, 3), 0], xs, sem.at[0])
-    load.start()
-    load.wait()
-    store = pltpu.make_async_copy(xs, x0_ref, sem.at[1])
-    store.start()
-    store.wait()
-
-
-def pack_kernel(first_ref, x_ref, g_ref, x1_ref, fg_ref, near_ref, xs, gs, sem):
+def pack_kernel(x_ref, g_ref, x0_ref, near_ref, x1_ref, fg_ref, x0, near, x1, fg, sem):
     odd = lax.axis_index("row") & 1
     mine, other = pl.ds(odd, 3), pl.ds(1 - odd, 3)
-    loads = [pltpu.make_async_copy(x_ref, xs, sem.at[0]), pltpu.make_async_copy(g_ref, gs, sem.at[1])]
+    moves = [
+        (x_ref.at[mine, 0], x0, x0_ref),
+        (x_ref.at[other], near.at[0], near_ref.at[0]),
+        (g_ref.at[other], near.at[1], near_ref.at[1]),
+        (x_ref.at[mine, 1], x1, x1_ref),
+        (g_ref.at[mine], fg, fg_ref),
+    ]
+    loads = [pltpu.make_async_copy(source, room, sem.at[n]) for n, (source, room, target) in enumerate(moves)]
+    stores = [pltpu.make_async_copy(room, target, sem.at[5 + n]) for n, (source, room, target) in enumerate(moves)]
     for copy in loads:
         copy.start()
-    loads[0].wait()
-    copies = [
-        pltpu.make_async_copy(xs.at[other], near_ref.at[0], sem.at[2]),
-        pltpu.make_async_copy(xs.at[mine, 1], x1_ref, sem.at[3]),
-        pltpu.make_async_copy(gs.at[other], near_ref.at[1], sem.at[4]),
-        pltpu.make_async_copy(gs.at[mine], fg_ref, sem.at[5]),
-    ]
-    for copy in copies[:2]:
-        copy.start()
-    loads[1].wait()
-    for copy in copies[2:]:
-        copy.start()
-    for copy in copies:
+    for load, store in zip(loads, stores):
+        load.wait()
+        store.start()
+    for copy in stores:
         copy.wait()
 
 
@@ -431,7 +420,7 @@
         out_shape=[jax.ShapeDtypeStruct(s, BF) for s in outs],
         in_specs=[ANY] * len(args),
         out_specs=[ANY] * len(outs),
-        scratch_shapes=[pltpu.VMEM(s, BF) for s in scratch] + [pltpu.SemaphoreType.DMA((6,))],
+        scratch_shapes=[pltpu.VMEM(s, BF) for s in scratch] + [pltpu.SemaphoreType.DMA((10,))],
         name=name,
     )(*args)
 
@@ -493,10 +482,9 @@
     place, split = column_maps()
     x4, g4 = (a.reshape(row_count // 2, 2, col_count, width) for a in (features, grad_output))
     rim = (col_count, width)
-    send_x0 = raw_call(first_kernel, "first", [(3,) + rim], [(3,) + rim], (x4,))[0]
+    sends = [(3,) + rim, (2, 3, 2) + rim, (3,) + rim, (3, 2) + rim]
+    send_x0, send_near, send_x1, send_g = raw_call(pack_kernel, "pack", sends, sends, (x4, g4))
     far_x0 = lax.ppermute(send_x0, "row", far)
-    send_x1, send_g, send_near = raw_call(pack_kernel, "pack", [(3,) + rim, (3, 2) + rim, (2, 3, 2) + rim],
-                                          [x4.shape, g4.shape], (send_x0, x4, g4))
     near_xg = lax.ppermute(send_near, "row", near)
     q, do, xq, kv, xk = own_call(x4, g4, qkv_weight, place, split)
     far_x1 = lax.ppermute(after(send_x1, far_x0, xk), "row", far)

time: 69.8 us -> 69.9 us (level)
  local copies, waits for them, and re-layouts: 1.34 us -> 5.12 us
  starting transfers between devices: 27.2 us -> 25 us
  Pallas kernels: 37.3 us -> 35.7 us
    unnamed x22 -> x24, local copies, waits for them, and re-layouts: 1.21 us -> 5 us
    ppermute x1, starting transfers between devices: 11.6 us -> 8.67 us  [shards(): stat1_near = lax.ppermute(stat1, 'row', near)]
    pallas_call x2 -> x1, Pallas kernels: 4.37 us -> 2.57 us  [raw_call(): pl.pallas_call(kernel, out_shape=[jax.ShapeDtypeStruct(s, BF) for s in ou...]
    ppermute x1, starting transfers between devices: 2.31 us -> 3.33 us  [shards(): stat0_near = lax.ppermute(stat0, 'row', near)]
  transfers between devices with their start and end apart: 12 -> 12, of which waited for: 2 -> 2; matrix products, arithmetic and copies ran while one was open for 0% -> 0% of each run, Pallas kernels for 47% -> 48%
where the time goes in v4:
time: 69.9 us; the launch traced here: 69.5 us
  Pallas kernels  35.7 us (51%)
  starting transfers between devices  25 us (36%)
  local copies, waits for them, and re-layouts  5.12 us (7%)
  waiting for transfers between devices  1.75 us (3%)
  other arithmetic  0.98 us (1%)
  between operations  0.89 us (1%)
    pallas_call x5, Pallas kernels, call(): pl.pallas_call(kernel, out_shape=[jax.ShapeDtypeStruct(s, t) for s, t in...  29.6 us
    ppermute x5, starting transfers between devices, exchange(): lax.ppermute(lax.dynamic_index_in_dim(x, mine ^ turn, dim, keepdims=False...  9.66 us
    ppermute x1, starting transfers between devices, shards(): stat1_near = lax.ppermute(stat1, 'row', near)  8.67 us
    unnamed x24, local copies, waits for them, and re-layouts  5 us
    pallas_call x1, Pallas kernels, own_call(): pl.pallas_call(own_kernel, out_shape=[jax.ShapeDtypeStruct(s, BF) for s i...  3.52 us
    ppermute x1, starting transfers between devices, shards(): stat0_near = lax.ppermute(stat0, 'row', near)  3.33 us
    pallas_call x1, Pallas kernels, raw_call(): pl.pallas_call(kernel, out_shape=[jax.ShapeDtypeStruct(s, BF) for s in ou...  2.57 us
  transfers between devices with their start and end apart: 12, of which 2 were waited for; matrix products, arithmetic and copies ran while one was open for 0% of the time, Pallas kernels for 48%

profile of v4, /device:TPU:0, one launch (start us, length us, event | category | flops | bytes accessed | tf_op | source)
XLA Modules:
  0.0 69.5 jit_solution(10721085544929567665)
XLA Ops:
  0.6 2.6 %pack.1 = (bf16[3,128,384]{2,1,0:T(8,128)(2,1)}, bf16[2,3,2,128,384]{4,3,2,1,0:T(8,128)(2,1)}, bf16[3,128,384]{2,1,0:T(8,128)(2,1)}, bf16[3,2,128,384]{3,2,1,0:T(8,128)(2,1)}) custom-call(bf16[4,2,128,384]{3,2,1,0:T(8,128)(2,1)} %bitcast.18, bf16[4,2,128,384]{3,2,1,0:T(8,128)(2,1)} %bitcast.20), custom_call_target="tpu_custom_call" | custom-call | tf_op jit(solution)/shard_map/pack/pallas_call | solution.py:418
  3.2 0.5 collective-permute-start
  3.7 0.7 collective-permute-start.1
  4.4 0.0 copy-start
  4.4 1.1 %copy-done = bf16[8,128,384]{2,1,0:T(8,128)(2,1)S(1)} copy-done((bf16[8,128,384]{2,1,0:T(8,128)(2,1)S(1)}, bf16[8,128,384]{2,1,0:T(8,128)(2,1)}, u32[]{:S(2)}) %copy-start) | copy-done | bytes 786456
  5.6 1.1 %copy-done.1 = bf16[8,128,384]{2,1,0:T(8,128)(2,1)S(1)} copy-done((bf16[8,128,384]{2,1,0:T(8,128)(2,1)S(1)}, bf16[8,128,384]{2,1,0:T(8,128)(2,1)}, u32[]{:S(2)}) %copy-start.1) | copy-done | bytes 786456
  6.7 1.2 %copy-done.2 = bf16[384,1152]{1,0:T(8,128)(2,1)S(1)} copy-done((bf16[384,1152]{1,0:T(8,128)(2,1)S(1)}, bf16[384,1152]{1,0:T(8,128)(2,1)}, u32[]{:S(2)}) %copy-start.2) | copy-done | bytes 884760
  7.9 0.8 %copy-done.6 = bf16[160,128]{1,0:T(8,128)(2,1)S(1)} copy-done((bf16[160,128]{1,0:T(8,128)(2,1)S(1)}, bf16[160,128]{1,0:T(8,128)(2,1)}, u32[]{:S(2)}) %copy-start.6) | copy-done | bytes 40984
  8.6 0.8 %copy-done.9 = bf16[128,128]{1,0:T(8,128)(2,1)S(1)} copy-done((bf16[128,128]{1,0:T(8,128)(2,1)S(1)}, bf16[128,128]{1,0:T(8,128)(2,1)}, u32[]{:S(2)}) %copy-start.9) | copy-done | bytes 32792
  9.4 3.5 %own.1 = (bf16[2,3,2,8,32,128]{5,4,3,2,1,0:T(8,128)(2,1)S(1)}, bf16[2,3,2,8,32,128]{5,4,3,2,1,0:T(8,128)(2,1)S(1)}, bf16[2,2,8,32,384]{4,3,2,1,0:T(8,128)(2,1)S(...) custom-call(bf16[4,2,128,384]{3,2,1,0:T(8,128)(2,1)S(1)} %bitcast.19, ...), custom_call_target="tpu_custom_call" | custom-call | flops 4000000000 | bytes 1048576 | tf_op jit(solution)/shard_map/own/pallas_call | solution.py:430
  12.9 0.0 collective-permute-done.1.refs_1_
  13.0 0.0 copy-done.11
  13.0 0.7 collective-permute-start.2
  13.7 0.0 collective-permute-done.refs_0_
  13.7 0.0 copy-done.3
  13.7 0.0 copy-done.4
  13.7 0.0 copy-done.7
  13.7 7.8 %attend.2 = (bf16[864,384]{1,0:T(8,128)(2,1)S(1)}, bf16[3,2,8,32,128]{4,3,2,1,0:T(8,128)(2,1)S(1)}, f32[3,2,4,80,256]{4,3,2,1,0:T(8,128)S(1)}, f32[2,3,2,8,128]{4,3,2,1,0:T(8,128)S(1)}, f32[384,1152]{1,0:T(8,128)S(1)}) custom-call(bf16[2,3,2,128,384]{4,3,2,1,0:T(8,128)(2,1)S(1)} %collective-permute-done.refs_0_, ...), custom_call_target="tpu_custom_call" | custom-call | flops 10000000000 | bytes 1048576 | tf_op jit(solution)/shard_map/attend/pallas_call | solution.py:405
  21.5 0.0 collective-permute-done.2.refs_1_
  21.6 0.9 %collective-permute-start.3 = (bf16[864,384]{1,0:T(8,128)(2,1)S(1)}, bf16[864,384]{1,0:T(8,128)(2,1)S(1)}, u32[]{:S(2)}, u32[]{:S(2)}) collective-permute-start(bf16[864,384]{1,0:T(8,128)(2,1)S(1)} %get-tuple-element.47), channel_id=1, source_target_pairs={{1,2},{3,4},{5,6},{7,8},{9,10},{11,12},{13,14},{2,1},{4,3},{6,5},{... | collective-permute-start | bytes 1990664 | tf_op jit(solution)/shard_map/ppermute | solution.py:493
  22.4 7.7 %attend.3 = (bf16[3,2,8,32,128]{4,3,2,1,0:T(8,128)(2,1)S(1)}, f32[3,2,4,80,256]{4,3,2,1,0:T(8,128)S(1)}, f32[2,3,2,8,128]{4,3,2,1,0:T(8,128)S(1)}, f32[384,1152]{1,0:T(8,128)S(1)}) custom-call(bf16[2,3,2,128,384]{4,3,2,1,0:T(8,128)(2,1)S(1)} %collective-permute-done.refs_0_, bf16[3,128,384]{2,1,0:T(8,128)(2,1)S(1)} %collective-permute-done.2.refs_1_, ...), custom_call_target="tpu_custom_call" | custom-call | flops 10000000000 | bytes 1048576 | tf_op jit(solution)/shard_map/attend/pallas_call | solution.py:405
  30.2 8.7 %collective-permute-start.5 = (f32[2,3,2,8,128]{4,3,2,1,0:T(8,128)S(1)}, f32[2,3,2,8,128]{4,3,2,1,0:T(8,128)S(1)}, u32[]{:S(2)}, u32[]{:S(2)}) collective-permute-start(f32[2,3,2,8,128]{4,3,2,1,0:T(8,128)S(1)} %get-tuple-element.52), channel_id=1, source_target_pairs={{0,1},{1,0},{2,3},{3,2},{4,5},{5,4},{6,7},{7,6},{8,9},{9,8},{10,11... | collective-permute-start | bytes 147464 | tf_op jit(solution)/shard_map/ppermute | solution.py:497
  38.9 0.7 collective-permute-start.6
  39.5 0.0 copy-start.10
  39.5 0.2 add.45
  39.7 3.3 %collective-permute-start.4 = (f32[2,3,2,8,128]{4,3,2,1,0:T(8,128)S(1)}, f32[2,3,2,8,128]{4,3,2,1,0:T(8,128)S(1)}, u32[]{:S(2)}, u32[]{:S(2)}) collective-permute-start(f32[2,3,2,8,128]{4,3,2,1,0:T(8,128)S(1)} %get-tuple-element.48), channel_id=1, source_target_pairs={{0,1},{1,0},{2,3},{3,2},{4,5},{5,4},{6,7},{7,6},{8,9},{9,8},{10,11... | collective-permute-start | bytes 147464 | tf_op jit(solution)/shard_map/ppermute | solution.py:494
  43.1 0.1 collective-permute-start.7
  43.2 0.7 %collective-permute-done.4.refs_3_ = f32[2,3,2,8,128]{4,3,2,1,0:T(8,128)S(1)} collective-permute-done((f32[2,3,2,8,128]{4,3,2,1,0:T(8,128)S(1)}, f32[2,3,2,8,128]{4,3,2,1,0:T(8,128)S(1)}, u32[]{:S(2)}, u32[]{:S(2)}) %collective-permute-start.4) | collective-permute-done | bytes 49184 | tf_op jit(solution)/shard_map/ppermute | solution.py:494
  43.9 0.0 collective-permute-done.3.refs_2_
  43.9 0.0 copy-done.10
  43.9 5.2 %cross.2.dkv0_ref = bf16[3,2,4,80,256]{4,3,2,1,0:T(8,128)(2,1)S(1)} custom-call(bf16[2,3,2,128,384]{4,3,2,1,0:T(8,128)(2,1)S(1)} %collective-permute-done.refs_0_, bf16[3,128,384]{2,1,0:T(8,128)(2,1)S(1)} %collective-permute-done.1.refs_1_, bf16[864,384]{1,0:T(8,128)(2,1)S(1)} %collective-permute-done.3.refs_2_, ...), custom_call_target="tpu_custom_call" | custom-call | flops 6000000000 | bytes 1048576 | tf_op jit(solution)/shard_map/cross/pallas_call | solution.py:405
  49.2 0.0 collective-permute-done.7
  49.2 0.1 bitcast_add_fusion
  49.3 4.6 %collective-permute-start.8 = (bf16[4,24,1152]{2,1,0:T(8,128)(2,1)S(1)}, bf16[4,24,1152]{2,1,0:T(8,128)(2,1)S(1)}, u32[]{:S(2)}, u32[]{:S(2)}) collective-permute-start(bf16[4,24,1152]{2,1,0:T(8,128)(2,1)S(1)} %fusion.1), channel_id=1, source_target_pairs={{0,2},{1,3},{2,0},{3,1},{4,6},{5,7},{6,4},{7,5},{8,10},{9,11},{10,... | collective-permute-start | bytes 663560 | tf_op jit(solution)/shard_map/ppermute | solution.py:393
  53.9 0.0 collective-permute-done.5.refs_3_
  53.9 0.0 collective-permute-done.6.refs_4_
  53.9 0.0 copy-start.8
  54.0 5.0 %cross.3.dkv1_ref = bf16[3,2,4,80,256]{4,3,2,1,0:T(8,128)(2,1)S(1)} custom-call(bf16[2,3,2,128,384]{4,3,2,1,0:T(8,128)(2,1)S(1)} %collective-permute-done.refs_0_, bf16[3,128,384]{2,1,0:T(8,128)(2,1)S(1)} %collective-permute-done.2.refs_1_, bf16[864,384]{1,0:T(8,128)(2,1)S(1)} %collective-permute-done.3.refs_2_, ...), custom_call_target="tpu_custom_call" | custom-call | flops 6000000000 | bytes 1048576 | tf_op jit(solution)/shard_map/cross/pallas_call | solution.py:405
  59.0 0.0 collective-permute-done.8
  59.1 3.6 %collective-permute-start.10 = (bf16[1,24,1152]{2,1,0:T(8,128)(2,1)S(1)}, bf16[1,24,1152]{2,1,0:T(8,128)(2,1)S(1)}, u32[]{:S(2)}, u32[]{:S(2)}) collective-permute-start(bf16[1,24,1152]{2,1,0:T(8,128)(2,1)S(1)} %get-tuple-element.63), channel_id=1, source_target_pairs={{0,8},{1,9},{2,10},{3,11},{4,12},{5,13},{6,14},{7,15},{8,0},{9,1},... | collective-permute-start | bytes 165896 | tf_op jit(solution)/shard_map/ppermute | solution.py:393
  62.7 1.3 %collective-permute-start.11 = (bf16[1,24,1152]{2,1,0:T(8,128)(2,1)S(1)}, bf16[1,24,1152]{2,1,0:T(8,128)(2,1)S(1)}, u32[]{:S(2)}, u32[]{:S(2)}) collective-permute-start(bf16[1,24,1152]{2,1,0:T(8,128)(2,1)S(1)} %get-tuple-element.62), channel_id=1, source_target_pairs={{0,12},{1,13},{2,14},{3,15},{4,8},{5,9},{6,10},{7,11},{8,4},{9,5},... | collective-permute-start | bytes 165896 | tf_op jit(solution)/shard_map/ppermute | solution.py:393
  64.0 0.0 collective-permute-start.9
  64.0 0.0 copy-done.5
  64.0 3.8 %final.1 = bf16[8,128,384]{2,1,0:T(8,128)(2,1)} custom-call(bf16[3,2,8,32,128]{4,3,2,1,0:T(8,128)(2,1)S(1)} %get-tuple-element.40.dq0_ref, bf16[3,2,8,32,128]{4,3,2,1,0:T(8,128)(2,1)S(1)} %get-tuple-element.45.dq1_ref, bf16[3,2,4,80,256]{4,3,2,1,0:T(8,128)(2,1)S(1)} %cross.2.dkv0_ref, bf16[3,2,4,80,256]{4,3,2,1,0:T(8,128)(2,1)S(1)} %cross.3.dkv1_ref, ...), custom_call_target="tpu_custom_call" | custom-call | flops 4000000000 | bytes 1048576 | tf_op jit(solution)/shard_map/final/pallas_call | solution.py:405
  67.8 0.0 collective-permute-done.10
  67.8 1.0 %collective-permute-done.11 = bf16[1,24,1152]{2,1,0:T(8,128)(2,1)S(1)} collective-permute-done((bf16[1,24,1152]{2,1,0:T(8,128)(2,1)S(1)}, bf16[1,24,1152]{2,1,0:T(8,128)(2,1)S(1)}, u32[]{:S(2)}, u32[]{:S(2)}) %collective-permute-start.11) | collective-permute-done | bytes 55328 | tf_op jit(solution)/shard_map/ppermute | solution.py:393
  68.8 0.0 collective-permute-done.9
  68.8 0.7 multiply_bitcast_fusion
  (14 shorter events, 0.2 us)
Async XLA Ops:
  3.2 10.4 %collective-permute-start = (bf16[2,3,2,128,384]{4,3,2,1,0:T(8,128)(2,1)}, bf16[2,3,2,128,384]{4,3,2,1,0:T(8,128)(2,1)S(1)}, u32[]{:S(2)}, u32[]{:S(2)}) collective-permute-start(bf16[2,3,2,128,384]{4,3,2,1,0:T(8,128)(2,1)} %get-tuple-element.32), channel_id=1, source_target_pairs={{0,1},{1,0},{2,3},{3,2},{4,5},{5,4},{6,7},{7,6},{8,9},{9,8},{10,11... | collective-permute-start | bytes 3538952 | tf_op jit(solution)/shard_map/ppermute | solution.py:488
  3.7 9.2 %collective-permute-start.1 = (bf16[3,128,384]{2,1,0:T(8,128)(2,1)}, bf16[3,128,384]{2,1,0:T(8,128)(2,1)S(1)}, u32[]{:S(2)}, u32[]{:S(2)}) collective-permute-start(bf16[3,128,384]{2,1,0:T(8,128)(2,1)} %get-tuple-element.33), channel_id=1, source_target_pairs={{1,2},{3,4},{5,6},{7,8},{9,10},{11,12},{13,14},{2,1},{4,3},{6,5},{... | collective-permute-start | bytes 884744 | tf_op jit(solution)/shard_map/ppermute | solution.py:487
  4.4 1.1 %copy-start = (bf16[8,128,384]{2,1,0:T(8,128)(2,1)S(1)}, bf16[8,128,384]{2,1,0:T(8,128)(2,1)}, u32[]{:S(2)}) copy-start(bf16[8,128,384]{2,1,0:T(8,128)(2,1)} %param.5) | copy-start | bytes 2359300
  5.6 1.1 %copy-start.1 = (bf16[8,128,384]{2,1,0:T(8,128)(2,1)S(1)}, bf16[8,128,384]{2,1,0:T(8,128)(2,1)}, u32[]{:S(2)}) copy-start(bf16[8,128,384]{2,1,0:T(8,128)(2,1)} %param.7) | copy-start | bytes 2359300
  6.7 1.2 %copy-start.2 = (bf16[384,1152]{1,0:T(8,128)(2,1)S(1)}, bf16[384,1152]{1,0:T(8,128)(2,1)}, u32[]{:S(2)}) copy-start(bf16[384,1152]{1,0:T(8,128)(2,1)} %w_ref.1) | copy-start | bytes 2654212
  7.9 0.8 %copy-start.6 = (bf16[160,128]{1,0:T(8,128)(2,1)S(1)}, bf16[160,128]{1,0:T(8,128)(2,1)}, u32[]{:S(2)}) copy-start(bf16[160,128]{1,0:T(8,128)(2,1)} %constant.41.clone.refs_3_.refs_8_) | copy-start | bytes 122884
  8.6 0.8 %copy-start.9 = (bf16[128,128]{1,0:T(8,128)(2,1)S(1)}, bf16[128,128]{1,0:T(8,128)(2,1)}, u32[]{:S(2)}) copy-start(bf16[128,128]{1,0:T(8,128)(2,1)} %constant.42.clone.refs_4_.refs_7_.refs_8_) | copy-start | bytes 98308
  9.4 3.6 %copy-start.11 = (bf16[3,128,384]{2,1,0:T(8,128)(2,1)S(1)}, bf16[3,128,384]{2,1,0:T(8,128)(2,1)}, u32[]{:S(2)}) copy-start(bf16[3,128,384]{2,1,0:T(8,128)(2,1)} %get-tuple-element.42) | copy-start | bytes 884740
  9.4 4.3 %copy-start.3 = (bf16[384,1152]{1,0:T(8,128)(2,1)S(1)}, bf16[384,1152]{1,0:T(8,128)(2,1)}, u32[]{:S(2)}) copy-start(bf16[384,1152]{1,0:T(8,128)(2,1)} %w_ref.1) | copy-start | bytes 2654212
  9.4 4.3 %copy-start.4 = (bf16[3,2,128,384]{3,2,1,0:T(8,128)(2,1)S(1)}, bf16[3,2,128,384]{3,2,1,0:T(8,128)(2,1)}, u32[]{:S(2)}) copy-start(bf16[3,2,128,384]{3,2,1,0:T(8,128)(2,1)} %get-tuple-element.39.refs_9_) | copy-start | bytes 1769476
  9.4 4.3 %copy-start.7 = (bf16[160,128]{1,0:T(8,128)(2,1)S(1)}, bf16[160,128]{1,0:T(8,128)(2,1)}, u32[]{:S(2)}) copy-start(bf16[160,128]{1,0:T(8,128)(2,1)} %constant.41.clone.refs_3_.refs_8_) | copy-start | bytes 122884
  13.0 8.6 %collective-permute-start.2 = (bf16[3,128,384]{2,1,0:T(8,128)(2,1)S(1)}, bf16[3,128,384]{2,1,0:T(8,128)(2,1)S(1)}, u32[]{:S(2)}, u32[]{:S(2)}) collective-permute-start(bf16[3,128,384]{2,1,0:T(8,128)(2,1)S(1)} %copy-done.11), channel_id=1, source_target_pairs={{1,2},{3,4},{5,6},{7,8},{9,10},{11,12},{13,14},{2,1},{4,3},{6,5},{... | collective-permute-start | bytes 884744 | tf_op jit(solution)/shard_map/ppermute | solution.py:490
  21.6 22.4 %collective-permute-start.3 = (bf16[864,384]{1,0:T(8,128)(2,1)S(1)}, bf16[864,384]{1,0:T(8,128)(2,1)S(1)}, u32[]{:S(2)}, u32[]{:S(2)}) collective-permute-start(bf16[864,384]{1,0:T(8,128)(2,1)S(1)} %get-tuple-element.47), channel_id=1, source_target_pairs={{1,2},{3,4},{5,6},{7,8},{9,10},{11,12},{13,14},{2,1},{4,3},{6,5},{... | collective-permute-start | bytes 1990664 | tf_op jit(solution)/shard_map/ppermute | solution.py:493
  30.2 23.7 %collective-permute-start.5 = (f32[2,3,2,8,128]{4,3,2,1,0:T(8,128)S(1)}, f32[2,3,2,8,128]{4,3,2,1,0:T(8,128)S(1)}, u32[]{:S(2)}, u32[]{:S(2)}) collective-permute-start(f32[2,3,2,8,128]{4,3,2,1,0:T(8,128)S(1)} %get-tuple-element.52), channel_id=1, source_target_pairs={{0,1},{1,0},{2,3},{3,2},{4,5},{5,4},{6,7},{7,6},{8,9},{9,8},{10,11... | collective-permute-start | bytes 147464 | tf_op jit(solution)/shard_map/ppermute | solution.py:497
  38.9 15.1 %collective-permute-start.6 = (f32[2,3,2,8,128]{4,3,2,1,0:T(8,128)S(1)}, f32[2,3,2,8,128]{4,3,2,1,0:T(8,128)S(1)}, u32[]{:S(2)}, u32[]{:S(2)}) collective-permute-start(f32[2,3,2,8,128]{4,3,2,1,0:T(8,128)S(1)} %get-tuple-element.52), channel_id=1, source_target_pairs={{1,2},{3,4},{5,6},{7,8},{9,10},{11,12},{13,14},{2,1},{4,3},{6,5},{... | collective-permute-start | bytes 147464 | tf_op jit(solution)/shard_map/ppermute | solution.py:498
  39.5 4.4 %copy-start.10 = (bf16[128,128]{1,0:T(8,128)(2,1)S(1)}, bf16[128,128]{1,0:T(8,128)(2,1)}, u32[]{:S(2)}) copy-start(bf16[128,128]{1,0:T(8,128)(2,1)} %constant.42.clone.refs_4_.refs_7_.refs_8_) | copy-start | bytes 98308
  39.7 4.2 %collective-permute-start.4 = (f32[2,3,2,8,128]{4,3,2,1,0:T(8,128)S(1)}, f32[2,3,2,8,128]{4,3,2,1,0:T(8,128)S(1)}, u32[]{:S(2)}, u32[]{:S(2)}) collective-permute-start(f32[2,3,2,8,128]{4,3,2,1,0:T(8,128)S(1)} %get-tuple-element.48), channel_id=1, source_target_pairs={{0,1},{1,0},{2,3},{3,2},{4,5},{5,4},{6,7},{7,6},{8,9},{9,8},{10,11... | collective-permute-start | bytes 147464 | tf_op jit(solution)/shard_map/ppermute | solution.py:494
  43.1 6.1 %collective-permute-start.7 = (bf16[8,24,1152]{2,1,0:T(8,128)(2,1)S(1)}, bf16[8,24,1152]{2,1,0:T(8,128)(2,1)S(1)}, u32[]{:S(2)}, u32[]{:S(2)}) collective-permute-start(bf16[8,24,1152]{2,1,0:T(8,128)(2,1)S(1)} %fusion), channel_id=1, source_target_pairs={{0,1},{1,0},{2,3},{3,2},{4,5},{5,4},{6,7},{7,6},{8,9},{9,8},{10,11... | collective-permute-start | bytes 1327112 | tf_op jit(solution)/shard_map/ppermute | solution.py:393
  49.3 9.7 %collective-permute-start.8 = (bf16[4,24,1152]{2,1,0:T(8,128)(2,1)S(1)}, bf16[4,24,1152]{2,1,0:T(8,128)(2,1)S(1)}, u32[]{:S(2)}, u32[]{:S(2)}) collective-permute-start(bf16[4,24,1152]{2,1,0:T(8,128)(2,1)S(1)} %fusion.1), channel_id=1, source_target_pairs={{0,2},{1,3},{2,0},{3,1},{4,6},{5,7},{6,4},{7,5},{8,10},{9,11},{10,... | collective-permute-start | bytes 663560 | tf_op jit(solution)/shard_map/ppermute | solution.py:393
  53.9 10.1 %copy-start.5 = (bf16[128,160]{1,0:T(8,128)(2,1)S(1)}, bf16[128,160]{1,0:T(8,128)(2,1)}, u32[]{:S(2)}) copy-start(bf16[128,160]{1,0:T(8,128)(2,1)} %constant.45.unplace_ref) | copy-start | bytes 122884
  53.9 10.1 %copy-start.8 = (bf16[128,128]{1,0:T(8,128)(2,1)S(1)}, bf16[128,128]{1,0:T(8,128)(2,1)}, u32[]{:S(2)}) copy-start(bf16[128,128]{1,0:T(8,128)(2,1)} %constant.46.unsplit_ref) | copy-start | bytes 98308
  59.1 8.7 %collective-permute-start.10 = (bf16[1,24,1152]{2,1,0:T(8,128)(2,1)S(1)}, bf16[1,24,1152]{2,1,0:T(8,128)(2,1)S(1)}, u32[]{:S(2)}, u32[]{:S(2)}) collective-permute-start(bf16[1,24,1152]{2,1,0:T(8,128)(2,1)S(1)} %get-tuple-element.63), channel_id=1, source_target_pairs={{0,8},{1,9},{2,10},{3,11},{4,12},{5,13},{6,14},{7,15},{8,0},{9,1},... | collective-permute-start | bytes 165896 | tf_op jit(solution)/shard_map/ppermute | solution.py:393
  62.7 6.1 %collective-permute-start.11 = (bf16[1,24,1152]{2,1,0:T(8,128)(2,1)S(1)}, bf16[1,24,1152]{2,1,0:T(8,128)(2,1)S(1)}, u32[]{:S(2)}, u32[]{:S(2)}) collective-permute-start(bf16[1,24,1152]{2,1,0:T(8,128)(2,1)S(1)} %get-tuple-element.62), channel_id=1, source_target_pairs={{0,12},{1,13},{2,14},{3,15},{4,8},{5,9},{6,10},{7,11},{8,4},{9,5},... | collective-permute-start | bytes 165896 | tf_op jit(solution)/shard_map/ppermute | solution.py:393
  64.0 4.8 %collective-permute-start.9 = (bf16[1,24,1152]{2,1,0:T(8,128)(2,1)S(1)}, bf16[1,24,1152]{2,1,0:T(8,128)(2,1)S(1)}, u32[]{:S(2)}, u32[]{:S(2)}) collective-permute-start(bf16[1,24,1152]{2,1,0:T(8,128)(2,1)S(1)} %get-tuple-element.64), channel_id=1, source_target_pairs={{0,4},{1,5},{2,6},{3,7},{4,0},{5,1},{6,2},{7,3},{8,12},{9,13},{10,... | collective-permute-start | bytes 165896 | tf_op jit(solution)/shard_map/ppermute | solution.py:393
